TPU v7x, 32 devices: a whole 2x2x4 slice. The times are simulated.
32 devices in a mesh: dp: 8 (over z, core), seq: 4 (over y, x).
Axes of the slice: x: 2, y: 2, z: 4, core: 2. Of those that a mesh axis runs over, the one named last changes fastest.
Arguments:
- char_ids: int32 [4, 8, 1024], P(None, 'dp', 'seq'), may hold values from 0 to 255
- targets: int32 [4, 8, 1024], P(None, 'dp', 'seq'), may hold values from 0 to 255
- seg_ids: int32 [4, 8, 1024], P(None, 'dp', 'seq'), may hold values from 0 to 255, as said below
- lengths: int32 [4, 8], P(None, 'dp'), may hold values from 512 to 1024
- owner_slot: int32 [26], replicated, may hold values from 0 to 39, as said below
- step_count: int32 [1], replicated, may hold values from 2 to 20
- master: float32 [40, 512, 512], P('seq', 'dp'), may hold values from -0.25 to 0.25
- tile_first: float32 [40, 512, 512], P('seq', 'dp'), may hold values from -3.0517578e-05 to 3.0517578e-05
- tile_second: float32 [40, 512, 512], P('seq', 'dp'), may hold values from 9.683462e-12 to 1.5405509e-10
- gain_rows: float32 [6, 512], replicated, may hold values from 0.5 to 1.5
- gain_first: float32 [6, 512], replicated, may hold values from -0.00030517578 to 0.00030517578
- gain_second: float32 [6, 512], replicated, may hold values from 9.683462e-10 to 1.5405508e-08
Outputs:
- loss_value: float32 [1], replicated
- grad_norm: float32 [1], replicated
- master_new: float32 [40, 512, 512], P('seq', 'dp')
- first_new: float32 [40, 512, 512], P('seq', 'dp')
- second_new: float32 [40, 512, 512], P('seq', 'dp')
- weights_low: bfloat16 [40, 512, 512], P('seq', 'dp')
- gains_new: float32 [6, 512], replicated
- gain_first_new: float32 [6, 512], replicated
- gain_second_new: float32 [6, 512], replicated
Inputs may be any that keep to these rules, and one draw needn't show every extreme that they name: `seg_ids`: each segment number of a sequence appears, the numbers never fall along the sequence, and a segment has at most 16 characters. `owner_slot`: the 26 matrices have distinct slots; slot s belongs to seq index s // 10; one seq index holds 10 matrices, others fewer.
All inputs are finite; a program needn't handle non-finite values.
Results may differ from a plain program's by a relative error of at most 0.0008.
The roundings to bfloat16 on the way count: a program that leaves them out, or rounds other values in their place, can miss the bound.
Values may be sent and summed in bfloat16 or wider, within the bound.
A program may use at most 448 MiB of HBM per device.

v0:
```python
import jax
import jax.numpy as jnp
from jax import lax
from jax.sharding import PartitionSpec as P

HEADS = 8
SEG_DEV = 64


BETA_ONE = 0.9
BETA_TWO = 0.95
ADAM_EPS = 1e-08
WEIGHT_DECAY = 0.1
RATE_TILES = 0.03
RATE_GAINS = 0.2
CLIP_NORM = 0.05
PRIOR_RATE = 0.25
NORM_EPS = 1e-06
MASKED = -1e30


def product(left, right):
    return jnp.dot(left, right, preferred_element_type=jnp.float32)


def product_tn(left, right):
    return lax.dot_general(
        left, right, (((0,), (0,)), ((), ())), preferred_element_type=jnp.float32
    )


def product_nt(left, right):
    return lax.dot_general(
        left, right, (((1,), (1,)), ((), ())), preferred_element_type=jnp.float32
    )


def exact_tn(left, right):
    return lax.dot_general(
        left,
        right,
        (((0,), (0,)), ((), ())),
        precision=lax.Precision.HIGHEST,
        preferred_element_type=jnp.float32,
    )


def rms_norm(values, gain):
    return values * lax.rsqrt(jnp.mean(values * values, axis=-1, keepdims=True) + NORM_EPS) * gain


def split_heads(tensor):
    return tensor.reshape(tensor.shape[0], HEADS, tensor.shape[1] // HEADS).transpose(1, 0, 2)


def join_heads(tensor):
    return tensor.transpose(1, 0, 2).reshape(tensor.shape[1], tensor.shape[0] * tensor.shape[2])


def block_weights(tiles):
    w_qkv = jnp.concatenate([tiles[0], tiles[1], tiles[2]], axis=1)
    w_up = jnp.concatenate([tiles[4], tiles[5], tiles[6], tiles[7]], axis=1)
    w_down = jnp.concatenate([tiles[8], tiles[9], tiles[10], tiles[11]], axis=0)
    return (w_qkv, w_up, w_down)


def causal_mask(row_count, key_count):
    first_row = lax.axis_index("seq") * row_count
    return (first_row + jnp.arange(row_count))[:, None] >= jnp.arange(key_count)[None, :]


def block_forward(hidden_in, tiles, gain_attn, gain_ffn, segment):
    row_count, model_width = hidden_in.shape
    w_qkv, w_up, w_down = block_weights(tiles)
    normed = rms_norm(hidden_in, gain_attn).astype(jnp.bfloat16)
    qkv_low = product(normed, w_qkv).astype(jnp.bfloat16)
    if segment:
        gathered = lax.all_gather(qkv_low[:, model_width:], "seq", axis=0, tiled=True)
    else:
        gathered = lax.all_gather(qkv_low[:, model_width:], "seq", axis=0, tiled=True)
    allowed = causal_mask(row_count, gathered.shape[0])
    factor = (model_width // HEADS) ** (-0.5)

    def head_forward(triple):
        q_head, k_head, v_head = triple
        scores = jnp.where(allowed, product_nt(q_head, k_head) * factor, MASKED)
        peak = jnp.max(scores, axis=1, keepdims=True)
        log_total = peak + jnp.log(jnp.sum(jnp.exp(scores - peak), axis=1, keepdims=True))
        weights = jnp.exp(scores - log_total).astype(jnp.bfloat16)
        return (product(weights, v_head), log_total[:, 0])

    head_out, log_totals = lax.map(
        head_forward,
        (
            split_heads(qkv_low[:, :model_width]),
            split_heads(gathered[:, :model_width]),
            split_heads(gathered[:, model_width:]),
        ),
    )
    attended = join_heads(head_out).astype(jnp.bfloat16)
    after_attn = hidden_in + product(attended, tiles[3])
    inner = product(rms_norm(after_attn, gain_ffn).astype(jnp.bfloat16), w_up)
    block_out = after_attn + product(jax.nn.gelu(inner).astype(jnp.bfloat16), w_down)
    return (block_out, (hidden_in, qkv_low, gathered, log_totals, attended, after_attn, inner))


def block_backward(grad_out, saved, tiles, gain_attn, gain_ffn, segment):
    hidden_in, qkv_low, gathered, log_totals, attended, after_attn, inner = saved
    row_count, model_width = hidden_in.shape
    w_qkv, w_up, w_down = block_weights(tiles)
    grad_ffn = grad_out.astype(jnp.bfloat16)
    activated, gelu_pull = jax.vjp(jax.nn.gelu, inner)
    grad_down = product_tn(activated.astype(jnp.bfloat16), grad_ffn)
    grad_inner = gelu_pull(product_nt(grad_ffn, w_down))[0].astype(jnp.bfloat16)
    normed_ffn, ffn_pull = jax.vjp(rms_norm, after_attn, gain_ffn)
    grad_up = product_tn(normed_ffn.astype(jnp.bfloat16), grad_inner)
    grad_normed_in, grad_gain_ffn = ffn_pull(product_nt(grad_inner, w_up))
    grad_after = grad_out + grad_normed_in
    grad_branch = grad_after.astype(jnp.bfloat16)
    grad_wout = product_tn(attended, grad_branch)
    grad_attended = product_nt(grad_branch, tiles[3]).astype(jnp.bfloat16)
    allowed = causal_mask(row_count, gathered.shape[0])
    factor = (model_width // HEADS) ** (-0.5)

    def head_backward(bundle):
        q_head, k_head, v_head, upstream, log_head = bundle
        scores = jnp.where(allowed, product_nt(q_head, k_head) * factor, MASKED)
        weights = jnp.exp(scores - log_head[:, None])
        grad_values = product_tn(weights.astype(jnp.bfloat16), upstream)
        grad_weights = product_nt(upstream, v_head)
        inner_sum = jnp.sum(weights * grad_weights, axis=1, keepdims=True)
        grad_scores = (weights * (grad_weights - inner_sum)).astype(jnp.bfloat16)
        return (
            product(grad_scores, k_head) * factor,
            product_tn(grad_scores, q_head) * factor,
            grad_values,
        )

    grad_query, grad_keys, grad_values = lax.map(
        head_backward,
        (
            split_heads(qkv_low[:, :model_width]),
            split_heads(gathered[:, :model_width]),
            split_heads(gathered[:, model_width:]),
            split_heads(grad_attended),
            log_totals,
        ),
    )
    grad_kv_all = jnp.concatenate([join_heads(grad_keys), join_heads(grad_values)], axis=1)
    if segment:
        grad_kv = lax.psum_scatter(grad_kv_all, "seq", scatter_dimension=0, tiled=True)
    else:
        grad_kv = lax.psum_scatter(grad_kv_all, "seq", scatter_dimension=0, tiled=True)
    grad_qkv = jnp.concatenate([join_heads(grad_query), grad_kv], axis=1).astype(jnp.bfloat16)
    normed_attn, attn_pull = jax.vjp(rms_norm, hidden_in, gain_attn)
    grad_wqkv = product_tn(normed_attn.astype(jnp.bfloat16), grad_qkv)
    grad_normed_x, grad_gain_attn = attn_pull(product_nt(grad_qkv, w_qkv))
    grad_in = grad_after + grad_normed_x
    pieces = [
        grad_wqkv[:, part_index * model_width : (part_index + 1) * model_width]
        for part_index in range(3)
    ]
    pieces = pieces + [grad_wout]
    pieces = pieces + [
        grad_up[:, part_index * model_width : (part_index + 1) * model_width]
        for part_index in range(4)
    ]
    pieces = pieces + [
        grad_down[part_index * model_width : (part_index + 1) * model_width]
        for part_index in range(4)
    ]
    return (grad_in, jnp.stack(pieces), grad_gain_attn, grad_gain_ffn)


def micro_step(tiles, gain_rows, chars_row, target_row, segment_row, length_one, micro_count):
    char_count = chars_row.shape[0]
    model_width = tiles.shape[2]
    vocab_size = model_width // 2
    seq_count = lax.axis_size("seq")
    seg_total = SEG_DEV * seq_count
    position = lax.axis_index("seq") * char_count + jnp.arange(char_count)
    is_valid = (position < length_one).astype(jnp.float32)
    vocab_iota = jnp.arange(vocab_size)
    char_hot = chars_row[:, None] == vocab_iota[None, :]
    embed_low = tiles[25, :vocab_size]
    head_low = tiles[25, vocab_size:]
    start_hidden = product(char_hot.astype(jnp.bfloat16), embed_low)
    char_out, char_saved = block_forward(
        start_hidden, tiles[0:12], gain_rows[0], gain_rows[1], False
    )
    char_low = char_out.astype(jnp.bfloat16)
    boundary_hidden = jnp.tanh(product(char_low, tiles[24]))
    root_width = model_width ** (-0.5)
    boundary_prob = jax.nn.sigmoid(jnp.sum(boundary_hidden * gain_rows[5], axis=1) * root_width)
    slot_iota = jnp.arange(seg_total)
    pool_hot = segment_row[None, :] + 1 == slot_iota[:, None]
    lift_hot = segment_row[:, None] == slot_iota[None, :]
    part_sums = product(pool_hot.astype(jnp.bfloat16), char_low).reshape(
        seq_count, SEG_DEV, model_width
    )
    side_info = jnp.stack(
        [
            jnp.sum(pool_hot.astype(jnp.float32), axis=1),
            jnp.any(lift_hot, axis=0).astype(jnp.float32),
        ],
        axis=0,
    )
    side_info = side_info.reshape(2, seq_count, SEG_DEV).transpose(1, 0, 2)
    sums_in, side_in = (
        lax.all_to_all(part_sums, "seq", split_axis=0, concat_axis=0, tiled=True),
        lax.all_to_all(side_info, "seq", split_axis=0, concat_axis=0, tiled=True),
    )
    row_counts = jnp.sum(side_in[:, 0, :], axis=0)
    divisor = jnp.maximum(row_counts, 1.0)[:, None]
    pooled = jnp.sum(sums_in, axis=0) / divisor
    seg_out, seg_saved = block_forward(pooled, tiles[12:24], gain_rows[2], gain_rows[3], True)
    outgoing = side_in[:, 1, :, None].astype(jnp.bfloat16) * seg_out.astype(jnp.bfloat16)[None]
    returned = lax.all_to_all(outgoing, "seq", split_axis=0, concat_axis=0, tiled=True)
    merged = char_out + product(
        lift_hot.astype(jnp.bfloat16), returned.reshape(seg_total, model_width)
    )
    final_norm, final_pull = jax.vjp(rms_norm, merged, gain_rows[4])
    final_low = final_norm.astype(jnp.bfloat16)
    logits = product_nt(final_low, head_low)
    peak = jnp.max(logits, axis=1, keepdims=True)
    log_total = peak[:, 0] + jnp.log(jnp.sum(jnp.exp(logits - peak), axis=1))
    target_hot = (target_row[:, None] == vocab_iota[None, :]).astype(jnp.float32)
    picked = jnp.sum(logits * target_hot, axis=1)
    ce_local = jnp.sum(is_valid * (log_total - picked))
    ce_all, soft_count, count_all = lax.psum(
        (ce_local, jnp.sum(is_valid * boundary_prob), jnp.sum(is_valid)), ("dp", "seq")
    )
    weight_ce = is_valid / (micro_count * count_all)
    grad_logits = ((jnp.exp(logits - log_total[:, None]) - target_hot) * weight_ce[:, None]).astype(
        jnp.bfloat16
    )
    grad_head = product_tn(grad_logits, final_low)
    grad_merged, grad_gain_final = final_pull(product(grad_logits, head_low))
    grad_rows = exact_tn(lift_hot.astype(jnp.float32), grad_merged).reshape(
        seq_count, SEG_DEV, model_width
    )
    grad_seg = jnp.sum(
        lax.all_to_all(grad_rows, "seq", split_axis=0, concat_axis=0, tiled=True), axis=0
    )
    grad_pooled, seg_tiles, grad_gain_two, grad_gain_three = block_backward(
        grad_seg, seg_saved, tiles[12:24], gain_rows[2], gain_rows[3], True
    )
    grad_sums = (side_in[:, 0, :, None] > 0).astype(jnp.float32) * (grad_pooled / divisor)[None]
    grad_back = lax.all_to_all(grad_sums, "seq", split_axis=0, concat_axis=0, tiled=True).reshape(
        seg_total, model_width
    )
    grad_char = grad_merged + exact_tn(pool_hot.astype(jnp.float32), grad_back)
    prior_slope = (
        lax.digamma(soft_count + 1.0)
        - lax.digamma(count_all - soft_count + 1.0)
        - jnp.log(PRIOR_RATE)
        + jnp.log(1.0 - PRIOR_RATE)
    ) / (count_all * micro_count)
    grad_boundary_logit = is_valid * prior_slope * boundary_prob * (1.0 - boundary_prob)
    grad_gain_boundary = (
        jnp.sum(grad_boundary_logit[:, None] * boundary_hidden, axis=0) * root_width
    )
    grad_pre = (
        grad_boundary_logit[:, None]
        * gain_rows[5][None, :]
        * root_width
        * (1.0 - boundary_hidden * boundary_hidden)
    ).astype(jnp.bfloat16)
    grad_boundary = product_tn(char_low, grad_pre)
    grad_char = grad_char + product_nt(grad_pre, tiles[24])
    grad_start, char_tiles, grad_gain_zero, grad_gain_one = block_backward(
        grad_char, char_saved, tiles[0:12], gain_rows[0], gain_rows[1], False
    )
    grad_embed = exact_tn(char_hot.astype(jnp.float32), grad_start)
    tile_grads = jnp.concatenate(
        [
            char_tiles,
            seg_tiles,
            grad_boundary[None],
            jnp.concatenate([grad_embed, grad_head], axis=0)[None],
        ],
        axis=0,
    )
    gain_grads = jnp.stack(
        [
            grad_gain_zero,
            grad_gain_one,
            grad_gain_two,
            grad_gain_three,
            grad_gain_final,
            grad_gain_boundary,
        ]
    )
    prior_term = (
        -(
            lax.lgamma(count_all + 1.0)
            - lax.lgamma(soft_count + 1.0)
            - lax.lgamma(count_all - soft_count + 1.0)
            + soft_count * jnp.log(PRIOR_RATE)
            + (count_all - soft_count) * jnp.log(1.0 - PRIOR_RATE)
        )
        / count_all
    )
    return (tile_grads, gain_grads, (ce_all / count_all + prior_term) / micro_count)


def gather_tiles(master, owner_slot):
    shard_low = master.astype(jnp.bfloat16)
    full_rows = lax.all_gather(shard_low, "dp", axis=1, tiled=True)
    all_slots = lax.all_gather(full_rows, "seq", axis=0, tiled=True)
    return jnp.take(all_slots, owner_slot, axis=0)


def reduce_tiles(tile_grads, owner_slot, slot_count):
    placed = (
        jnp.zeros((slot_count,) + tile_grads.shape[1:], jnp.float32).at[owner_slot].set(tile_grads)
    )
    per_owner = lax.psum_scatter(placed, "seq", scatter_dimension=0, tiled=True)
    return lax.psum_scatter(per_owner, "dp", scatter_dimension=1, tiled=True)


def adam_step(param, moment_a, moment_b, grad_in, rate, decay, step_float):
    new_first = BETA_ONE * moment_a + (1.0 - BETA_ONE) * grad_in
    new_second = BETA_TWO * moment_b + (1.0 - BETA_TWO) * grad_in * grad_in
    first_hat = new_first / (1.0 - BETA_ONE**step_float)
    second_hat = new_second / (1.0 - BETA_TWO**step_float)
    updated = param - rate * (first_hat / (jnp.sqrt(second_hat) + ADAM_EPS) + decay * param)
    return (updated, new_first, new_second)


def body(
    char_ids,
    targets,
    seg_ids,
    lengths,
    owner_slot,
    step_count,
    master,
    tile_first,
    tile_second,
    gain_rows,
    gain_first,
    gain_second,
):
    micro_count = char_ids.shape[0]
    model_width = master.shape[2]
    slot_count = master.shape[0] * lax.axis_size("seq")
    tile_total = jnp.zeros((owner_slot.shape[0], model_width, model_width), jnp.float32)
    gain_total = jnp.zeros_like(gain_rows)
    loss_total = jnp.zeros((), jnp.float32)
    for micro in range(micro_count):
        tiles = gather_tiles(master, owner_slot)
        tile_part, gain_part, loss_part = micro_step(
            tiles,
            gain_rows,
            char_ids[micro, 0],
            targets[micro, 0],
            seg_ids[micro, 0],
            lengths[micro, 0],
            micro_count,
        )
        tile_total = tile_total + tile_part
        gain_total = gain_total + gain_part
        loss_total = loss_total + loss_part
    shard_total = reduce_tiles(tile_total, owner_slot, slot_count)
    gain_sum, square_sum = lax.psum((gain_total, jnp.sum(shard_total * shard_total)), ("dp", "seq"))
    grad_norm = jnp.sqrt(square_sum + jnp.sum(gain_sum * gain_sum))
    clip_factor = jnp.minimum(1.0, CLIP_NORM / (grad_norm + 1e-06))
    step_float = step_count[0].astype(jnp.float32)
    local_ids = lax.axis_index("seq") * master.shape[0] + jnp.arange(master.shape[0])
    owned = jnp.any(local_ids[:, None] == owner_slot[None, :], axis=1)[:, None, None]
    new_tiles, new_first, new_second = adam_step(
        master,
        tile_first,
        tile_second,
        shard_total * clip_factor,
        RATE_TILES,
        WEIGHT_DECAY,
        step_float,
    )
    master_new = jnp.where(owned, new_tiles, master)
    first_new = jnp.where(owned, new_first, tile_first)
    second_new = jnp.where(owned, new_second, tile_second)
    gains_new, gain_first_new, gain_second_new = adam_step(
        gain_rows, gain_first, gain_second, gain_sum * clip_factor, RATE_GAINS, 0.0, step_float
    )
    return (
        loss_total.reshape(1),
        grad_norm.reshape(1),
        master_new,
        first_new,
        second_new,
        master_new.astype(jnp.bfloat16),
        gains_new,
        gain_first_new,
        gain_second_new,
    )


def solution(mesh):
    return jax.shard_map(
        body,
        mesh=mesh,
        in_specs=(
            P(None, "dp", "seq"),
            P(None, "dp", "seq"),
            P(None, "dp", "seq"),
            P(None, "dp"),
            P(),
            P(),
            P("seq", "dp", None),
            P("seq", "dp", None),
            P("seq", "dp", None),
            P(),
            P(),
            P(),
        ),
        out_specs=(
            P(),
            P(),
            P("seq", "dp", None),
            P("seq", "dp", None),
            P("seq", "dp", None),
            P("seq", "dp", None),
            P(),
            P(),
            P(),
        ),
        check_vma=False,
    )
```

profile of v0, /device:TPU:0, one launch (start us, length us, event | category | flops | bytes accessed | tf_op | source)
XLA Modules:
  0.0 2400.1 jit_solution(409107259535028867)
XLA Ops:
  9.5 59.4 %all-gather.7.cloned.1.call-done = bf16[10,512,512]{2,1,0:T(8,128)(2,1)} async-done(((bf16[10,64,512]{2,1,0:T(8,128)(2,1)}), bf16[10,512,512]{2,1,0:T(8,128)(2,1)}) %all-gather.7.cloned.1.call-update) | async-done | bytes 5242896 | tf_op jit(solution)/shard_map/all_gather | solution.py:309
  70.2 192.6 %all-gather.9.cloned.1.call-done = bf16[40,512,512]{2,1,0:T(8,128)(2,1)} async-done(((bf16[10,512,512]{2,1,0:T(8,128)(2,1)}), bf16[40,512,512]{2,1,0:T(8,128)(2,1)}) %all-gather.9.cloned.1.call-update) | async-done | bytes 20971536 | tf_op jit(solution)/shard_map/all_gather | solution.py:310
  262.8 13.5 gather_fusion
  276.4 7.5 broadcast_select_fusion
  284.0 4.6 copy-done
  322.1 4.2 all-to-all-start
  350.7 7.1 slice_bitcast_fusion.96
  375.6 24.5 %while.228 = (s32[]{:T(128)}, bf16[8,256,64]{1,2,0:T(8,128)(2,1)S(1)}, f32[8,256]{1,0:T(8,128)S(1)}, bf16[8,256,64]{2,1,0:T(8,128)(2,1)S(1)}, bf16[8,1024,64]{2,...) while((s32[]{:T(128)}, ...), condition=%wide.region_58.60_spmd.clone, body=%wide.region_55.59_spmd.clone.sunk | while | flops 69205760 | bytes 3813473 | solution.py:92
  406.9 4.4 all-to-all-start.7
  424.4 24.8 %while.226 = (s32[]{:T(128)}, bf16[8,256,64]{1,2,0:T(8,128)(2,1)S(1)}, f32[8,256]{1,0:T(8,128)S(1)}, bf16[8,256,64]{2,1,0:T(8,128)(2,1)}, bf16[8,1024,64]{2,1,0:...) while((s32[]{:T(128)}, ...), condition=%wide.region_31.33_spmd.clone, body=%wide.region_28.32_spmd.clone.sunk | while | flops 69205760 | bytes 3813473 | solution.py:92
  464.2 24.8 %while.224 = (s32[]{:T(128)}, bf16[8,256,64]{1,2,0:T(8,128)(2,1)S(1)}, f32[8,256]{1,0:T(8,128)S(1)}, bf16[8,256,64]{2,1,0:T(8,128)(2,1)}, bf16[8,1024,64]{2,1,0:...) while((s32[]{:T(128)}, ...), condition=%wide.region_4.6_spmd.clone, body=%wide.region_1.5_spmd.clone.sunk | while | flops 69205760 | bytes 3813473 | solution.py:92
  517.3 25.2 %while.230 = (s32[]{:T(128)}, bf16[8,256,64]{1,2,0:T(8,128)(2,1)S(1)}, f32[8,256]{1,0:T(8,128)S(1)}, bf16[8,256,64]{2,1,0:T(8,128)(2,1)}, bf16[8,1024,64]{2,1,0:...) while((s32[]{:T(128)}, ...), condition=%wide.region_85.87_spmd.clone, body=%wide.region_82.86_spmd.clone.sunk | while | flops 69205760 | bytes 3813473 | solution.py:92
  552.8 4.2 all-to-all-start.10
  587.0 10.0 all_gather.43
  603.4 20.6 while.229
  636.4 10.5 all_gather.45
  655.6 26.4 %while.231 = (s32[]{:T(128)}, bf16[8,64,64]{2,1,0:T(8,128)(2,1)}, f32[8,64]{1,0:T(8,128)}, bf16[8,64,64]{2,1,0:T(8,128)(2,1)}, bf16[8,256,64]{2,1,0:T(8,128)(2,1...) while((s32[]{:T(128)}, bf16[8,64,64]{2,1,0:T(8,128)(2,1)}, ...), condition=%wide.region_95.97_spmd.clone, body=%wide.region_92.96_spmd.clone.sunk | while | flops 4325314 | bytes 383101 | solution.py:92
  689.4 10.0 all_gather.41
  707.4 20.5 while.227
  735.3 9.3 all_gather.39
  752.6 20.6 while.225
  788.9 4.7 all-to-all-done.11
  826.9 40.0 %all-reduce.2 = (f32[]{:T(128)}, f32[]{:T(128)}, f32[]{:T(128)}, f32[]{:T(128)}, f32[]{:T(128)}, /*index=5*/f32[]{:T(128)}, f32[]{:T(128)}, f32[]{:T(128)}) all-reduce(f32[]{:T(128)} %get-tuple-element.1712, f32[]{:T(128)} %get-tuple-element.1711, f32[]{:T(128)} %get-tuple-element.1709, ...), channel_id=1, replica_groups=mesh['dp'=8,'seq'=4] {'dp','seq'}, use_global_device_ids=true, to_apply=%region_23.25 | all-reduce | flops 8 | bytes 64 | tf_op jit(solution)/shard_map/psum | solution.py:230
  910.1 4.4 all-to-all-start.18
  922.2 4.4 all-to-all-start.12
  946.9 4.1 all-to-all-start.16
  970.4 40.4 %while.232 = (s32[]{:T(128)}, bf16[8,64,64]{2,1,0:T(8,128)(2,1)S(1)}, f32[8,256,64]{1,2,0:T(8,128)S(1)}, f32[8,256,64]{1,2,0:T(8,128)S(1)}, bf16[8,64,64]{2,1,0:...) while((s32[]{:T(128)}, ...), condition=%wide.region_113.115_spmd.clone, body=%wide.region_111.114_spmd.clone.sunk | while | flops 10670018 | bytes 924273 | solution.py:139
  1016.4 45.0 %while.236 = (s32[]{:T(128)}, bf16[8,64,64]{2,1,0:T(8,128)(2,1)}, f32[8,256,64]{1,2,0:T(8,128)S(1)}, f32[8,256,64]{1,2,0:T(8,128)S(1)}, bf16[8,64,64]{2,1,0:T(8,...) while((s32[]{:T(128)}, bf16[8,64,64]{2,1,0:T(8,128)(2,1)}, ...), condition=%wide.region_141.143_spmd.clone, body=%wide.region_139.142_spmd.clone.sunk | while | flops 10670018 | bytes 924273 | solution.py:139
  1066.5 40.4 %while.238 = (s32[]{:T(128)}, bf16[8,64,64]{2,1,0:T(8,128)(2,1)S(1)}, f32[8,256,64]{1,2,0:T(8,128)S(1)}, f32[8,256,64]{1,2,0:T(8,128)S(1)}, bf16[8,64,64]{2,1,0:...) while((s32[]{:T(128)}, ...), condition=%wide.region_155.157_spmd.clone, body=%wide.region_153.156_spmd.clone.sunk | while | flops 10670018 | bytes 924273 | solution.py:139
  1111.2 46.2 %while.234 = (s32[]{:T(128)}, bf16[8,64,64]{2,1,0:T(8,128)(2,1)S(1)}, f32[8,256,64]{1,2,0:T(8,128)S(1)}, f32[8,256,64]{1,2,0:T(8,128)S(1)}, bf16[8,64,64]{2,1,0:...) while((s32[]{:T(128)}, ...), condition=%wide.region_127.129_spmd.clone, body=%wide.region_125.128_spmd.clone.sunk | while | flops 10670018 | bytes 924273 | solution.py:139
  1208.0 4.2 all-to-all-start.15
  1213.9 5.1 fusion.383
  1226.0 5.1 fusion.369
  1237.3 4.2 fusion.362
  1263.9 67.1 %while.233 = (s32[]{:T(128)}, bf16[8,256,64]{1,2,0:T(8,128)(2,1)}, f32[8,1024,64]{1,2,0:T(8,128)S(1)}, f32[8,1024,64]{1,2,0:T(8,128)}, bf16[8,256,64]{2,1,0:T(8,...) while((s32[]{:T(128)}, bf16[8,256,64]{1,2,0:T(8,128)(2,1)}, ...), condition=%wide.region_119.121_spmd.clone, body=%wide.region_117.120_spmd.clone.sunk | while | flops 170475264 | bytes 9448561 | solution.py:139
  1347.5 68.0 %while.237 = (s32[]{:T(128)}, bf16[8,256,64]{1,2,0:T(8,128)(2,1)S(1)}, f32[8,1024,64]{1,2,0:T(8,128)}, f32[8,1024,64]{1,2,0:T(8,128)}, bf16[8,256,64]{2,1,0:T(8,...) while((s32[]{:T(128)}, ...), condition=%wide.region_147.149_spmd.clone, body=%wide.region_145.148_spmd.clone.sunk | while | flops 170475264 | bytes 9448561 | solution.py:139
  1415.6 5.0 pad_maximum_fusion.2
  1423.8 61.7 %while.239 = (s32[]{:T(128)}, bf16[8,256,64]{1,2,0:T(8,128)(2,1)S(1)}, f32[8,1024,64]{1,2,0:T(8,128)}, f32[8,1024,64]{1,2,0:T(8,128)}, bf16[8,256,64]{2,1,0:T(8,...) while((s32[]{:T(128)}, ...), condition=%wide.region_161.163_spmd.clone, body=%wide.region_159.162_spmd.clone.sunk | while | flops 170475264 | bytes 9448561 | solution.py:139
  1485.6 4.9 pad_maximum_fusion.3
  1493.8 61.7 %while.235 = (s32[]{:T(128)}, bf16[8,256,64]{1,2,0:T(8,128)(2,1)S(1)}, f32[8,1024,64]{1,2,0:T(8,128)}, f32[8,1024,64]{1,2,0:T(8,128)}, bf16[8,256,64]{2,1,0:T(8,...) while((s32[]{:T(128)}, ...), condition=%wide.region_133.135_spmd.clone, body=%wide.region_131.134_spmd.clone.sunk | while | flops 170475264 | bytes 9448561 | solution.py:139
  1555.5 5.0 pad_maximum_fusion.1
  1759.5 44.5 %add_add_fusion = f32[26,512,512]{2,1,0:T(8,128)} fusion(f32[26,512,512]{2,1,0:T(8,128)} %fusion.496, f32[26,512,512]{2,1,0:T(8,128)} %fusion.495, f32[26,512,512]{2,1,0:T(8,128)} %fusion.493, f32[26,512,512]{2,1,0:T(8,128)} %fusion.494), kind=kLoop, calls=%fused_computation.454 | loop fusion | flops 20447232 | bytes 136314880 | tf_op jit(solution)/shard_map/add | solution.py:362
  1804.0 13.8 broadcast_in_dim.423
  1817.9 48.9 %scatter_fusion = f32[40,512,512]{2,1,0:T(8,128)} fusion(f32[40,512,512]{2,1,0:T(8,128)} %broadcast_in_dim.423, s32[26]{0:T(128)S(1)} %copy-done.448, f32[26,512,512]{2,1,0:T(8,128)} %add_add_fusion), kind=kCustom, calls=%fused_computation.1 | custom fusion | bytes 81789032 | tf_op jit(solution)/shard_map/scatter | solution.py:316
  1867.0 357.8 %reduce-scatter.39.cloned.1.call-done = f32[10,512,512]{2,1,0:T(8,128)} async-done(((f32[40,512,512]{2,1,0:T(8,128)}), f32[10,512,512]{2,1,0:T(8,128)}) %reduce-scatter.39.cloned.1.call-update) | async-done | bytes 10485776
  2241.4 95.2 %reduce-scatter.29.cloned.1.call-done = f32[10,64,512]{2,1,0:T(8,128)} async-done(((f32[10,512,512]{2,1,0:T(8,128)}), f32[10,64,512]{2,1,0:T(8,128)}) %reduce-scatter.29.cloned.1.call-update) | async-done | bytes 1310736 | tf_op jit(solution)/shard_map/reduce_scatter | solution.py:319
  2338.9 38.3 %all-reduce.1 = (f32[]{:T(128)}, f32[]{:T(128)}, f32[]{:T(128)}, f32[]{:T(128)}, f32[]{:T(128)}, /*index=5*/f32[6,512]{1,0:T(8,128)S(1)}) all-reduce(f32[]{:T(128)} %get-tuple-element.1713, f32[]{:T(128)} %get-tuple-element.1710, f32[]{:T(128)} %get-tuple-element.2214, ...), channel_id=1, replica_groups=mesh['dp'=8,'seq'=4] {'dp','seq'}, use_global_device_ids=true, to_apply=%region_21.23 | all-reduce | flops 3077 | bytes 24616 | tf_op jit(solution)/shard_map/psum | solution.py:230
  2385.1 5.9 fusion.785
  (2393 shorter events, 1295.0 us)
Async XLA Ops:
  7.2 61.7 %all-gather.7.cloned.1.call-start = ((), (), s32[]{:S(2)}) async-start(), calls=%async_computation.30 | async-start | bytes 5898240 | tf_op jit(solution)/shard_map/all_gather | solution.py:309
  9.5 253.3 %all-gather.9.cloned.1.call-start = ((), (), s32[]{:S(2)}) async-start(), calls=%async_computation.31 | async-start | bytes 26214400 | tf_op jit(solution)/shard_map/all_gather | solution.py:310
  68.9 293.5 %all-gather.15.cloned.1.call-start = ((), (), s32[]{:S(2)}) async-start(), calls=%async_computation.34 | async-start | bytes 2621440 | tf_op jit(solution)/shard_map/all_gather | solution.py:80
  69.6 214.5 %copy-start.365 = (s32[1,1,256]{2,1,0:T(1,128)}, s32[1,1,256]{2,1,0:T(1,128)S(1)}, u32[]{:S(2)}) copy-start(s32[1,1,256]{2,1,0:T(1,128)S(1)} %get-tuple-element.2111) | copy-start | bytes 3076
  69.6 225.8 %copy-start.361 = (s32[1,1,256]{2,1,0:T(1,128)}, s32[1,1,256]{2,1,0:T(1,128)S(1)}, u32[]{:S(2)}) copy-start(s32[1,1,256]{2,1,0:T(1,128)S(1)} %get-tuple-element.2112) | copy-start | bytes 3076
  69.6 257.5 %copy-start.367 = (s32[1,1,256]{2,1,0:T(1,128)}, s32[1,1,256]{2,1,0:T(1,128)S(1)}, u32[]{:S(2)}) copy-start(s32[1,1,256]{2,1,0:T(1,128)S(1)} %get-tuple-element.2113) | copy-start | bytes 3076
  69.6 270.2 %copy-start.363 = (s32[1,1,256]{2,1,0:T(1,128)}, s32[1,1,256]{2,1,0:T(1,128)S(1)}, u32[]{:S(2)}) copy-start(s32[1,1,256]{2,1,0:T(1,128)S(1)} %get-tuple-element.2114) | copy-start | bytes 3076
  70.2 270.9 %copy-start.299 = (f32[1,512]{1,0:T(1,128)}, f32[1,512]{1,0:T(1,128)S(1)}, u32[]{:S(2)}) copy-start(f32[1,512]{1,0:T(1,128)S(1)} %get-tuple-element.2102) | copy-start | bytes 6148
  70.2 479.8 %copy-start.296 = (f32[1,512]{1,0:T(1,128)}, f32[1,512]{1,0:T(1,128)S(1)}, u32[]{:S(2)}) copy-start(f32[1,512]{1,0:T(1,128)S(1)} %get-tuple-element.2097) | copy-start | bytes 6148
  292.1 12.6 all-to-all-start.6
  295.3 116.0 %all-gather.13.cloned.1.call-start = ((), (), s32[]{:S(2)}) async-start(), calls=%async_computation.33 | async-start | bytes 2621440 | tf_op jit(solution)/shard_map/all_gather | solution.py:80
  301.8 192.5 %copy-start.336 = (s32[256]{0:T(256)}, s32[256]{0:T(256)S(1)}, u32[]{:S(2)}) copy-start(s32[256]{0:T(256)S(1)} %broadcast_add_fusion.2) | copy-start | bytes 3076
  302.2 195.2 %copy-start.334 = (s32[256]{0:T(256)}, s32[256]{0:T(256)S(1)}, u32[]{:S(2)}) copy-start(s32[256]{0:T(256)S(1)} %broadcast_add_fusion.3) | copy-start | bytes 3076
  304.7 8.7 all-to-all-start.9
  313.4 8.7 all-to-all-start.3
  322.1 11.9 all-to-all-start
  326.3 124.7 %all-gather.11.cloned.1.call-start = ((), (), s32[]{:S(2)}) async-start(), calls=%async_computation.32 | async-start | bytes 2621440 | tf_op jit(solution)/shard_map/all_gather | solution.py:80
  332.0 172.1 %all-gather.17.cloned.1.call-start = ((), (), s32[]{:S(2)}) async-start(), calls=%async_computation.35 | async-start | bytes 2621440 | tf_op jit(solution)/shard_map/all_gather | solution.py:80
  406.9 145.8 %all-to-all-start.7 = ((f32[4,64,512]{2,1,0:T(8,128)}), f32[4,64,512]{2,1,0:T(8,128)}, u32[]{:S(2)}, u32[]{:S(2)}) async-start(f32[4,64,512]{2,1,0:T(8,128)} %bitcast.87), calls=%async_computation.7 | async-start | bytes 1048576 | tf_op jit(solution)/shard_map/all_to_all | solution.py:210
  552.8 10.8 all-to-all-start.10
  563.5 10.0 all-to-all-start.4
  573.6 10.0 all-to-all-start.1
  577.1 154.3 %copy-start.183 = (f32[64,512]{1,0:T(8,128)}, f32[64,512]{1,0:T(8,128)S(1)}, u32[]{:S(2)}) copy-start(f32[64,512]{1,0:T(8,128)S(1)} %reduce_sum.1112) | copy-start | bytes 393220
  632.3 151.3 %all-to-all-start.8 = ((bf16[4,64,512]{2,1,0:T(8,128)(2,1)}), bf16[4,64,512]{2,1,0:T(8,128)(2,1)}, u32[]{:S(2)}, u32[]{:S(2)}) async-start(bf16[4,64,512]{2,1,0:T(8,128)(2,1)} %broadcast_multiply_fusion.5), calls=%async_computation.8 | async-start | bytes 524288 | tf_op jit(solution)/shard_map/all_to_all | solution.py:218
  783.6 10.0 all-to-all-start.11
  793.5 8.8 all-to-all-start.5
  802.3 8.8 all-to-all-start.2
  910.1 12.2 all-to-all-start.18
  922.2 12.3 all-to-all-start.12
  934.5 12.4 all-to-all-start.14
  946.9 11.5 all-to-all-start.16
  951.1 227.9 %reduce-scatter.31.cloned.1.call-start = ((), (), s32[]{:S(2)}) async-start(), calls=%async_computation.41 | async-start | bytes 1310720
  1014.1 166.0 %reduce-scatter.35.cloned.1.call-start = ((), (), s32[]{:S(2)}) async-start(), calls=%async_computation.43 | async-start | bytes 1310720
  1066.3 115.0 %reduce-scatter.37.cloned.1.call-start = ((), (), s32[]{:S(2)}) async-start(), calls=%async_computation.44 | async-start | bytes 1310720
  1110.6 79.5 %reduce-scatter.33.cloned.1.call-start = ((), (), s32[]{:S(2)}) async-start(), calls=%async_computation.42 | async-start | bytes 1310720
  1195.8 12.2 all-to-all-start.19
  1208.0 12.1 all-to-all-start.15
  1220.1 11.1 all-to-all-start.13
  1231.3 12.9 all-to-all-start.17
  1235.4 384.6 %reduce-scatter.21.cloned.1.call-start = ((), (), s32[]{:S(2)}) async-start(), calls=%async_computation.36 | async-start | bytes 5242880 | tf_op jit(solution)/shard_map/reduce_scatter | solution.py:153
  1335.1 286.3 %reduce-scatter.25.cloned.1.call-start = ((), (), s32[]{:S(2)}) async-start(), calls=%async_computation.38 | async-start | bytes 5242880 | tf_op jit(solution)/shard_map/reduce_scatter | solution.py:153
  1420.6 202.2 %reduce-scatter.27.cloned.1.call-start = ((), (), s32[]{:S(2)}) async-start(), calls=%async_computation.39 | async-start | bytes 5242880 | tf_op jit(solution)/shard_map/reduce_scatter | solution.py:153
  1490.5 147.1 %reduce-scatter.23.cloned.1.call-start = ((), (), s32[]{:S(2)}) async-start(), calls=%async_computation.37 | async-start | bytes 5242880 | tf_op jit(solution)/shard_map/reduce_scatter | solution.py:153
  1560.6 664.3 %reduce-scatter.39.cloned.1.call-start = ((), (), s32[]{:S(2)}) async-start(), calls=%async_computation.45 | async-start | bytes 52428800
  1866.7 469.9 %reduce-scatter.29.cloned.1.call-start = ((), (), s32[]{:S(2)}) async-start(), calls=%async_computation.40 | async-start | bytes 11796480 | tf_op jit(solution)/shard_map/reduce_scatter | solution.py:319
  2225.1 159.4 %copy-start.319 = (f32[6,512]{1,0:T(8,128)S(1)}, f32[6,512]{1,0:T(8,128)}, u32[]{:S(2)}) copy-start(f32[6,512]{1,0:T(8,128)} %param.55) | copy-start | bytes 36868
  2225.1 159.4 %copy-start.338 = (f32[6,512]{1,0:T(8,128)S(1)}, f32[6,512]{1,0:T(8,128)}, u32[]{:S(2)}) copy-start(f32[6,512]{1,0:T(8,128)} %param.57) | copy-start | bytes 36868
  2225.1 159.4 %copy-start.339 = (f32[6,512]{1,0:T(8,128)S(1)}, f32[6,512]{1,0:T(8,128)}, u32[]{:S(2)}) copy-start(f32[6,512]{1,0:T(8,128)} %param.56) | copy-start | bytes 36868
  (491 other events, 3089.8 us)
Sparse Core Ops, SparseCore 0:
  10.2 58.6 all-gather.6
  70.8 191.9 all-gather.8
  290.8 35.3 all-gather.14
  327.9 35.2 all-gather.12
  364.9 35.3 all-gather.10
  402.0 40.3 all-gather.16
  1014.2 28.3 reduce-scatter.30
  1066.4 28.1 reduce-scatter.34
  1110.7 28.0 reduce-scatter.36
  1161.9 28.0 reduce-scatter.32
  1335.2 54.4 reduce-scatter.20
  1420.7 54.3 reduce-scatter.24
  1490.6 54.3 reduce-scatter.26
  1560.7 54.3 reduce-scatter.22
  1866.9 357.9 reduce-scatter.38
  2227.2 109.4 reduce-scatter.28
where the time goes:
time: 2430 us; the launch traced here: 2400 us
  matrix products  777 us (32%)
  waiting for transfers between devices  730 us (30%)
  local copies, waits for them, and re-layouts  447 us (18%)
  other arithmetic  176 us (7%)
  blocking collectives  118 us (5%)
  starting transfers between devices  80 us (3%)
  between operations  67.7 us (3%)
    unnamed x21, waiting for transfers between devices  358 us
    dot_general x232, matrix products, product_nt(): lax.dot_general(left, right, (((1,), (1,)), ((), ())), preferred_element_...  305 us
    dot_general x180, matrix products, product(): return jnp.dot(left, right, preferred_element_type=jnp.float32)  228 us
    dot_general x168, matrix products, product_tn(): lax.dot_general(left, right, (((0,), (0,)), ((), ())), preferred_element_...  226 us
    all_gather x1, waiting for transfers between devices, gather_tiles(): all_slots = lax.all_gather(full_rows, 'seq', axis=0, tiled=True)  193 us
    unnamed x1061, local copies, waits for them, and re-layouts  172 us
    reduce_scatter x1, waiting for transfers between devices, reduce_tiles(): return lax.psum_scatter(per_owner, 'dp', scatter_dimension=1, tiled=True)  95.2 us
    psum x2, blocking collectives, micro_step(): lax.psum((ce_local, jnp.sum(is_valid * boundary_prob), jnp.sum(is_valid))...  78.3 us
  transfers between devices with their start and end apart: 36, of which 16 were waited for; matrix products, arithmetic and copies ran while one was open for 37% of the time, Pallas kernels for 0%

commit v1 on v0

--- a/solution.py
+++ b/solution.py
@@ -328,6 +328,224 @@
     return (updated, new_first, new_second)
 
 
+def attention_whole(qkv_low, model_width, head_width):
+    length = qkv_low.shape[0]
+    allowed = jnp.arange(length)[:, None] >= jnp.arange(length)[None, :]
+    factor = head_width ** (-0.5)
+
+    def head_forward(triple):
+        q_head, k_head, v_head = triple
+        scores = jnp.where(allowed, product_nt(q_head, k_head) * factor, MASKED)
+        peak = jnp.max(scores, axis=1, keepdims=True)
+        log_total = peak + jnp.log(jnp.sum(jnp.exp(scores - peak), axis=1, keepdims=True))
+        weights = jnp.exp(scores - log_total).astype(jnp.bfloat16)
+        return (product(weights, v_head), log_total[:, 0])
+
+    head_out, log_totals = lax.map(
+        head_forward,
+        (
+            split_heads(qkv_low[:, :model_width]),
+            split_heads(qkv_low[:, model_width : 2 * model_width]),
+            split_heads(qkv_low[:, 2 * model_width :]),
+        ),
+    )
+    return (join_heads(head_out).astype(jnp.bfloat16), log_totals)
+
+
+def attention_whole_back(qkv_low, grad_attended, log_totals, model_width, head_width):
+    length = qkv_low.shape[0]
+    allowed = jnp.arange(length)[:, None] >= jnp.arange(length)[None, :]
+    factor = head_width ** (-0.5)
+
+    def head_backward(bundle):
+        q_head, k_head, v_head, upstream, log_head = bundle
+        scores = jnp.where(allowed, product_nt(q_head, k_head) * factor, MASKED)
+        weights = jnp.exp(scores - log_head[:, None])
+        grad_values = product_tn(weights.astype(jnp.bfloat16), upstream)
+        grad_weights = product_nt(upstream, v_head)
+        inner_sum = jnp.sum(weights * grad_weights, axis=1, keepdims=True)
+        grad_scores = (weights * (grad_weights - inner_sum)).astype(jnp.bfloat16)
+        return (
+            product(grad_scores, k_head) * factor,
+            product_tn(grad_scores, q_head) * factor,
+            grad_values,
+        )
+
+    grads = lax.map(
+        head_backward,
+        (
+            split_heads(qkv_low[:, :model_width]),
+            split_heads(qkv_low[:, model_width : 2 * model_width]),
+            split_heads(qkv_low[:, 2 * model_width :]),
+            split_heads(grad_attended),
+            log_totals,
+        ),
+    )
+    return jnp.concatenate([join_heads(piece) for piece in grads], axis=1).astype(jnp.bfloat16)
+
+
+def whole_forward(hidden_in, tiles, gain_attn, gain_ffn):
+    model_width = hidden_in.shape[1]
+    head_width = model_width // HEADS
+    w_qkv, w_up, w_down = block_weights(tiles)
+    normed = rms_norm(hidden_in, gain_attn).astype(jnp.bfloat16)
+    qkv_low = product(normed, w_qkv).astype(jnp.bfloat16)
+    attended, log_totals = attention_whole(qkv_low, model_width, head_width)
+    after_attn = hidden_in + product(attended, tiles[3])
+    inner = product(rms_norm(after_attn, gain_ffn).astype(jnp.bfloat16), w_up)
+    block_out = after_attn + product(jax.nn.gelu(inner).astype(jnp.bfloat16), w_down)
+    return (block_out, (hidden_in, qkv_low, log_totals, attended, after_attn, inner))
+
+
+def whole_backward(grad_out, saved, tiles, gain_attn, gain_ffn):
+    hidden_in, qkv_low, log_totals, attended, after_attn, inner = saved
+    model_width = hidden_in.shape[1]
+    head_width = model_width // HEADS
+    w_qkv, w_up, w_down = block_weights(tiles)
+    grad_ffn = grad_out.astype(jnp.bfloat16)
+    activated, gelu_pull = jax.vjp(jax.nn.gelu, inner)
+    grad_down = product_tn(activated.astype(jnp.bfloat16), grad_ffn)
+    grad_inner = gelu_pull(product_nt(grad_ffn, w_down))[0].astype(jnp.bfloat16)
+    normed_ffn, ffn_pull = jax.vjp(rms_norm, after_attn, gain_ffn)
+    grad_up = product_tn(normed_ffn.astype(jnp.bfloat16), grad_inner)
+    grad_normed_in, grad_gain_ffn = ffn_pull(product_nt(grad_inner, w_up))
+    grad_after = grad_out + grad_normed_in
+    grad_branch = grad_after.astype(jnp.bfloat16)
+    grad_wout = product_tn(attended, grad_branch)
+    grad_attended = product_nt(grad_branch, tiles[3]).astype(jnp.bfloat16)
+    grad_qkv = attention_whole_back(qkv_low, grad_attended, log_totals, model_width, head_width)
+    normed_attn, attn_pull = jax.vjp(rms_norm, hidden_in, gain_attn)
+    grad_wqkv = product_tn(normed_attn.astype(jnp.bfloat16), grad_qkv)
+    grad_normed_x, grad_gain_attn = attn_pull(product_nt(grad_qkv, w_qkv))
+    grad_in = grad_after + grad_normed_x
+    pieces = [grad_wqkv[:, i * model_width : (i + 1) * model_width] for i in range(3)]
+    pieces = pieces + [grad_wout]
+    pieces = pieces + [grad_up[:, i * model_width : (i + 1) * model_width] for i in range(4)]
+    pieces = pieces + [grad_down[i * model_width : (i + 1) * model_width] for i in range(4)]
+    return (grad_in, pieces, grad_gain_attn, grad_gain_ffn)
+
+
+def gather_tiles_whole(master, owner_slot):
+    shard_low = master.astype(jnp.bfloat16)
+    all_slots = lax.all_gather(shard_low, "seq", axis=0, tiled=True)
+    picked = jnp.take(all_slots, owner_slot, axis=0)
+    return lax.all_gather(picked, "dp", axis=1, tiled=True)
+
+
+def reduce_tiles_whole(tile_grads, owner_slot, slot_count):
+    rows_own = lax.psum_scatter(tile_grads, "dp", scatter_dimension=1, tiled=True)
+    hot = (jnp.arange(slot_count)[:, None] == owner_slot[None, :])
+    source = jnp.sum(jnp.where(hot, jnp.arange(owner_slot.shape[0])[None, :], 0), axis=1)
+    owned = jnp.any(hot, axis=1)[:, None, None]
+    placed = jnp.where(owned, jnp.take(rows_own, source, axis=0), 0.0)
+    return lax.psum_scatter(placed, "seq", scatter_dimension=0, tiled=True)
+
+
+def whole_step(char_ids, targets, seg_ids, lengths, owner_slot, master, gain_rows):
+    micro_count = char_ids.shape[0]
+    seq_count = lax.axis_size("seq")
+    seq_me = lax.axis_index("seq")
+    model_width = master.shape[2]
+    vocab_size = model_width // 2
+    seg_total = SEG_DEV * seq_count
+    ids = jnp.stack([char_ids[:, 0], targets[:, 0], seg_ids[:, 0]], axis=1)
+    ids = lax.all_to_all(ids, "seq", split_axis=0, concat_axis=2, tiled=True)[0]
+    chars_row, target_row, segment_row = ids[0], ids[1], ids[2]
+    length_one = lax.dynamic_index_in_dim(lengths[:, 0], seq_me, keepdims=False)
+    tiles = gather_tiles_whole(master, owner_slot)
+    char_count = chars_row.shape[0]
+    is_valid = (jnp.arange(char_count) < length_one).astype(jnp.float32)
+    vocab_iota = jnp.arange(vocab_size)
+    char_hot = chars_row[:, None] == vocab_iota[None, :]
+    embed_low = tiles[25, :vocab_size]
+    head_low = tiles[25, vocab_size:]
+    start_hidden = product(char_hot.astype(jnp.bfloat16), embed_low)
+    char_out, char_saved = whole_forward(start_hidden, tiles[0:12], gain_rows[0], gain_rows[1])
+    char_low = char_out.astype(jnp.bfloat16)
+    boundary_hidden = jnp.tanh(product(char_low, tiles[24]))
+    root_width = model_width ** (-0.5)
+    boundary_prob = jax.nn.sigmoid(jnp.sum(boundary_hidden * gain_rows[5], axis=1) * root_width)
+    soft_count, count_all = lax.psum(
+        (jnp.sum(is_valid * boundary_prob), length_one.astype(jnp.float32)), "dp"
+    )
+    slot_iota = jnp.arange(seg_total)
+    pool_hot = segment_row[None, :] + 1 == slot_iota[:, None]
+    lift_hot = segment_row[:, None] == slot_iota[None, :]
+    row_counts = jnp.sum(pool_hot.astype(jnp.float32), axis=1)
+    divisor = jnp.maximum(row_counts, 1.0)[:, None]
+    pooled = product(pool_hot.astype(jnp.bfloat16), char_low) / divisor
+    seg_out, seg_saved = whole_forward(pooled, tiles[12:24], gain_rows[2], gain_rows[3])
+    merged = char_out + product(lift_hot.astype(jnp.bfloat16), seg_out.astype(jnp.bfloat16))
+    final_norm, final_pull = jax.vjp(rms_norm, merged, gain_rows[4])
+    final_low = final_norm.astype(jnp.bfloat16)
+    logits = product_nt(final_low, head_low)
+    peak = jnp.max(logits, axis=1, keepdims=True)
+    log_total = peak[:, 0] + jnp.log(jnp.sum(jnp.exp(logits - peak), axis=1))
+    target_hot = (target_row[:, None] == vocab_iota[None, :]).astype(jnp.float32)
+    picked = jnp.sum(logits * target_hot, axis=1)
+    ce_local = jnp.sum(is_valid * (log_total - picked))
+    weight_ce = is_valid / (micro_count * count_all)
+    grad_logits = ((jnp.exp(logits - log_total[:, None]) - target_hot) * weight_ce[:, None]).astype(
+        jnp.bfloat16
+    )
+    grad_head = product_tn(grad_logits, final_low)
+    grad_merged, grad_gain_final = final_pull(product(grad_logits, head_low))
+    grad_seg = exact_tn(lift_hot.astype(jnp.float32), grad_merged)
+    grad_pooled, seg_pieces, grad_gain_two, grad_gain_three = whole_backward(
+        grad_seg, seg_saved, tiles[12:24], gain_rows[2], gain_rows[3]
+    )
+    grad_char = grad_merged + exact_tn(pool_hot.astype(jnp.float32), grad_pooled / divisor)
+    prior_slope = (
+        lax.digamma(soft_count + 1.0)
+        - lax.digamma(count_all - soft_count + 1.0)
+        - jnp.log(PRIOR_RATE)
+        + jnp.log(1.0 - PRIOR_RATE)
+    ) / (count_all * micro_count)
+    grad_boundary_logit = is_valid * prior_slope * boundary_prob * (1.0 - boundary_prob)
+    grad_gain_boundary = (
+        jnp.sum(grad_boundary_logit[:, None] * boundary_hidden, axis=0) * root_width
+    )
+    grad_pre = (
+        grad_boundary_logit[:, None]
+        * gain_rows[5][None, :]
+        * root_width
+        * (1.0 - boundary_hidden * boundary_hidden)
+    ).astype(jnp.bfloat16)
+    grad_boundary = product_tn(char_low, grad_pre)
+    grad_char = grad_char + product_nt(grad_pre, tiles[24])
+    grad_start, char_pieces, grad_gain_zero, grad_gain_one = whole_backward(
+        grad_char, char_saved, tiles[0:12], gain_rows[0], gain_rows[1]
+    )
+    grad_embed = exact_tn(char_hot.astype(jnp.float32), grad_start)
+    tile_grads = jnp.stack(
+        char_pieces
+        + seg_pieces
+        + [grad_boundary, jnp.concatenate([grad_embed, grad_head], axis=0)]
+    )
+    gain_grads = jnp.stack(
+        [
+            grad_gain_zero,
+            grad_gain_one,
+            grad_gain_two,
+            grad_gain_three,
+            grad_gain_final,
+            grad_gain_boundary,
+        ]
+    )
+    prior_term = (
+        -(
+            lax.lgamma(count_all + 1.0)
+            - lax.lgamma(soft_count + 1.0)
+            - lax.lgamma(count_all - soft_count + 1.0)
+            + soft_count * jnp.log(PRIOR_RATE)
+            + (count_all - soft_count) * jnp.log(1.0 - PRIOR_RATE)
+        )
+        / count_all
+    )
+    loss_part = (ce_local / count_all + prior_term / lax.axis_size("dp")) / micro_count
+    return (tile_grads, gain_grads, loss_part)
+
+
 def body(
     char_ids,
     targets,
@@ -345,25 +563,34 @@
     micro_count = char_ids.shape[0]
     model_width = master.shape[2]
     slot_count = master.shape[0] * lax.axis_size("seq")
-    tile_total = jnp.zeros((owner_slot.shape[0], model_width, model_width), jnp.float32)
-    gain_total = jnp.zeros_like(gain_rows)
-    loss_total = jnp.zeros((), jnp.float32)
-    for micro in range(micro_count):
-        tiles = gather_tiles(master, owner_slot)
-        tile_part, gain_part, loss_part = micro_step(
-            tiles,
-            gain_rows,
-            char_ids[micro, 0],
-            targets[micro, 0],
-            seg_ids[micro, 0],
-            lengths[micro, 0],
-            micro_count,
+    if micro_count == lax.axis_size("seq"):
+        tile_grads, gain_part, loss_part = whole_step(
+            char_ids, targets, seg_ids, lengths, owner_slot, master, gain_rows
         )
-        tile_total = tile_total + tile_part
-        gain_total = gain_total + gain_part
-        loss_total = loss_total + loss_part
-    shard_total = reduce_tiles(tile_total, owner_slot, slot_count)
-    gain_sum, square_sum = lax.psum((gain_total, jnp.sum(shard_total * shard_total)), ("dp", "seq"))
+        shard_total = reduce_tiles_whole(tile_grads, owner_slot, slot_count)
+        gain_sum, square_sum, loss_total = lax.psum(
+            (gain_part, jnp.sum(shard_total * shard_total), loss_part), ("dp", "seq")
+        )
+    else:
+        tile_total = jnp.zeros((owner_slot.shape[0], model_width, model_width), jnp.float32)
+        gain_total = jnp.zeros_like(gain_rows)
+        loss_total = jnp.zeros((), jnp.float32)
+        for micro in range(micro_count):
+            tiles = gather_tiles(master, owner_slot)
+            tile_part, gain_part, loss_part = micro_step(
+                tiles,
+                gain_rows,
+                char_ids[micro, 0],
+                targets[micro, 0],
+                seg_ids[micro, 0],
+                lengths[micro, 0],
+                micro_count,
+            )
+            tile_total = tile_total + tile_part
+            gain_total = gain_total + gain_part
+            loss_total = loss_total + loss_part
+        shard_total = reduce_tiles(tile_total, owner_slot, slot_count)
+        gain_sum, square_sum = lax.psum((gain_total, jnp.sum(shard_total * shard_total)), ("dp", "seq"))
     grad_norm = jnp.sqrt(square_sum + jnp.sum(gain_sum * gain_sum))
     clip_factor = jnp.minimum(1.0, CLIP_NORM / (grad_norm + 1e-06))
     step_float = step_count[0].astype(jnp.float32)

time: 2430 us -> 954 us (0.39)
  matrix products: 777 us -> 264 us
  local copies, waits for them, and re-layouts: 447 us -> 70 us
  waiting for transfers between devices: 730 us -> 481 us
  other arithmetic: 176 us -> 40.8 us
  starting transfers between devices: 80 us -> 3.42 us
  blocking collectives: 118 us -> 55.5 us
  between operations: 67.7 us -> 31.1 us
    unnamed x21 -> x4, waiting for transfers between devices: 358 us -> 0.07 us
    reduce_scatter x5 -> x2, waiting for transfers between devices: 95.3 us -> 318 us  [the longest x1 264 us: reduce_tiles_whole(): lax.psum_scatter(tile_grads, 'dp', scatter_dimension=1, tiled=True)]
    dot_general x232 -> x58, matrix products: 305 us -> 102 us  [product_nt(): lax.dot_general(left, right, (((1,), (1,)), ((), ())), preferred_element_...]
    dot_general x180 -> x44, matrix products: 228 us -> 75.3 us  [product(): return jnp.dot(left, right, preferred_element_type=jnp.float32)]
    dot_general x168 -> x42, matrix products: 226 us -> 81.8 us  [product_tn(): lax.dot_general(left, right, (((0,), (0,)), ((), ())), preferred_element_...]
    unnamed x1061 -> x208, local copies, waits for them, and re-layouts: 172 us -> 34.8 us
    all_gather x6 -> x2, waiting for transfers between devices: 252 us -> 160 us  [the longest x1 117 us: gather_tiles_whole(): return lax.all_gather(picked, 'dp', axis=1, tiled=True)]
    all_to_all x20 -> x1, starting transfers between devices: 77.9 us -> 3.25 us  [whole_step(): ids = lax.all_to_all(ids, 'seq', split_axis=0, concat_axis=2, tiled=True)[0]]
  transfers between devices with their start and end apart: 36 -> 5, of which waited for: 16 -> 5; matrix products, arithmetic and copies ran while one was open for 37% -> 0% of each run, Pallas kernels for 0% -> 0%
where the time goes in v1:
time: 954 us; the launch traced here: 947 us
  waiting for transfers between devices  481 us (50%)
  matrix products  264 us (28%)
  local copies, waits for them, and re-layouts  70 us (7%)
  blocking collectives  55.5 us (6%)
  other arithmetic  40.8 us (4%)
  between operations  31.1 us (3%)
    reduce_scatter x1, waiting for transfers between devices, reduce_tiles_whole(): lax.psum_scatter(tile_grads, 'dp', scatter_dimension=1, tiled=True)  264 us
    all_gather x1, waiting for transfers between devices, gather_tiles_whole(): return lax.all_gather(picked, 'dp', axis=1, tiled=True)  117 us
    dot_general x58, matrix products, product_nt(): lax.dot_general(left, right, (((1,), (1,)), ((), ())), preferred_element_...  102 us
    dot_general x42, matrix products, product_tn(): lax.dot_general(left, right, (((0,), (0,)), ((), ())), preferred_element_...  81.8 us
    dot_general x44, matrix products, product(): return jnp.dot(left, right, preferred_element_type=jnp.float32)  75.3 us
    reduce_scatter x1, waiting for transfers between devices, reduce_tiles_whole(): return lax.psum_scatter(placed, 'seq', scatter_dimension=0, tiled=True)  53.4 us
    all_gather x1, waiting for transfers between devices, gather_tiles_whole(): all_slots = lax.all_gather(shard_low, 'seq', axis=0, tiled=True)  43.2 us
    psum x1, blocking collectives, body(): lax.psum((gain_part, jnp.sum(shard_total * shard_total), loss_part), ('dp...  40.6 us
  transfers between devices with their start and end apart: 5, of which 5 were waited for; matrix products, arithmetic and copies ran while one was open for 0% of the time, Pallas kernels for 0%

profile of v1, /device:TPU:0, one launch (start us, length us, event | category | flops | bytes accessed | tf_op | source)
XLA Modules:
  0.0 946.8 jit_solution(13144643910041792487)
XLA Ops:
  9.6 43.2 %all-gather.3.cloned.1.call-done = bf16[40,64,512]{2,1,0:T(8,128)(2,1)} async-done(((bf16[10,64,512]{2,1,0:T(8,128)(2,1)}), bf16[40,64,512]{2,1,0:T(8,128)(2,1)}) %all-gather.3.cloned.1.call-update) | async-done | bytes 2621456 | tf_op jit(solution)/shard_map/all_gather | solution.py:430
  52.8 2.4 gather_fusion
  57.4 3.3 all-to-all-start
  62.1 3.2 all-to-all-done
  65.5 116.7 %all-gather.5.cloned.1.call-done = bf16[26,512,512]{2,1,0:T(8,128)(2,1)} async-done(((bf16[26,64,512]{2,1,0:T(8,128)(2,1)}), bf16[26,512,512]{2,1,0:T(8,128)(2,1)}) %all-gather.5.cloned.1.call-update) | async-done | bytes 13631504 | tf_op jit(solution)/shard_map/all_gather | solution.py:432
  200.0 32.4 %while.56 = (s32[]{:T(128)}, bf16[8,1024,64]{1,2,0:T(8,128)(2,1)S(1)}, f32[8,1024]{1,0:T(8,128)S(1)}, bf16[8,1024,64]{2,1,0:T(8,128)(2,1)}, bf16[8,1024,64]{2,1,...) while((s32[]{:T(128)}, bf16[8,1024,64]{1,2,0:T(8,128)(2,1)S(1)}, ...), condition=%wide.region_4.5_spmd.clone, body=%wide.region_1.4_spmd.clone.sunk | while | flops 283114496 | bytes 13670497 | solution.py:344
  234.7 7.2 slice_bitcast_fusion.30
  241.9 2.5 fusion.179
  244.6 3.5 convolution_add_fusion.2
  248.1 3.6 multiply_reduce_fusion.9
  253.0 14.9 %all-reduce.1 = (f32[]{:T(128)}, f32[]{:T(128)}) all-reduce(f32[]{:T(128)S(6)} %convert_element_type.157, f32[]{:T(128)} %select_reduce_fusion.2), channel_id=1, replica_groups=mesh['dp'=8,'seq'=4] {'dp'}, use_global_device_ids=true, to_apply=%region_18.19 | all-reduce | flops 2 | bytes 16 | tf_op jit(solution)/shard_map/psum | solution.py:468
  276.7 4.8 while.57
  283.4 3.8 fusion.182
  287.3 4.2 multiply_reduce_fusion.10
  298.0 2.4 multiply_reduce_fusion.3
  303.9 5.4 fusion.108
  309.3 3.0 fusion.192
  320.4 50.4 %while.58 = (s32[]{:T(128)}, bf16[8,256,64]{1,2,0:T(8,128)(2,1)}, bf16[8,256,64]{1,2,0:T(8,128)(2,1)}, bf16[8,256,64]{1,2,0:T(8,128)(2,1)}, bf16[8,256,64]{2,1,0...) while((s32[]{:T(128)}, bf16[8,256,64]{1,2,0:T(8,128)(2,1)}, ...), condition=%wide.region_29.30_spmd.clone, body=%wide.region_27.29_spmd.clone.sunk | while | flops 42630912 | bytes 2566257 | solution.py:374
  370.7 2.5 multiply_reduce_fusion.15
  373.3 2.4 fusion.183
  377.2 2.6 add_add_fusion.3
  379.9 12.0 %fusion.101 = bf16[1024,2048]{1,0:T(8,128)(2,1)S(1)} fusion(f32[1024,2048]{1,0:T(8,128)S(1)} %bitcast.514, f32[1024,512]{0,1:T(8,128)S(1)} %add_add_fusion.3, bf16[512,512]{1,0:T(8,128)(2,1)S(1)} %copy-done.48, bf16[512,512]{1,0:T(8,128)(2,1)S(1)} %copy-done.50, bf16[512,512]{1,0:T(8,128)(2,1)S(1)} %copy-done.52, bf16[512,512]{1,0:T(8,128)(2,1)S(1)} %copy-done.54), kind=kOutput, calls=%fused_computation.123 | convolution fusion | flops 2198339584 | bytes 16777216 | tf_op jit(solution)/shard_map/dot_general | solution.py:33
  392.0 5.0 fusion.165
  397.0 2.6 multiply_reduce_fusion.4
  399.7 4.4 fusion.224
  404.7 3.1 convolution_convert_fusion.2
  407.8 2.7 copy.116
  413.8 95.5 %while.59 = (s32[]{:T(128)}, bf16[8,1024,64]{1,2,0:T(8,128)(2,1)}, bf16[8,1024,64]{1,2,0:T(8,128)(2,1)}, bf16[8,1024,64]{1,2,0:T(8,128)(2,1)}, bf16[8,1024,64]{2...) while((s32[]{:T(128)}, bf16[8,1024,64]{1,2,0:T(8,128)(2,1)}, ...), condition=%wide.region_34.35_spmd.clone, body=%wide.region_32.34_spmd.clone.sunk | while | flops 681704448 | bytes 34104432 | solution.py:374
  418.9 2.4 fusion.304
  421.3 2.4 fusion.303
  430.8 2.4 fusion.304
  433.2 2.4 fusion.303
  442.7 2.4 fusion.304
  445.1 2.4 fusion.303
  454.6 2.4 fusion.304
  456.9 2.4 fusion.303
  466.5 2.4 fusion.304
  468.8 2.4 fusion.303
  478.4 2.4 fusion.304
  490.3 2.4 fusion.304
  502.2 2.4 fusion.304
  509.4 5.1 multiply_reduce_fusion.5
  552.1 264.4 %reduce-scatter.3.cloned.1.call-done = f32[26,64,512]{2,1,0:T(8,128)} async-done(((f32[26,512,512]{2,1,0:T(8,128)}), f32[26,64,512]{2,1,0:T(8,128)}) %reduce-scatter.3.cloned.1.call-update) | async-done | bytes 3407888 | tf_op jit(solution)/shard_map/reduce_scatter | solution.py:436
  816.5 5.2 gather_fusion.1
  821.7 6.1 select_select_fusion
  834.4 53.4 %reduce-scatter.5.cloned.1.call-done = f32[10,64,512]{2,1,0:T(8,128)} async-done(((f32[40,64,512]{2,1,0:T(8,128)}), f32[10,64,512]{2,1,0:T(8,128)}) %reduce-scatter.5.cloned.1.call-update) | async-done | bytes 1310736 | tf_op jit(solution)/shard_map/reduce_scatter | solution.py:441
  890.2 40.6 %all-reduce = (f32[1]{0:T(128)}, f32[]{:T(128)}, f32[6,512]{1,0:T(8,128)S(1)}) all-reduce(f32[1]{0:T(128)} %bitcast.56, f32[]{:T(128)} %multiply_reduce_fusion.13, f32[6,512]{1,0:T(8,128)S(1)} %stack.121), channel_id=1, replica_groups=mesh['dp'=8,'seq'=4] {'dp','seq'}, use_global_device_ids=true, to_apply=%region_22.23 | all-reduce | flops 3074 | bytes 24592 | tf_op jit(solution)/shard_map/psum | solution.py:571
  933.4 5.2 fusion.226
  (476 shorter events, 246.9 us)
Async XLA Ops:
  7.2 53.6 %copy-start = (s32[4,1]{0,1:T(1,128)S(1)}, s32[4,1]{0,1:T(1,128)}, u32[]{:S(2)}) copy-start(s32[4,1]{0,1:T(1,128)} %param.23) | copy-start | bytes 52
  7.2 45.6 %all-gather.3.cloned.1.call-start = ((), (), s32[]{:S(2)}) async-start(), calls=%async_computation.3 | async-start | bytes 3276800 | tf_op jit(solution)/shard_map/all_gather | solution.py:430
  9.5 172.7 %all-gather.5.cloned.1.call-start = ((), (), s32[]{:S(2)}) async-start(), calls=%async_computation.4 | async-start | bytes 15335424 | tf_op jit(solution)/shard_map/all_gather | solution.py:432
  55.3 5.4 copy-start.68
  57.4 7.9 all-to-all-start
  60.6 755.9 %reduce-scatter.3.cloned.1.call-start = ((), (), s32[]{:S(2)}) async-start(), calls=%async_computation.5 | async-start | bytes 30670848 | tf_op jit(solution)/shard_map/reduce_scatter | solution.py:436
  60.7 125.3 %copy-start.79 = (f32[1,512]{1,0:T(1,128)}, f32[1,512]{1,0:T(1,128)S(1)}, u32[]{:S(2)}) copy-start(f32[1,512]{1,0:T(1,128)S(1)} %get-tuple-element.488) | copy-start | bytes 6148
  65.3 120.7 %copy-start.72 = (s32[1,1,4,256]{3,1,2,0:T(1,128)}, s32[1,1,4,256]{3,1,2,0:T(1,128)S(1)}, u32[]{:S(2)}) copy-start(s32[1,1,4,256]{3,1,2,0:T(1,128)S(1)} %get-tuple-element.491) | copy-start | bytes 12292
  183.8 4.3 copy-start.70
  183.8 48.6 %copy-start.7 = (f32[1024,512]{0,1:T(8,128)}, f32[1024,512]{0,1:T(8,128)S(1)}, u32[]{:S(2)}) copy-start(f32[1024,512]{0,1:T(8,128)S(1)} %get-tuple-element.493) | copy-start | bytes 6291460
  183.8 4.2 copy-start.76
  234.6 9.9 %copy-start.16 = (f32[1024,512]{0,1:T(8,128)}, f32[1024,512]{0,1:T(8,128)S(1)}, u32[]{:S(2)}) copy-start(f32[1024,512]{0,1:T(8,128)S(1)} %get-tuple-element.495) | copy-start | bytes 6291460
  241.9 31.6 %copy-start.55 = (bf16[512,512]{1,0:T(8,128)(2,1)}, bf16[512,512]{1,0:T(8,128)(2,1)S(1)}, u32[]{:S(2)}) copy-start(bf16[512,512]{1,0:T(8,128)(2,1)S(1)} %get-tuple-element.461) | copy-start | bytes 1572868
  244.5 3.6 copy-start.87
  248.1 24.9 %copy-start.14 = (f32[1024,512]{0,1:T(8,128)}, f32[1024,512]{0,1:T(8,128)S(1)}, u32[]{:S(2)}) copy-start(f32[1024,512]{0,1:T(8,128)S(1)} %convolution_add_fusion.2) | copy-start | bytes 6291460
  281.5 5.7 copy-start.22
  281.5 5.7 copy-start.23
  281.5 5.7 copy-start.26
  281.5 5.7 copy-start.27
  283.4 29.0 %copy-start.18 = (f32[256,512]{1,0:T(8,128)}, f32[256,512]{1,0:T(8,128)S(1)}, u32[]{:S(2)}) copy-start(f32[256,512]{1,0:T(8,128)S(1)} %get-tuple-element.499) | copy-start | bytes 1572868
  309.3 3.1 copy-start.37
  370.7 9.1 slice-start
  373.2 3.7 copy-start.10
  375.7 4.2 slice-start.1
  391.9 5.0 copy-start.17
  391.9 5.0 copy-start.40
  392.0 5.0 copy-start.42
  392.0 5.0 copy-start.44
  392.0 5.0 copy-start.46
  404.7 115.8 %copy-start.4 = (f32[1024,512]{0,1:T(8,128)}, f32[1024,512]{0,1:T(8,128)S(1)}, u32[]{:S(2)}) copy-start(f32[1024,512]{0,1:T(8,128)S(1)} %fusion.109) | copy-start | bytes 6291460
  413.8 95.5 %copy-start.65 = (bf16[512,512]{1,0:T(8,128)(2,1)S(1)}, bf16[512,512]{1,0:T(8,128)(2,1)}, u32[]{:S(2)}) copy-start(bf16[512,512]{1,0:T(8,128)(2,1)} %copy-done.64) | copy-start | bytes 1572868
  413.8 95.5 %copy-start.77 = (f32[1024]{0:T(1024)S(1)}, f32[1024]{0:T(1024)}, u32[]{:S(2)}) copy-start(f32[1024]{0:T(1024)} %copy-done.76) | copy-start | bytes 12292
  413.8 95.5 %copy-start.80 = (f32[1,512]{1,0:T(1,128)S(1)}, f32[1,512]{1,0:T(1,128)}, u32[]{:S(2)}) copy-start(f32[1,512]{1,0:T(1,128)} %copy-done.79) | copy-start | bytes 6148
  509.3 5.1 copy-start.8
  509.3 5.1 copy-start.34
  509.4 5.1 copy-start.35
  509.4 5.1 copy-start.36
  524.1 3.3 copy-start.24
  537.9 3.2 copy-start.11
  551.3 336.5 %reduce-scatter.5.cloned.1.call-start = ((), (), s32[]{:S(2)}) async-start(), calls=%async_computation.6 | async-start | bytes 6553600 | tf_op jit(solution)/shard_map/reduce_scatter | solution.py:441
  827.8 6.5 copy-start.78
  827.9 6.5 copy-start.84
  827.9 104.9 %copy-start.69 = (f32[6,512]{1,0:T(8,128)S(1)}, f32[6,512]{1,0:T(8,128)}, u32[]{:S(2)}) copy-start(f32[6,512]{1,0:T(8,128)} %param.29) | copy-start | bytes 36868
  827.9 104.9 %copy-start.74 = (f32[6,512]{1,0:T(8,128)S(1)}, f32[6,512]{1,0:T(8,128)}, u32[]{:S(2)}) copy-start(f32[6,512]{1,0:T(8,128)} %param.31) | copy-start | bytes 36868
  827.9 104.9 %copy-start.75 = (f32[6,512]{1,0:T(8,128)S(1)}, f32[6,512]{1,0:T(8,128)}, u32[]{:S(2)}) copy-start(f32[6,512]{1,0:T(8,128)} %param.30) | copy-start | bytes 36868
  827.9 105.5 %copy-start.21 = (f32[10,64,512]{2,1,0:T(8,128)S(1)}, f32[10,64,512]{2,1,0:T(8,128)}, u32[]{:S(2)}) copy-start(f32[10,64,512]{2,1,0:T(8,128)} %param.26) | copy-start | bytes 3932164
  887.8 45.6 %copy-start.20 = (f32[10,64,512]{2,1,0:T(8,128)S(1)}, f32[10,64,512]{2,1,0:T(8,128)}, u32[]{:S(2)}) copy-start(f32[10,64,512]{2,1,0:T(8,128)} %reduce-scatter.5.cloned.1.call-done) | copy-start | bytes 3932164
  933.4 5.2 copy-start.1
  (47 other events, 105.0 us)
Sparse Core Ops, SparseCore 0:
  10.4 42.3 all-gather.2
  56.8 125.3 all-gather.4
  551.4 265.1 reduce-scatter.2
  828.0 59.7 reduce-scatter.4

commit v2 on v1

--- a/solution.py
+++ b/solution.py
@@ -1,6 +1,10 @@
+import functools
+
 import jax
 import jax.numpy as jnp
 from jax import lax
+from jax.experimental import pallas as pl
+from jax.experimental.pallas import tpu as pltpu
 from jax.sharding import PartitionSpec as P
 
 HEADS = 8
@@ -328,60 +332,654 @@
     return (updated, new_first, new_second)
 
 
+MESH = pl.DeviceIdType.MESH
+VMEM_LIMIT = 60 * 1024 * 1024
+
+
+def remote(src, dst, send_sem, recv_sem, peer):
+    return pltpu.make_async_remote_copy(
+        src_ref=src, dst_ref=dst, send_sem=send_sem, recv_sem=recv_sem, device_id=peer, device_id_type=MESH
+    )
+
+
+def places():
+    dp = lax.axis_index("dp")
+    seq = lax.axis_index("seq")
+    return dp, seq, dp // 2, dp % 2
+
+
+def seq_peer(seq, step):
+    return ((seq // 2 + step // 2) % 2) * 2 + (seq % 2 + step % 2) % 2
+
+
+def meet(peers):
+    barrier = pltpu.get_barrier_semaphore()
+    for peer in peers:
+        pl.semaphore_signal(barrier, inc=1, device_id=peer, device_id_type=MESH)
+    pl.semaphore_wait(barrier, len(peers))
+
+
+def gather_kernel(
+    chunks, slot_ref, low_ref, ids_ref, full_ref, ids_out, slots, own, x_send, x_recv, own_sem,
+    n_send, n_recv, f_send, f_recv, c_send, c_recv, i_send, i_recv, i_own,
+):
+    dp, seq, z, core = places()
+    held, rows, _ = low_ref.shape
+    tile_count = full_ref.shape[0]
+    half = tile_count // 2
+    step_rows = rows // chunks
+    sibling = (z * 2 + 1 - core, seq)
+    up, down = ((z + 1) % 4 * 2 + core, seq), ((z + 3) % 4 * 2 + core, seq)
+    side = [(dp, seq_peer(seq, j)) for j in (1, 2, 3)]
+    meet([sibling, up, down] + side)
+
+    def rows_of(owner_z, chunk):
+        return pl.ds(pl.multiple_of((owner_z * 2 + core) * rows + chunk * step_rows, step_rows), step_rows)
+
+    def part(chunk):
+        return pl.ds(chunk * step_rows, step_rows)
+
+    side_copies = []
+    for chunk in range(chunks):
+        for j in range(3):
+            copy = remote(
+                low_ref.at[:, part(chunk)], slots[chunk].at[pl.ds(held * seq, held)],
+                x_send.at[chunk, j], x_recv.at[chunk, j], side[j],
+            )
+            copy.start()
+            side_copies.append(copy)
+        for j in range(3):
+            if chunk == 0:
+                copy = remote(
+                    ids_ref.at[side[j][1]], ids_out.at[seq], i_send.at[j], i_recv.at[j], side[j]
+                )
+                copy.start()
+                side_copies.append(copy)
+        slots[chunk][pl.ds(held * seq, held)] = low_ref[:, part(chunk), :]
+    ids_copy = pltpu.make_async_copy(ids_ref.at[seq], ids_out.at[seq], i_own)
+    ids_copy.start()
+
+    def near(chunk):
+        for j in range(3):
+            remote(
+                low_ref.at[:, part(chunk)], slots[chunk].at[pl.ds(held * seq, held)],
+                x_send.at[chunk, j], x_recv.at[chunk, j], side[j],
+            ).wait_recv()
+
+        def pick(tile, carry):
+            own[chunk, tile] = slots[chunk][slot_ref[tile]]
+            return carry
+
+        lax.fori_loop(0, tile_count, pick, 0)
+        place = full_ref.at[:, rows_of(z, chunk)]
+        for way, peer in enumerate((up, down)):
+            copy = remote(own.at[chunk], place, n_send.at[chunk, way], n_recv.at[chunk, way], peer)
+            copy.start()
+        copy = remote(own.at[chunk], place, c_send.at[chunk, 0], c_recv.at[chunk, 0], sibling)
+        copy.start()
+        copy = pltpu.make_async_copy(own.at[chunk], place, own_sem.at[chunk])
+        copy.start()
+
+    def far(chunk):
+        for way, peer in enumerate((up, down)):
+            origin = (z + 3) % 4 if way == 0 else (z + 1) % 4
+            place = full_ref.at[:, rows_of(origin, chunk)]
+            remote(own.at[chunk], place, n_send.at[chunk, way], n_recv.at[chunk, way], peer).wait_recv()
+            portion = full_ref.at[pl.ds(way * half, half), rows_of(origin, chunk)]
+            copy = remote(portion, portion, f_send.at[chunk, way], f_recv.at[chunk, way], peer)
+            copy.start()
+            copy = remote(place, place, c_send.at[chunk, 1 + way], c_recv.at[chunk, 1 + way], sibling)
+            copy.start()
+
+    def last(chunk):
+        for way, peer in enumerate((up, down)):
+            portion = full_ref.at[pl.ds(way * half, half), rows_of((z + 2) % 4, chunk)]
+            remote(portion, portion, f_send.at[chunk, way], f_recv.at[chunk, way], peer).wait_recv()
+            copy = remote(portion, portion, c_send.at[chunk, 3 + way], c_recv.at[chunk, 3 + way], sibling)
+            copy.start()
+
+    for tick in range(chunks + 2):
+        if tick < chunks:
+            near(tick)
+        if 0 <= tick - 1 < chunks:
+            far(tick - 1)
+        if 0 <= tick - 2 < chunks:
+            last(tick - 2)
+    for copy in side_copies:
+        copy.wait_send()
+    for j in range(3):
+        remote(ids_ref.at[side[j][1]], ids_out.at[seq], i_send.at[j], i_recv.at[j], side[j]).wait_recv()
+    ids_copy.wait()
+    for chunk in range(chunks):
+        place = full_ref.at[:, rows_of(z, chunk)]
+        for way, peer in enumerate((up, down)):
+            remote(own.at[chunk], place, n_send.at[chunk, way], n_recv.at[chunk, way], peer).wait_send()
+            portion = full_ref.at[pl.ds(way * half, half), rows_of(z, chunk)]
+            remote(portion, portion, f_send.at[chunk, way], f_recv.at[chunk, way], peer).wait_send()
+        pltpu.make_async_copy(own.at[chunk], place, own_sem.at[chunk]).wait()
+        for turn in range(5):
+            piece = full_ref.at[:, rows_of(z, chunk)] if turn < 3 else full_ref.at[pl.ds(0, half), rows_of(z, chunk)]
+            remote(piece, piece, c_send.at[chunk, turn], c_recv.at[chunk, turn], sibling).wait()
+
+
+def gather_tiles_kernel(low, ids, owner_slot):
+    held, rows, width = low.shape
+    tile_count = owner_slot.shape[0]
+    seq_count, dp_count = lax.axis_size("seq"), lax.axis_size("dp")
+    chunks = 4
+    step_rows = rows // chunks
+    dma = pltpu.SemaphoreType.DMA
+    return pl.pallas_call(
+        functools.partial(gather_kernel, chunks),
+        out_shape=(
+            jax.ShapeDtypeStruct((tile_count, dp_count * rows, width), low.dtype),
+            jax.ShapeDtypeStruct(ids.shape, ids.dtype),
+        ),
+        in_specs=[
+            pl.BlockSpec(memory_space=pltpu.SMEM),
+            pl.BlockSpec(memory_space=pltpu.VMEM),
+            pl.BlockSpec(memory_space=pltpu.VMEM),
+        ],
+        out_specs=(pl.BlockSpec(memory_space=pl.ANY), pl.BlockSpec(memory_space=pltpu.VMEM)),
+        scratch_shapes=[
+            [pltpu.VMEM((seq_count * held, step_rows, width), low.dtype)] * chunks,
+            pltpu.VMEM((chunks, tile_count, step_rows, width), low.dtype),
+            dma((chunks, 3)), dma((chunks, 3)), dma((chunks,)),
+            dma((chunks, 2)), dma((chunks, 2)), dma((chunks, 2)), dma((chunks, 2)),
+            dma((chunks, 5)), dma((chunks, 5)), dma((3,)), dma((3,)), dma,
+        ],
+        name="gather_tiles",
+        compiler_params=pltpu.CompilerParams(
+            collective_id=0, has_side_effects=True, vmem_limit_bytes=VMEM_LIMIT
+        ),
+    )(owner_slot, low, ids)
+
+
+CODE_TOP = 32000.0
+ROUNDER = 12582912.0
+
+
+def encode(value):
+    upper, lower = value[0:8, :], value[8:16, :]
+    size = jnp.maximum(jnp.abs(upper), jnp.abs(lower))
+    most = jnp.maximum(jnp.max(size, axis=1, keepdims=True), 1e-30)
+    ratio = CODE_TOP / most
+    coded = jnp.concatenate([upper * ratio, lower * ratio], axis=0)
+    coded = ((coded + ROUNDER) - ROUNDER).astype(jnp.int32).astype(jnp.int16)
+    return coded, most * (1.0 / CODE_TOP)
+
+
+def decode(coded, unit):
+    value = coded.astype(jnp.int32).astype(jnp.float32)
+    return jnp.concatenate([value[0:8, :] * unit, value[8:16, :] * unit], axis=0)
+
+
+def reduce_kernel(
+    source_ref, valid_ref, grads_ref, small_ref, out_ref, small_out, square_out,
+    own, other, b1_out, b1_in, b2_out, b2_in, c_out, c_in, d_out, d_in,
+    b1_unit_out, b1_unit_in, b2_unit_out, b2_unit_in, c_unit_out, c_unit_in, d_unit_out, d_unit_in,
+    final, small_dp, small_seq, square_dp, square_seq,
+    l_sem, a_send, a_recv, b1_send, b1_recv, b2_send, b2_recv, c_send, c_recv, d_send, d_recv,
+    p_send, p_recv, q_send, q_recv, r_send, r_recv, s_send, s_recv,
+):
+    dp, seq, z, core = places()
+    across, along = seq % 2, seq // 2
+    held = out_ref.shape[0]
+    tile_count = grads_ref.shape[0]
+    pairs = tile_count // 2
+    sibling = (z * 2 + 1 - core, seq)
+    beside = [(dp, along * 2 + 1 - across), (dp, (1 - along) * 2 + across)]
+    side = [(dp, seq_peer(seq, j)) for j in (1, 2, 3)]
+    column = [((dp + j) % 8, seq) for j in range(1, 8)]
+    tower = [((z + j) % 4 * 2 + core, seq) for j in (1, 2, 3)]
+    meet(side + column)
+    lane = lax.broadcasted_iota(jnp.int32, (8, 128), 1)
+
+    def core_copy(pair):
+        two = pl.ds(pair * 2, 2)
+        return remote(grads_ref.at[two, :, 1 - core], other.at[two], a_send.at[pair], a_recv.at[pair], sibling)
+
+    def local_copy(pair):
+        two = pl.ds(pair * 2, 2)
+        return pltpu.make_async_copy(grads_ref.at[two, :, core], own.at[two], l_sem.at[pair])
+
+    def with_units(values, units, send, recv, peer):
+        return [
+            remote(values[0], values[1], send.at[0], recv.at[0], peer),
+            remote(units[0], units[1], send.at[1], recv.at[1], peer),
+        ]
+
+    def first_copies(pair, order):
+        tile = pair * 2 + order
+        return with_units(
+            (b1_out.at[tile], b1_in.at[tile]), (b1_unit_out.at[tile], b1_unit_in.at[tile]),
+            b1_send.at[tile], b1_recv.at[tile], beside[order],
+        )
+
+    def second_copies(pair, order):
+        tile = pair * 2 + order
+        return with_units(
+            (b2_out.at[tile], b2_in.at[tile]), (b2_unit_out.at[tile], b2_unit_in.at[tile]),
+            b2_send.at[tile], b2_recv.at[tile], beside[1 - order],
+        )
+
+    def tower_copies(pair, j):
+        two = pl.ds(pair * 2, 2)
+        return with_units(
+            (c_out.at[j, two], c_in.at[j, two]), (c_unit_out.at[j, pair], c_unit_in.at[j, pair]),
+            c_send.at[j, pair], c_recv.at[j, pair], tower[j],
+        )
+
+    def share_copies(pair, j):
+        two = pl.ds(pair * 2, 2)
+        return with_units(
+            (d_out.at[two], d_in.at[j, two]), (d_unit_out.at[pair], d_unit_in.at[j, pair]),
+            d_send.at[j, pair], d_recv.at[j, pair], side[j],
+        )
+
+    def start_all(copies):
+        for copy in copies:
+            copy.start()
+
+    def arrive_all(copies):
+        for copy in copies:
+            copy.wait_recv()
+
+    def sent_all(copies):
+        for copy in copies:
+            copy.wait_send()
+
+    def small_copy(j):
+        return remote(small_ref, small_dp.at[dp], p_send.at[j], p_recv.at[j], column[j])
+
+    def small_side(j):
+        return remote(small_seq.at[seq], small_seq.at[seq], q_send.at[j], q_recv.at[j], side[j])
+
+    def square_copy(j):
+        return remote(square_dp.at[dp], square_dp.at[dp], r_send.at[j], r_recv.at[j], column[j])
+
+    def square_side(j):
+        return remote(square_seq.at[seq], square_seq.at[seq], s_send.at[j], s_recv.at[j], side[j])
+
+    for j in range(7):
+        small_copy(j).start()
+
+    def launch(pair, carry):
+        core_copy(pair).start()
+        local_copy(pair).start()
+        return carry
+
+    lax.fori_loop(0, pairs, launch, 0)
+
+    def cell(tile, order, floor, line, mine):
+        if order == 0:
+            return (tile, floor, line, across if mine else 1 - across)
+        return (tile, floor, along if mine else 1 - along, line)
+
+    def stage_one(pair):
+        core_copy(pair).wait_recv()
+        local_copy(pair).wait()
+
+        def add(step, carry):
+            tile, floor = pair * 2 + step // 4, step % 4
+            own[tile, floor] = own[tile, floor] + other[tile, floor]
+            return carry
+
+        lax.fori_loop(0, 8, add, 0)
+        for order in range(2):
+            tile = pair * 2 + order
+            units = jnp.zeros((8, 128), jnp.float32)
+            for floor in range(4):
+                for line in range(2):
+                    coded, unit = encode(own[cell(tile, order, floor, line, False)])
+                    b1_out[tile, floor * 2 + line] = coded
+                    units = jnp.where(lane == floor * 2 + line, unit, units)
+            b1_unit_out[tile] = units
+            start_all(first_copies(pair, order))
+
+    def stage_two(pair):
+        for order in range(2):
+            tile = pair * 2 + order
+            arrive_all(first_copies(pair, order))
+            got = b1_unit_in[tile]
+            units = jnp.zeros((8, 128), jnp.float32)
+            keep = along if order == 0 else across
+            for floor in range(4):
+                for line in range(2):
+                    block = floor * 2 + line
+                    spot = cell(tile, order, floor, line, True)
+                    own[spot] = own[spot] + decode(b1_in[tile, block], got[:, block : block + 1])
+                spot = cell(tile, order, floor, 1 - keep, True)
+                coded, unit = encode(own[spot])
+                b2_out[tile, floor] = coded
+                units = jnp.where(lane == floor, unit, units)
+            b2_unit_out[tile] = units
+            start_all(second_copies(pair, order))
+
+    def stage_three(pair):
+        for order in range(2):
+            tile = pair * 2 + order
+            arrive_all(second_copies(pair, order))
+            got = b2_unit_in[tile]
+            for floor in range(4):
+                spot = (tile, floor, along, across)
+                own[spot] = own[spot] + decode(b2_in[tile, floor], got[:, floor : floor + 1])
+        for j in range(3):
+            units = jnp.zeros((8, 128), jnp.float32)
+            for order in range(2):
+                tile = pair * 2 + order
+                coded, unit = encode(own[tile, (z + j + 1) % 4, along, across])
+                c_out[j, tile] = coded
+                units = jnp.where(lane == order, unit, units)
+            c_unit_out[j, pair] = units
+            start_all(tower_copies(pair, j))
+
+    def stage_four(pair):
+        for j in range(3):
+            arrive_all(tower_copies(pair, j))
+        units = jnp.zeros((8, 128), jnp.float32)
+        for order in range(2):
+            tile = pair * 2 + order
+            total = own[tile, z, along, across]
+            for j in range(3):
+                total = total + decode(c_in[j, tile], c_unit_in[j, pair][:, order : order + 1])
+            final[tile, seq] = total
+            coded, unit = encode(total)
+            d_out[tile] = coded
+            units = jnp.where(lane == order, unit, units)
+        d_unit_out[pair] = units
+        for j in range(3):
+            start_all(share_copies(pair, j))
+
+    def stage_five(pair):
+        for j in range(3):
+            arrive_all(share_copies(pair, j))
+            for order in range(2):
+                tile = pair * 2 + order
+                final[tile, side[j][1]] = decode(d_in[j, tile], d_unit_in[j, pair][:, order : order + 1])
+
+    stages = (stage_one, stage_two, stage_three, stage_four, stage_five)
+    lag = 2
+
+    def tick(step, carry):
+        for number, stage in enumerate(stages):
+            pair = step - lag * number
+
+            @pl.when(jnp.logical_and(pair >= 0, pair < pairs))
+            def _():
+                stage(pair)
+
+        return carry
+
+    lax.fori_loop(0, 4, tick, 0)
+    small_dp[dp] = small_ref[...]
+    for j in range(7):
+        small_copy(j).wait_recv()
+    total = small_dp[0]
+    for j in range(1, 8):
+        total = total + small_dp[j]
+    small_seq[seq] = total
+    for j in range(3):
+        small_side(j).start()
+    lax.fori_loop(4, pairs + lag * 4, tick, 0)
+
+    def collect(slot, square):
+        keep = valid_ref[slot] > 0
+        for quarter in range(4):
+            value = final[source_ref[slot], quarter]
+            value = jnp.where(keep, value, jnp.zeros_like(value))
+            out_ref[slot, quarter * 16 : quarter * 16 + 16, :] = value
+            square = square + value * value
+        return square
+
+    square = lax.fori_loop(0, held, collect, jnp.zeros((16, out_ref.shape[2]), jnp.float32))
+    folded = square[0:8, 0:128]
+    for r in range(2):
+        for w in range(out_ref.shape[2] // 128):
+            if r or w:
+                folded = folded + square[8 * r : 8 * r + 8, 128 * w : 128 * w + 128]
+    square_dp[dp] = folded
+    for j in range(7):
+        square_copy(j).start()
+    for j in range(3):
+        small_side(j).wait_recv()
+    small_out[...] = (small_seq[0] + small_seq[1]) + (small_seq[2] + small_seq[3])
+    for j in range(7):
+        square_copy(j).wait_recv()
+    total = square_dp[0]
+    for j in range(1, 8):
+        total = total + square_dp[j]
+    square_seq[seq] = total
+    for j in range(3):
+        square_side(j).start()
+    for j in range(3):
+        square_side(j).wait_recv()
+    square_out[...] = (square_seq[0] + square_seq[1]) + (square_seq[2] + square_seq[3])
+    for j in range(7):
+        small_copy(j).wait_send()
+        square_copy(j).wait_send()
+    for j in range(3):
+        small_side(j).wait_send()
+        square_side(j).wait_send()
+
+    def drain(pair, carry):
+        core_copy(pair).wait_send()
+        for order in range(2):
+            sent_all(first_copies(pair, order))
+            sent_all(second_copies(pair, order))
+        for j in range(3):
+            sent_all(tower_copies(pair, j))
+            sent_all(share_copies(pair, j))
+        return carry
+
+    lax.fori_loop(0, pairs, drain, 0)
+
+
+def reduce_tiles_kernel(grads, small, source, valid, held):
+    tile_count, height, width = grads.shape
+    seq_count, dp_count = lax.axis_size("seq"), lax.axis_size("dp")
+    rows = height // dp_count
+    pairs = tile_count // 2
+    dma = pltpu.SemaphoreType.DMA
+    vmem = pl.BlockSpec(memory_space=pltpu.VMEM)
+    smem = pl.BlockSpec(memory_space=pltpu.SMEM)
+
+    def buffer(*shape):
+        return pltpu.VMEM(shape, jnp.float32)
+
+    def codes(*shape):
+        return pltpu.VMEM(shape + (16, width), jnp.int16)
+
+    return pl.pallas_call(
+        reduce_kernel,
+        out_shape=(
+            jax.ShapeDtypeStruct((held, rows, width), jnp.float32),
+            jax.ShapeDtypeStruct(small.shape, jnp.float32),
+            jax.ShapeDtypeStruct((8, 128), jnp.float32),
+        ),
+        in_specs=[smem, smem, pl.BlockSpec(memory_space=pl.ANY), vmem],
+        out_specs=(vmem, vmem, vmem),
+        scratch_shapes=[
+            buffer(tile_count, 4, 2, 2, 16, width),
+            buffer(tile_count, 4, 2, 2, 16, width),
+            codes(tile_count, 8), codes(tile_count, 8),
+            codes(tile_count, 4), codes(tile_count, 4),
+            codes(3, tile_count), codes(3, tile_count),
+            codes(tile_count), codes(3, tile_count),
+            buffer(tile_count, 8, 128), buffer(tile_count, 8, 128),
+            buffer(tile_count, 8, 128), buffer(tile_count, 8, 128),
+            buffer(3, pairs, 8, 128), buffer(3, pairs, 8, 128),
+            buffer(pairs, 8, 128), buffer(3, pairs, 8, 128),
+            buffer(tile_count, 4, 16, width),
+            buffer(dp_count, *small.shape),
+            buffer(seq_count, *small.shape),
+            buffer(dp_count, 8, 128),
+            buffer(seq_count, 8, 128),
+            dma((pairs,)), dma((pairs,)), dma((pairs,)),
+            dma((tile_count, 2)), dma((tile_count, 2)), dma((tile_count, 2)), dma((tile_count, 2)),
+            dma((3, pairs, 2)), dma((3, pairs, 2)), dma((3, pairs, 2)), dma((3, pairs, 2)),
+            dma((7,)), dma((7,)), dma((3,)), dma((3,)), dma((7,)), dma((7,)), dma((3,)), dma((3,)),
+        ],
+        name="reduce_tiles",
+        compiler_params=pltpu.CompilerParams(
+            collective_id=1, has_side_effects=True, vmem_limit_bytes=VMEM_LIMIT
+        ),
+    )(source, valid, grads.reshape(tile_count, 4, 2, 2, 2, 16, width), small)
+
+
+def column_kernel(value_ref, out_ref, gathered, send, recv):
+    dp, seq, _, _ = places()
+    column = [((dp + j) % 8, seq) for j in range(1, 8)]
+    meet(column)
+    gathered[dp] = value_ref[...]
+    copies = [
+        remote(value_ref, gathered.at[dp], send.at[j], recv.at[j], column[j]) for j in range(7)
+    ]
+    for copy in copies:
+        copy.start()
+    for copy in copies:
+        copy.wait()
+    total = gathered[0]
+    for j in range(1, 8):
+        total = total + gathered[j]
+    out_ref[...] = total
+
+
+def column_sum(value):
+    vmem = pl.BlockSpec(memory_space=pltpu.VMEM)
+    return pl.pallas_call(
+        column_kernel,
+        out_shape=jax.ShapeDtypeStruct(value.shape, value.dtype),
+        in_specs=[vmem],
+        out_specs=vmem,
+        scratch_shapes=[
+            pltpu.VMEM((lax.axis_size("dp"),) + value.shape, value.dtype),
+            pltpu.SemaphoreType.DMA((7,)),
+            pltpu.SemaphoreType.DMA((7,)),
+        ],
+        name="column_sum",
+        compiler_params=pltpu.CompilerParams(collective_id=2, has_side_effects=True),
+    )(value)
+
+
+def head_mask(shape, head):
+    lane = lax.broadcasted_iota(jnp.int32, shape, 1)
+    return (lane >= 64) if head else (lane < 64)
+
+
+def scores_t(k_pair, q_head, first_row):
+    scores = product_nt(k_pair, q_head)
+    count, queries = scores.shape
+    key = lax.broadcasted_iota(jnp.int32, (queries, queries), 0)
+    query = lax.broadcasted_iota(jnp.int32, (queries, queries), 1)
+    own = jnp.where(key <= query, scores[first_row:], MASKED)
+    return own if first_row == 0 else jnp.concatenate([scores[:first_row], own], axis=0)
+
+
+def attention_forward_kernel(q_ref, k_ref, v_ref, out_ref, log_ref, turned):
+    length, lanes = q_ref.shape
+    step = 256
+    factor = (lanes // 2) ** (-0.5)
+    turned[...] = v_ref[...].astype(jnp.float32).T.astype(jnp.bfloat16)
+    for first in range(0, length, step):
+        q_pair = q_ref[first : first + step, :] * jnp.asarray(factor, jnp.bfloat16)
+        pieces = []
+        for head in range(2):
+            q_head = jnp.where(head_mask(q_pair.shape, head), q_pair, jnp.zeros_like(q_pair))
+            scores = scores_t(k_ref[: first + step, :], q_head, first)
+            peak = jnp.max(scores, axis=0, keepdims=True)
+            raised = jnp.exp(scores - peak)
+            total = jnp.sum(raised, axis=0, keepdims=True)
+            weights = (raised * (1.0 / total)).astype(jnp.bfloat16)
+            log_ref[0, head : head + 1, first : first + step] = peak + jnp.log(total)
+            pieces.append(product(turned[64 * head : 64 * head + 64, : first + step], weights))
+        out_ref[first : first + step, :] = jnp.concatenate(pieces, axis=0).T.astype(out_ref.dtype)
+
+
+def attention_backward_kernel(q_ref, k_ref, v_ref, up_ref, log_ref, dq_ref, dk_ref, dv_ref, turned, dk_sum, dv_sum):
+    length, lanes = q_ref.shape
+    step = 256
+    factor = (lanes // 2) ** (-0.5)
+    turned[...] = k_ref[...].astype(jnp.float32).T.astype(jnp.bfloat16)
+    for first in reversed(range(0, length, step)):
+        span = first + step
+        q_pair = q_ref[first:span, :] * jnp.asarray(factor, jnp.bfloat16)
+        up_pair = up_ref[first:span, :]
+        queries, keys, values = [], [], []
+        for head in range(2):
+            keep = head_mask(q_pair.shape, head)
+            q_head = jnp.where(keep, q_pair, jnp.zeros_like(q_pair))
+            up_head = jnp.where(keep, up_pair, jnp.zeros_like(up_pair))
+            scores = scores_t(k_ref[:span, :], q_head, first)
+            weights = jnp.exp(scores - log_ref[0, head : head + 1, first:span])
+            grad_weights = product_nt(v_ref[:span, :], up_head)
+            values.append(product(weights.astype(jnp.bfloat16), up_head))
+            inner_sum = jnp.sum(weights * grad_weights, axis=0, keepdims=True)
+            grad_scores = (weights * (grad_weights - inner_sum)).astype(jnp.bfloat16)
+            keys.append(product(grad_scores, q_head))
+            queries.append(product(turned[64 * head : 64 * head + 64, :span], grad_scores))
+        dq_ref[first:span, :] = (jnp.concatenate(queries, axis=0).T * factor).astype(dq_ref.dtype)
+        grad_key = keys[0] + keys[1]
+        grad_value = values[0] + values[1]
+        if span == length:
+            dk_sum[...] = grad_key
+            dv_sum[...] = grad_value
+        else:
+            dk_sum[:span, :] = dk_sum[:span, :] + grad_key
+            dv_sum[:span, :] = dv_sum[:span, :] + grad_value
+    dk_ref[...] = dk_sum[...].astype(dk_ref.dtype)
+    dv_ref[...] = dv_sum[...].astype(dv_ref.dtype)
+
+
+def attention_specs(length, lanes, pairs):
+    return [pl.BlockSpec((length, lanes), lambda p, j=j: (0, j * pairs + p)) for j in range(3)]
+
+
 def attention_whole(qkv_low, model_width, head_width):
     length = qkv_low.shape[0]
-    allowed = jnp.arange(length)[:, None] >= jnp.arange(length)[None, :]
-    factor = head_width ** (-0.5)
-
-    def head_forward(triple):
-        q_head, k_head, v_head = triple
-        scores = jnp.where(allowed, product_nt(q_head, k_head) * factor, MASKED)
-        peak = jnp.max(scores, axis=1, keepdims=True)
-        log_total = peak + jnp.log(jnp.sum(jnp.exp(scores - peak), axis=1, keepdims=True))
-        weights = jnp.exp(scores - log_total).astype(jnp.bfloat16)
-        return (product(weights, v_head), log_total[:, 0])
-
-    head_out, log_totals = lax.map(
-        head_forward,
-        (
-            split_heads(qkv_low[:, :model_width]),
-            split_heads(qkv_low[:, model_width : 2 * model_width]),
-            split_heads(qkv_low[:, 2 * model_width :]),
+    lanes = 2 * head_width
+    pairs = model_width // lanes
+    return pl.pallas_call(
+        attention_forward_kernel,
+        out_shape=(
+            jax.ShapeDtypeStruct((length, model_width), jnp.bfloat16),
+            jax.ShapeDtypeStruct((pairs, 2, length), jnp.float32),
         ),
-    )
-    return (join_heads(head_out).astype(jnp.bfloat16), log_totals)
+        grid=(pairs,),
+        in_specs=attention_specs(length, lanes, pairs),
+        out_specs=(
+            pl.BlockSpec((length, lanes), lambda p: (0, p)),
+            pl.BlockSpec((1, 2, length), lambda p: (p, 0, 0)),
+        ),
+        scratch_shapes=[pltpu.VMEM((lanes, length), jnp.bfloat16)],
+        name="attention_forward",
+        compiler_params=pltpu.CompilerParams(vmem_limit_bytes=VMEM_LIMIT),
+    )(qkv_low, qkv_low, qkv_low)
 
 
 def attention_whole_back(qkv_low, grad_attended, log_totals, model_width, head_width):
     length = qkv_low.shape[0]
-    allowed = jnp.arange(length)[:, None] >= jnp.arange(length)[None, :]
-    factor = head_width ** (-0.5)
-
-    def head_backward(bundle):
-        q_head, k_head, v_head, upstream, log_head = bundle
-        scores = jnp.where(allowed, product_nt(q_head, k_head) * factor, MASKED)
-        weights = jnp.exp(scores - log_head[:, None])
-        grad_values = product_tn(weights.astype(jnp.bfloat16), upstream)
-        grad_weights = product_nt(upstream, v_head)
-        inner_sum = jnp.sum(weights * grad_weights, axis=1, keepdims=True)
-        grad_scores = (weights * (grad_weights - inner_sum)).astype(jnp.bfloat16)
-        return (
-            product(grad_scores, k_head) * factor,
-            product_tn(grad_scores, q_head) * factor,
-            grad_values,
-        )
-
-    grads = lax.map(
-        head_backward,
-        (
-            split_heads(qkv_low[:, :model_width]),
-            split_heads(qkv_low[:, model_width : 2 * model_width]),
-            split_heads(qkv_low[:, 2 * model_width :]),
-            split_heads(grad_attended),
-            log_totals,
-        ),
-    )
-    return jnp.concatenate([join_heads(piece) for piece in grads], axis=1).astype(jnp.bfloat16)
+    lanes = 2 * head_width
+    pairs = model_width // lanes
+    grads = pl.pallas_call(
+        attention_backward_kernel,
+        out_shape=tuple(jax.ShapeDtypeStruct((length, model_width), jnp.bfloat16) for _ in range(3)),
+        grid=(pairs,),
+        in_specs=attention_specs(length, lanes, pairs)
+        + [
+            pl.BlockSpec((length, lanes), lambda p: (0, p)),
+            pl.BlockSpec((1, 2, length), lambda p: (p, 0, 0)),
+        ],
+        out_specs=tuple(pl.BlockSpec((length, lanes), lambda p: (0, p)) for _ in range(3)),
+        scratch_shapes=[
+            pltpu.VMEM((lanes, length), jnp.bfloat16),
+            pltpu.VMEM((length, lanes), jnp.float32),
+            pltpu.VMEM((length, lanes), jnp.float32),
+        ],
+        name="attention_backward",
+        compiler_params=pltpu.CompilerParams(vmem_limit_bytes=VMEM_LIMIT),
+    )(qkv_low, qkv_low, qkv_low, grad_attended, log_totals)
+    return jnp.concatenate(grads, axis=1)
 
 
 def whole_forward(hidden_in, tiles, gain_attn, gain_ffn):
@@ -425,22 +1023,6 @@
     return (grad_in, pieces, grad_gain_attn, grad_gain_ffn)
 
 
-def gather_tiles_whole(master, owner_slot):
-    shard_low = master.astype(jnp.bfloat16)
-    all_slots = lax.all_gather(shard_low, "seq", axis=0, tiled=True)
-    picked = jnp.take(all_slots, owner_slot, axis=0)
-    return lax.all_gather(picked, "dp", axis=1, tiled=True)
-
-
-def reduce_tiles_whole(tile_grads, owner_slot, slot_count):
-    rows_own = lax.psum_scatter(tile_grads, "dp", scatter_dimension=1, tiled=True)
-    hot = (jnp.arange(slot_count)[:, None] == owner_slot[None, :])
-    source = jnp.sum(jnp.where(hot, jnp.arange(owner_slot.shape[0])[None, :], 0), axis=1)
-    owned = jnp.any(hot, axis=1)[:, None, None]
-    placed = jnp.where(owned, jnp.take(rows_own, source, axis=0), 0.0)
-    return lax.psum_scatter(placed, "seq", scatter_dimension=0, tiled=True)
-
-
 def whole_step(char_ids, targets, seg_ids, lengths, owner_slot, master, gain_rows):
     micro_count = char_ids.shape[0]
     seq_count = lax.axis_size("seq")
@@ -449,10 +1031,10 @@
     vocab_size = model_width // 2
     seg_total = SEG_DEV * seq_count
     ids = jnp.stack([char_ids[:, 0], targets[:, 0], seg_ids[:, 0]], axis=1)
-    ids = lax.all_to_all(ids, "seq", split_axis=0, concat_axis=2, tiled=True)[0]
-    chars_row, target_row, segment_row = ids[0], ids[1], ids[2]
+    ids = jnp.pad(ids, ((0, 0), (0, 5), (0, 0)))
+    tiles, ids = gather_tiles_kernel(master.astype(jnp.bfloat16), ids, owner_slot)
+    chars_row, target_row, segment_row = (ids[:, i].reshape(-1) for i in range(3))
     length_one = lax.dynamic_index_in_dim(lengths[:, 0], seq_me, keepdims=False)
-    tiles = gather_tiles_whole(master, owner_slot)
     char_count = chars_row.shape[0]
     is_valid = (jnp.arange(char_count) < length_one).astype(jnp.float32)
     vocab_iota = jnp.arange(vocab_size)
@@ -465,9 +1047,9 @@
     boundary_hidden = jnp.tanh(product(char_low, tiles[24]))
     root_width = model_width ** (-0.5)
     boundary_prob = jax.nn.sigmoid(jnp.sum(boundary_hidden * gain_rows[5], axis=1) * root_width)
-    soft_count, count_all = lax.psum(
-        (jnp.sum(is_valid * boundary_prob), length_one.astype(jnp.float32)), "dp"
-    )
+    counts = jnp.stack([jnp.sum(is_valid * boundary_prob), length_one.astype(jnp.float32)])
+    counts = column_sum(jnp.pad(counts[:, None], ((0, 6), (0, 127))))
+    soft_count, count_all = counts[0, 0], counts[1, 0]
     slot_iota = jnp.arange(seg_total)
     pool_hot = segment_row[None, :] + 1 == slot_iota[:, None]
     lift_hot = segment_row[:, None] == slot_iota[None, :]
@@ -563,14 +1145,21 @@
     micro_count = char_ids.shape[0]
     model_width = master.shape[2]
     slot_count = master.shape[0] * lax.axis_size("seq")
-    if micro_count == lax.axis_size("seq"):
+    if (micro_count, lax.axis_size("seq"), lax.axis_size("dp")) == (4, 4, 8):
         tile_grads, gain_part, loss_part = whole_step(
             char_ids, targets, seg_ids, lengths, owner_slot, master, gain_rows
         )
-        shard_total = reduce_tiles_whole(tile_grads, owner_slot, slot_count)
-        gain_sum, square_sum, loss_total = lax.psum(
-            (gain_part, jnp.sum(shard_total * shard_total), loss_part), ("dp", "seq")
+        local = lax.axis_index("seq") * master.shape[0] + jnp.arange(master.shape[0])
+        hot = local[:, None] == owner_slot[None, :]
+        valid = jnp.any(hot, axis=1).astype(jnp.int32)
+        source = jnp.sum(jnp.where(hot, jnp.arange(owner_slot.shape[0])[None, :], 0), axis=1)
+        small = jnp.concatenate(
+            [gain_part, jnp.pad(loss_part.reshape(1, 1), ((0, 1), (0, model_width - 1)))]
         )
+        shard_total, small, squares = reduce_tiles_kernel(
+            tile_grads, small, source, valid, master.shape[0]
+        )
+        gain_sum, loss_total, square_sum = small[0:6], small[6, 0], jnp.sum(squares)
     else:
         tile_total = jnp.zeros((owner_slot.shape[0], model_width, model_width), jnp.float32)
         gain_total = jnp.zeros_like(gain_rows)

time: 954 us -> 503 us (0.53)
  waiting for transfers between devices: 481 us -> 0 us
  Pallas kernels: 0 us -> 293 us
  matrix products: 264 us -> 97.2 us
  blocking collectives: 55.5 us -> 0 us
  other arithmetic: 40.8 us -> 20.2 us
  between operations: 31.1 us -> 17 us
    reduce_scatter x2 -> x0, waiting for transfers between devices: 318 us -> none  [the longest x1 264 us: reduce_tiles_whole(): lax.psum_scatter(tile_grads, 'dp', scatter_dimension=1, tiled=True)]
    pallas_call x0 -> x7, Pallas kernels: none -> 293 us  [the longest x1 128 us: gather_tiles_kernel(): pl.pallas_call(functools.partial(gather_kernel, chunks), out_shape=(jax.S...]
    all_gather x2 -> x0, waiting for transfers between devices: 160 us -> none  [the longest x1 117 us: gather_tiles_whole(): return lax.all_gather(picked, 'dp', axis=1, tiled=True)]
    dot_general x58 -> x10, matrix products: 102 us -> 35.5 us  [product_nt(): lax.dot_general(left, right, (((1,), (1,)), ((), ())), preferred_element_...]
    dot_general x42 -> x10, matrix products: 81.8 us -> 24.4 us  [product_tn(): lax.dot_general(left, right, (((0,), (0,)), ((), ())), preferred_element_...]
    psum x2 -> x0, blocking collectives: 55.5 us -> none  [the longest x1 40.6 us: body(): lax.psum((gain_part, jnp.sum(shard_total * shard_total), loss_part), ('dp...]
    dot_general x44 -> x12, matrix products: 75.3 us -> 29.8 us  [product(): return jnp.dot(left, right, preferred_element_type=jnp.float32)]
    unnamed x208 -> x211, local copies, waits for them, and re-layouts: 34.8 us -> 40.6 us
  transfers between devices with their start and end apart: 5 -> 0, of which waited for: 5 -> 0; matrix products, arithmetic and copies ran while one was open for 0% -> 0% of each run, Pallas kernels for 0% -> 0%
where the time goes in v2:
time: 503 us; the launch traced here: 495 us
  Pallas kernels  293 us (58%)
  matrix products  97.2 us (19%)
  local copies, waits for them, and re-layouts  67.2 us (13%)
  other arithmetic  20.2 us (4%)
  between operations  17 us (3%)
    pallas_call x1, Pallas kernels, gather_tiles_kernel(): pl.pallas_call(functools.partial(gather_kernel, chunks), out_shape=(jax.S...  128 us
    pallas_call x1, Pallas kernels, reduce_tiles_kernel(): pl.pallas_call(reduce_kernel, out_shape=(jax.ShapeDtypeStruct((held, rows...  103 us
    unnamed x211, local copies, waits for them, and re-layouts  40.6 us
    dot_general x10, matrix products, product_nt(): lax.dot_general(left, right, (((1,), (1,)), ((), ())), preferred_element_...  35.5 us
    dot_general x12, matrix products, product(): return jnp.dot(left, right, preferred_element_type=jnp.float32)  29.8 us
    pallas_call x2, Pallas kernels, attention_whole_back(): pl.pallas_call(attention_backward_kernel, out_shape=tuple((jax.ShapeDtype...  27.6 us
    pallas_call x2, Pallas kernels, attention_whole(): pl.pallas_call(attention_forward_kernel, out_shape=(jax.ShapeDtypeStruct(...  25.8 us
    dot_general x10, matrix products, product_tn(): lax.dot_general(left, right, (((0,), (0,)), ((), ())), preferred_element_...  24.4 us

profile of v2, /device:TPU:0, one launch (start us, length us, event | category | flops | bytes accessed | tf_op | source)
XLA Modules:
  0.0 494.7 jit_solution(14601702404657483458)
XLA Ops:
  3.5 1.4 fusion.93.source_ref
  7.7 2.2 convert_element_type.104.low_ref
  9.9 128.3 %gather_tiles.1 = (bf16[26,512,512]{2,1,0:T(8,128)(2,1)}, s32[4,8,256]{2,1,0:T(8,128)}) custom-call(s32[26]{0:T(128)} %slot_ref.1, bf16[10,64,512]{2,1,0:T(8,128)(2,1)} %convert_element_type.104.low_ref, s32[4,8,256]{2,1,0:T(8,128)} %pad.12.ids_ref), custom_call_target="tpu_custom_call" | custom-call | tf_op jit(solution)/shard_map/gather_tiles/pallas_call | solution.py:472
  139.3 1.5 slice_bitcast_fusion.21
  140.8 1.8 multiply_reduce_fusion.10
  142.6 3.6 convolution_convert_fusion.q_ref.k_ref.v_ref
  146.3 20.3 %attention_forward.2 = (bf16[1024,512]{1,0:T(8,128)(2,1)}, f32[4,2,1024]{2,1,0:T(2,128)}) custom-call(bf16[1024,1536]{1,0:T(8,128)(2,1)} %convolution_convert_fusion.q_ref.k_ref.v_ref, bf16[1024,1536]{1,0:T(8,128)(2,1)} %convolution_convert_fusion.q_ref.k_ref.v_ref, bf16[1024,1536]{1,0:T(8,128)(2,1)} %convolution_convert_fusion.q_ref.k_ref.v_ref), custom_call_target="tpu_custom_call" | custom-call | tf_op jit(solution)/shard_map/attention_forward/pallas_call | solution.py:942
  166.5 2.1 multiply_reduce_fusion.9
  168.7 7.0 %slice_bitcast_fusion.7 = (bf16[512,512]{1,0:T(8,128)(2,1)S(1)}, bf16[512,512]{1,0:T(8,128)(2,1)}, bf16[512,512]{1,0:T(8,128)(2,1)}, bf16[512,512]{1,0:T(8,128)(...) fusion(bf16[26,512,512]{2,1,0:T(8,128)(2,1)} %get-tuple-element.25), kind=kLoop, calls=%fused_computation.118 | loop fusion | bytes 19922944 | tf_op jit(solution)/shard_map/squeeze | solution.py:66
  177.0 2.5 fusion.70
  179.6 3.5 convolution_add_fusion.2
  183.7 1.5 convolution_convert_fusion.1.q_ref.k_ref.v_ref
  185.2 5.5 %attention_forward.3 = (bf16[256,512]{1,0:T(8,128)(2,1)}, f32[4,2,256]{2,1,0:T(2,128)}) custom-call(bf16[256,1536]{1,0:T(8,128)(2,1)} %convolution_convert_fusion.1.q_ref.k_ref.v_ref, bf16[256,1536]{1,0:T(8,128)(2,1)} %convolution_convert_fusion.1.q_ref.k_ref.v_ref, bf16[256,1536]{1,0:T(8,128)(2,1)} %convolution_convert_fusion.1.q_ref.k_ref.v_ref), custom_call_target="tpu_custom_call" | custom-call | tf_op jit(solution)/shard_map/attention_forward/pallas_call | solution.py:942
  190.7 1.5 multiply_reduce_fusion.15
  192.3 3.6 fusion.73
  195.9 4.2 multiply_reduce_fusion.8
  200.1 1.6 fusion.133
  202.0 3.2 multiply_reduce_fusion.7
  207.8 8.2 %column_sum.1 = f32[8,128]{1,0:T(8,128)} custom-call(f32[8,128]{1,0:T(8,128)} %pad.13.value_ref), custom_call_target="tpu_custom_call" | custom-call | tf_op jit(solution)/shard_map/column_sum/pallas_call | solution.py:850
  215.9 1.3 fusion.132
  229.7 4.2 fusion.113
  235.0 1.5 fusion.117
  236.4 1.8 multiply_reduce_fusion.1
  238.3 1.3 copy-done.6
  239.6 1.9 fusion.39
  241.8 5.5 %fusion.13 = bf16[256,2048]{1,0:T(8,128)(2,1)S(1)} fusion(f32[256,2048]{1,0:T(8,128)S(1)} %copy-done.39, bf16[512,512]{1,0:T(8,128)(2,1)S(1)} %copy-done.73, bf16[512,512]{1,0:T(8,128)(2,1)S(1)} %copy-done.74, bf16[512,512]{1,0:T(8,128)(2,1)S(1)} %copy-done.75, bf16[512,512]{1,0:T(8,128)(2,1)S(1)} %copy-done.76, f32[256,512]{1,0:T(8,128)S(1)} %fusion.39), kind=kOutput, calls=%fused_computation.23 | convolution fusion | flops 555876352 | bytes 5767168 | tf_op jit(solution)/shard_map/dot_general | solution.py:37
  248.5 2.1 convolution_convert_fusion.3.up_ref
  250.6 5.2 %attention_backward.2 = (bf16[256,512]{1,0:T(8,128)(2,1)}, bf16[256,512]{1,0:T(8,128)(2,1)}, bf16[256,512]{1,0:T(8,128)(2,1)}) custom-call(bf16[256,1536]{1,0:T(8,128)(2,1)} %convolution_convert_fusion.1.q_ref.k_ref.v_ref, bf16[256,1536]{1,0:T(8,128)(2,1)} %convolution_convert_fusion.1.q_ref.k_ref.v_ref, ...), custom_call_target="tpu_custom_call" | custom-call | tf_op jit(solution)/shard_map/attention_backward/pallas_call | solution.py:964
  258.8 2.1 multiply_reduce_fusion.12
  264.0 2.4 add_add_fusion.3
  267.4 2.2 fusion.124
  270.3 1.7 fusion.128
  272.0 1.7 slice-done.1
  274.2 12.2 %fusion.6 = bf16[1024,2048]{1,0:T(8,128)(2,1)S(1)} fusion(f32[1024,2048]{1,0:T(8,128)S(1)} %bitcast.209, f32[1024,512]{0,1:T(8,128)S(1)} %add_add_fusion.3, bf16[512,512]{1,0:T(8,128)(2,1)S(1)} %copy-done.58, bf16[512,512]{1,0:T(8,128)(2,1)S(1)} %copy-done.60, bf16[512,512]{1,0:T(8,128)(2,1)S(1)} %copy-done.62, bf16[512,512]{1,0:T(8,128)(2,1)S(1)} %copy-done.64), kind=kOutput, calls=%fused_computation.8 | convolution fusion | flops 2198339584 | bytes 16777216 | tf_op jit(solution)/shard_map/dot_general | solution.py:37
  286.3 4.0 fusion.51
  290.4 2.2 fusion.126
  294.0 2.7 multiply_reduce_fusion.2
  296.7 4.4 fusion.121
  301.6 2.8 convolution_convert_fusion.2.up_ref
  304.4 22.4 %attention_backward.3 = (bf16[1024,512]{1,0:T(8,128)(2,1)}, bf16[1024,512]{1,0:T(8,128)(2,1)}, bf16[1024,512]{1,0:T(8,128)(2,1)}) custom-call(bf16[1024,1536]{1,0:T(8,128)(2,1)} %convolution_convert_fusion.q_ref.k_ref.v_ref, bf16[1024,1536]{1,0:T(8,128)(2,1)} %convolution_convert_fusion.q_ref.k_ref.v_ref, ...), custom_call_target="tpu_custom_call" | custom-call | tf_op jit(solution)/shard_map/attention_backward/pallas_call | solution.py:964
  326.8 3.1 fusion.48
  329.9 2.2 fusion.127
  335.4 3.3 multiply_reduce_fusion.3
  338.7 3.5 fusion.120
  342.9 4.3 fusion.16
  378.5 103.2 %reduce_tiles.1 = (f32[10,64,512]{2,1,0:T(8,128)}, f32[8,512]{1,0:T(8,128)}, f32[8,128]{1,0:T(8,128)}) custom-call(s32[10]{0:T(128)} %fusion.93.source_ref, s32[10]{0:T(128)} %convert_element_type.103.valid_ref, f32[26,4,2,2,2,16,512]{6,5,4,3,2,1,0:T(8,128)} %constant_dynamic-update-slice_fusion.6.grads_ref, f32[8,512]{1,0:T(8,128)} %concatenate.46.small_ref), custom_call_target="tpu_custom_call" | custom-call | tf_op jit(solution)/shard_map/reduce_tiles/pallas_call | solution.py:793
  486.9 1.4 multiply_subtract_fusion
  488.3 5.1 %fusion.123 = (bf16[10,64,512]{2,1,0:T(8,128)(2,1)}, f32[10,64,512]{2,1,0:T(8,128)}, f32[10,64,512]{2,1,0:T(8,128)}, f32[10,64,512]{2,1,0:T(8,128)}) fusion(f32[10,64,512]{2,1,0:T(8,128)S(1)} %copy-done.14, f32[]{:T(128)} %bitcast.78, f32[10,64,512]{2,1,0:T(8,128)S(1)} %copy-done.42, f32[]{:T(128)} %bitcast.77, f32[10,64,512]{2,1,0:T(8,128)} %get-tuple-element.38, ...), kind=kLoop, calls=%fused_computation.263 | loop fusion | flops 6553600 | bytes 9830422 | tf_op jit(solution)/shard_map/convert_element_type | solution.py:1209
  (260 shorter events, 62.8 us)
Async XLA Ops:
  3.5 2.8 copy-start.86
  142.6 23.9 %copy-start.4 = (f32[1024,512]{0,1:T(8,128)}, f32[1024,512]{0,1:T(8,128)S(1)}, u32[]{:S(2)}) copy-start(f32[1024,512]{0,1:T(8,128)S(1)} %get-tuple-element.116) | copy-start | bytes 6291460
  168.7 10.9 %copy-start.10 = (f32[1024,512]{0,1:T(8,128)}, f32[1024,512]{0,1:T(8,128)S(1)}, u32[]{:S(2)}) copy-start(f32[1024,512]{0,1:T(8,128)S(1)} %get-tuple-element.118) | copy-start | bytes 6291460
  175.7 3.8 copy-start.57
  175.7 3.8 copy-start.59
  175.7 3.8 copy-start.61
  175.7 3.8 copy-start.63
  175.7 7.9 %copy-start.65 = (bf16[512,512]{1,0:T(8,128)(2,1)}, bf16[512,512]{1,0:T(8,128)(2,1)S(1)}, u32[]{:S(2)}) copy-start(bf16[512,512]{1,0:T(8,128)(2,1)S(1)} %get-tuple-element.66) | copy-start | bytes 1572868
  175.7 7.9 %copy-start.66 = (bf16[512,512]{1,0:T(8,128)(2,1)}, bf16[512,512]{1,0:T(8,128)(2,1)S(1)}, u32[]{:S(2)}) copy-start(bf16[512,512]{1,0:T(8,128)(2,1)S(1)} %get-tuple-element.67) | copy-start | bytes 1572868
  175.8 7.9 %copy-start.67 = (bf16[512,512]{1,0:T(8,128)(2,1)}, bf16[512,512]{1,0:T(8,128)(2,1)S(1)}, u32[]{:S(2)}) copy-start(bf16[512,512]{1,0:T(8,128)(2,1)S(1)} %get-tuple-element.68) | copy-start | bytes 1572868
  175.8 16.5 %copy-start.68 = (bf16[512,512]{1,0:T(8,128)(2,1)}, bf16[512,512]{1,0:T(8,128)(2,1)S(1)}, u32[]{:S(2)}) copy-start(bf16[512,512]{1,0:T(8,128)(2,1)S(1)} %get-tuple-element.58) | copy-start | bytes 1572868
  179.6 3.5 copy-start.88
  183.6 7.1 %copy-start.15 = (f32[256,512]{1,0:T(8,128)}, f32[256,512]{1,0:T(8,128)S(1)}, u32[]{:S(2)}) copy-start(f32[256,512]{1,0:T(8,128)S(1)} %get-tuple-element.120) | copy-start | bytes 1572868
  192.2 3.6 copy-start.12
  229.7 4.2 copy-start.2
  241.8 6.6 %copy-start.17 = (f32[256,512]{1,0:T(8,128)}, f32[256,512]{1,0:T(8,128)S(1)}, u32[]{:S(2)}) copy-start(f32[256,512]{1,0:T(8,128)S(1)} %fusion.39) | copy-start | bytes 1572868
  241.8 5.5 %copy-start.13 = (f32[256,512]{1,0:T(8,128)S(1)}, f32[256,512]{1,0:T(8,128)}, u32[]{:S(2)}) copy-start(f32[256,512]{1,0:T(8,128)} %copy-done.12) | copy-start | bytes 1572868
  241.8 5.5 %copy-start.69 = (bf16[512,512]{1,0:T(8,128)(2,1)S(1)}, bf16[512,512]{1,0:T(8,128)(2,1)}, u32[]{:S(2)}) copy-start(bf16[512,512]{1,0:T(8,128)(2,1)} %copy-done.68) | copy-start | bytes 1572868
  241.8 5.5 %copy-start.70 = (bf16[512,512]{1,0:T(8,128)(2,1)S(1)}, bf16[512,512]{1,0:T(8,128)(2,1)}, u32[]{:S(2)}) copy-start(bf16[512,512]{1,0:T(8,128)(2,1)} %get-tuple-element.63) | copy-start | bytes 1572868
  241.8 5.5 %copy-start.71 = (bf16[512,512]{1,0:T(8,128)(2,1)S(1)}, bf16[512,512]{1,0:T(8,128)(2,1)}, u32[]{:S(2)}) copy-start(bf16[512,512]{1,0:T(8,128)(2,1)} %get-tuple-element.64) | copy-start | bytes 1572868
  241.8 5.5 %copy-start.72 = (bf16[512,512]{1,0:T(8,128)(2,1)S(1)}, bf16[512,512]{1,0:T(8,128)(2,1)}, u32[]{:S(2)}) copy-start(bf16[512,512]{1,0:T(8,128)(2,1)} %get-tuple-element.65) | copy-start | bytes 1572868
  250.6 8.1 %copy-start.16 = (f32[256,512]{1,0:T(8,128)S(1)}, f32[256,512]{1,0:T(8,128)}, u32[]{:S(2)}) copy-start(f32[256,512]{1,0:T(8,128)} %copy-done.15) | copy-start | bytes 1572868
  260.9 2.6 copy-start.7
  264.0 2.4 copy-start.18
  264.0 2.4 copy-start.40
  267.4 4.6 slice-start
  269.6 4.1 slice-start.1
  270.3 3.4 copy-start.58
  270.3 3.6 copy-start.60
  270.3 3.7 copy-start.62
  270.3 3.9 copy-start.64
  290.3 2.8 copy-start.11
  290.3 3.2 copy-start.50
  290.3 3.3 copy-start.52
  290.3 3.5 copy-start.54
  290.4 3.6 copy-start.56
  326.8 3.1 copy-start.20
  342.8 4.3 copy-start.41
  342.8 4.4 copy-start.38
  356.5 2.3 copy-start.33
  357.6 2.3 copy-start.32
  378.4 108.4 %copy-start.83 = (f32[6,512]{1,0:T(8,128)S(1)}, f32[6,512]{1,0:T(8,128)}, u32[]{:S(2)}) copy-start(f32[6,512]{1,0:T(8,128)} %param.21) | copy-start | bytes 36868
  378.4 108.4 %copy-start.84 = (f32[6,512]{1,0:T(8,128)S(1)}, f32[6,512]{1,0:T(8,128)}, u32[]{:S(2)}) copy-start(f32[6,512]{1,0:T(8,128)} %param.23) | copy-start | bytes 36868
  378.4 108.4 %copy-start.85 = (f32[6,512]{1,0:T(8,128)S(1)}, f32[6,512]{1,0:T(8,128)}, u32[]{:S(2)}) copy-start(f32[6,512]{1,0:T(8,128)} %param.22) | copy-start | bytes 36868
  378.4 109.8 %copy-start.14 = (f32[10,64,512]{2,1,0:T(8,128)S(1)}, f32[10,64,512]{2,1,0:T(8,128)}, u32[]{:S(2)}) copy-start(f32[10,64,512]{2,1,0:T(8,128)} %param.18) | copy-start | bytes 3932164
  378.5 109.8 %copy-start.42 = (f32[10,64,512]{2,1,0:T(8,128)S(1)}, f32[10,64,512]{2,1,0:T(8,128)}, u32[]{:S(2)}) copy-start(f32[10,64,512]{2,1,0:T(8,128)} %param.20) | copy-start | bytes 3932164
  378.5 109.8 %copy-start.87 = (pred[10]{0:T(512)(128)(4,1)S(1)}, pred[10]{0:T(512)(128)(4,1)}, u32[]{:S(2)}) copy-start(pred[10]{0:T(512)(128)(4,1)} %copy-done.86) | copy-start | bytes 34
  488.3 5.1 %copy-start.1 = (s32[4,1]{0,1:T(1,128)S(1)}, s32[4,1]{0,1:T(1,128)}, u32[]{:S(2)}) copy-start(s32[4,1]{0,1:T(1,128)} %param.15) | copy-start | bytes 52
  (43 other events, 79.4 us)

commit v3 on v2

--- a/solution.py
+++ b/solution.py
@@ -1,4 +1,5 @@
 import functools
+import math
 
 import jax
 import jax.numpy as jnp
@@ -21,6 +22,7 @@
 PRIOR_RATE = 0.25
 NORM_EPS = 1e-06
 MASKED = -1e30
+LOG_ODDS = math.log(1.0 - PRIOR_RATE) - math.log(PRIOR_RATE)
 
 
 def product(left, right):
@@ -334,6 +336,7 @@
 
 MESH = pl.DeviceIdType.MESH
 VMEM_LIMIT = 60 * 1024 * 1024
+STEP_VMEM = 63 * 1024 * 1024
 
 
 def remote(src, dst, send_sem, recv_sem, peer):
@@ -827,41 +830,6 @@
     )(source, valid, grads.reshape(tile_count, 4, 2, 2, 2, 16, width), small)
 
 
-def column_kernel(value_ref, out_ref, gathered, send, recv):
-    dp, seq, _, _ = places()
-    column = [((dp + j) % 8, seq) for j in range(1, 8)]
-    meet(column)
-    gathered[dp] = value_ref[...]
-    copies = [
-        remote(value_ref, gathered.at[dp], send.at[j], recv.at[j], column[j]) for j in range(7)
-    ]
-    for copy in copies:
-        copy.start()
-    for copy in copies:
-        copy.wait()
-    total = gathered[0]
-    for j in range(1, 8):
-        total = total + gathered[j]
-    out_ref[...] = total
-
-
-def column_sum(value):
-    vmem = pl.BlockSpec(memory_space=pltpu.VMEM)
-    return pl.pallas_call(
-        column_kernel,
-        out_shape=jax.ShapeDtypeStruct(value.shape, value.dtype),
-        in_specs=[vmem],
-        out_specs=vmem,
-        scratch_shapes=[
-            pltpu.VMEM((lax.axis_size("dp"),) + value.shape, value.dtype),
-            pltpu.SemaphoreType.DMA((7,)),
-            pltpu.SemaphoreType.DMA((7,)),
-        ],
-        name="column_sum",
-        compiler_params=pltpu.CompilerParams(collective_id=2, has_side_effects=True),
-    )(value)
-
-
 def head_mask(shape, head):
     lane = lax.broadcasted_iota(jnp.int32, shape, 1)
     return (lane >= 64) if head else (lane < 64)
@@ -876,256 +844,471 @@
     return own if first_row == 0 else jnp.concatenate([scores[:first_row], own], axis=0)
 
 
-def attention_forward_kernel(q_ref, k_ref, v_ref, out_ref, log_ref, turned):
-    length, lanes = q_ref.shape
-    step = 256
-    factor = (lanes // 2) ** (-0.5)
-    turned[...] = v_ref[...].astype(jnp.float32).T.astype(jnp.bfloat16)
-    for first in range(0, length, step):
-        q_pair = q_ref[first : first + step, :] * jnp.asarray(factor, jnp.bfloat16)
-        pieces = []
-        for head in range(2):
-            q_head = jnp.where(head_mask(q_pair.shape, head), q_pair, jnp.zeros_like(q_pair))
-            scores = scores_t(k_ref[: first + step, :], q_head, first)
-            peak = jnp.max(scores, axis=0, keepdims=True)
-            raised = jnp.exp(scores - peak)
-            total = jnp.sum(raised, axis=0, keepdims=True)
-            weights = (raised * (1.0 / total)).astype(jnp.bfloat16)
-            log_ref[0, head : head + 1, first : first + step] = peak + jnp.log(total)
-            pieces.append(product(turned[64 * head : 64 * head + 64, : first + step], weights))
-        out_ref[first : first + step, :] = jnp.concatenate(pieces, axis=0).T.astype(out_ref.dtype)
-
-
-def attention_backward_kernel(q_ref, k_ref, v_ref, up_ref, log_ref, dq_ref, dk_ref, dv_ref, turned, dk_sum, dv_sum):
-    length, lanes = q_ref.shape
-    step = 256
-    factor = (lanes // 2) ** (-0.5)
-    turned[...] = k_ref[...].astype(jnp.float32).T.astype(jnp.bfloat16)
-    for first in reversed(range(0, length, step)):
-        span = first + step
-        q_pair = q_ref[first:span, :] * jnp.asarray(factor, jnp.bfloat16)
-        up_pair = up_ref[first:span, :]
-        queries, keys, values = [], [], []
-        for head in range(2):
-            keep = head_mask(q_pair.shape, head)
-            q_head = jnp.where(keep, q_pair, jnp.zeros_like(q_pair))
-            up_head = jnp.where(keep, up_pair, jnp.zeros_like(up_pair))
-            scores = scores_t(k_ref[:span, :], q_head, first)
-            weights = jnp.exp(scores - log_ref[0, head : head + 1, first:span])
-            grad_weights = product_nt(v_ref[:span, :], up_head)
-            values.append(product(weights.astype(jnp.bfloat16), up_head))
-            inner_sum = jnp.sum(weights * grad_weights, axis=0, keepdims=True)
-            grad_scores = (weights * (grad_weights - inner_sum)).astype(jnp.bfloat16)
-            keys.append(product(grad_scores, q_head))
-            queries.append(product(turned[64 * head : 64 * head + 64, :span], grad_scores))
-        dq_ref[first:span, :] = (jnp.concatenate(queries, axis=0).T * factor).astype(dq_ref.dtype)
-        grad_key = keys[0] + keys[1]
-        grad_value = values[0] + values[1]
-        if span == length:
-            dk_sum[...] = grad_key
-            dv_sum[...] = grad_value
-        else:
-            dk_sum[:span, :] = dk_sum[:span, :] + grad_key
-            dv_sum[:span, :] = dv_sum[:span, :] + grad_value
-    dk_ref[...] = dk_sum[...].astype(dk_ref.dtype)
-    dv_ref[...] = dv_sum[...].astype(dv_ref.dtype)
-
-
-def attention_specs(length, lanes, pairs):
-    return [pl.BlockSpec((length, lanes), lambda p, j=j: (0, j * pairs + p)) for j in range(3)]
-
-
-def attention_whole(qkv_low, model_width, head_width):
-    length = qkv_low.shape[0]
-    lanes = 2 * head_width
-    pairs = model_width // lanes
+ROWS = 256
+
+
+def split_three(value):
+    high = value.astype(jnp.bfloat16)
+    rest = value - high.astype(jnp.float32)
+    middle = rest.astype(jnp.bfloat16)
+    return high, middle, (rest - middle.astype(jnp.float32)).astype(jnp.bfloat16)
+
+
+def exact_product(hot, value):
+    high, middle, low = split_three(value)
+    return (product(hot, low) + product(hot, middle)) + product(hot, high)
+
+
+def turn(value):
+    return value.astype(jnp.float32).T.astype(jnp.bfloat16)
+
+
+def root_scale(value):
+    return lax.rsqrt(jnp.mean(value * value, axis=-1, keepdims=True) + NORM_EPS)
+
+
+def norm_back(value, scale, gain, grad):
+    unit = value * scale
+    weighted = grad * gain
+    inner = jnp.mean(weighted * unit, axis=-1, keepdims=True)
+    return scale * (weighted - unit * inner), jnp.sum(grad * unit, axis=0, keepdims=True)
+
+
+def gelu_both(value):
+    root = 0.7978845608028654
+    square = value * value
+    reach = jnp.tanh(root * value * (1.0 + 0.044715 * square))
+    part = 0.5 * (1.0 + reach)
+    slope = part + value * (0.5 * (1.0 - reach * reach)) * (root * (1.0 + 3.0 * 0.044715 * square))
+    return value * part, slope
+
+
+def digamma(value):
+    moved = value + 8.0
+    inverse = 1.0 / moved
+    square = inverse * inverse
+    series = square * (1.0 / 12.0 - square * (1.0 / 120.0 - square * (1.0 / 252.0)))
+    total = jnp.log(moved) - 0.5 * inverse - series
+    for number in range(8):
+        total = total - 1.0 / (value + float(number))
+    return total
+
+
+def each_block(length, body):
+    def step(number, carry):
+        body(pl.ds(pl.multiple_of(number * ROWS, ROWS), ROWS))
+        return carry
+
+    lax.fori_loop(0, length // ROWS, step, 0)
+
+
+class Block:
+    def __init__(self, length, first_tile, gain_row, entry, qkv, logs, attended, after, inner, leave):
+        self.length, self.tile, self.gain_row = length, first_tile, gain_row
+        self.entry, self.qkv, self.logs, self.attended = entry, qkv, logs, attended
+        self.after, self.inner, self.leave = after, inner, leave
+
+
+def attend(block):
+    length = block.length
+
+    def pair_step(pair, carry):
+        lanes = [pl.ds(pl.multiple_of(part * 512 + pair * 128, 128), 128) for part in range(3)]
+        for first in range(0, length, ROWS):
+            span = first + ROWS
+            q_pair = block.qkv[first:span, lanes[0]] * jnp.asarray(0.125, jnp.bfloat16)
+            outs = []
+            for head in range(2):
+                q_head = jnp.where(head_mask(q_pair.shape, head), q_pair, jnp.zeros_like(q_pair))
+                scores = scores_t(block.qkv[0:span, lanes[1]], q_head, first)
+                peak = jnp.max(scores, axis=0, keepdims=True)
+                raised = jnp.exp(scores - peak)
+                total = jnp.sum(raised, axis=0, keepdims=True)
+                weights = (raised * (1.0 / total)).astype(jnp.bfloat16)
+                block.logs[pair, head : head + 1, first:span] = peak + jnp.log(total)
+                outs.append(product_tn(weights, block.qkv[0:span, lanes[2]]))
+            merged = jnp.where(head_mask(outs[0].shape, 0), outs[0], outs[1])
+            block.attended[first:span, lanes[0]] = merged.astype(jnp.bfloat16)
+        return carry
+
+    lax.fori_loop(0, 4, pair_step, 0)
+
+
+def attend_back(block, upstream, grad_qkv, key_sum, value_sum):
+    length = block.length
+
+    def pair_step(pair, carry):
+        lanes = [pl.ds(pl.multiple_of(part * 512 + pair * 128, 128), 128) for part in range(3)]
+        for first in reversed(range(0, length, ROWS)):
+            span = first + ROWS
+            q_pair = block.qkv[first:span, lanes[0]] * jnp.asarray(0.125, jnp.bfloat16)
+            up_pair = upstream[first:span, lanes[0]]
+            queries, keys, values = [], [], []
+            for head in range(2):
+                keep = head_mask(q_pair.shape, head)
+                q_head = jnp.where(keep, q_pair, jnp.zeros_like(q_pair))
+                up_head = jnp.where(keep, up_pair, jnp.zeros_like(up_pair))
+                k_pair = block.qkv[0:span, lanes[1]]
+                scores = scores_t(k_pair, q_head, first)
+                weights = jnp.exp(scores - block.logs[pair, head : head + 1, first:span])
+                grad_weights = product_nt(block.qkv[0:span, lanes[2]], up_head)
+                values.append(product(weights.astype(jnp.bfloat16), up_head))
+                inner_sum = jnp.sum(weights * grad_weights, axis=0, keepdims=True)
+                grad_scores = (weights * (grad_weights - inner_sum)).astype(jnp.bfloat16)
+                keys.append(product(grad_scores, q_head))
+                queries.append(product_tn(grad_scores, k_pair))
+            merged = jnp.where(head_mask(queries[0].shape, 0), queries[0], queries[1]) * 0.125
+            grad_qkv[first:span, lanes[0]] = merged.astype(jnp.bfloat16)
+            if span == length:
+                key_sum[0:span, :] = keys[0] + keys[1]
+                value_sum[0:span, :] = values[0] + values[1]
+            else:
+                key_sum[0:span, :] = key_sum[0:span, :] + (keys[0] + keys[1])
+                value_sum[0:span, :] = value_sum[0:span, :] + (values[0] + values[1])
+        grad_qkv[0:length, lanes[1]] = key_sum[0:length, :].astype(jnp.bfloat16)
+        grad_qkv[0:length, lanes[2]] = value_sum[0:length, :].astype(jnp.bfloat16)
+        return carry
+
+    lax.fori_loop(0, 4, pair_step, 0)
+
+
+def block_run(block, weights, gains):
+    tile = block.tile
+    gain_attn = gains[block.gain_row : block.gain_row + 1, :]
+    gain_ffn = gains[block.gain_row + 1 : block.gain_row + 2, :]
+
+    def project(rows):
+        value = block.entry[rows, :]
+        normed = (value * root_scale(value) * gain_attn).astype(jnp.bfloat16)
+        for part in range(3):
+            block.qkv[rows, 512 * part : 512 * part + 512] = product(normed, weights[tile + part]).astype(
+                jnp.bfloat16
+            )
+
+    each_block(block.length, project)
+    attend(block)
+
+    def feed(rows):
+        after = block.entry[rows, :] + product(block.attended[rows, :], weights[tile + 3])
+        block.after[rows, :] = after
+        normed = (after * root_scale(after) * gain_ffn).astype(jnp.bfloat16)
+        total = jnp.zeros_like(after)
+        for part in range(4):
+            inner = product(normed, weights[tile + 4 + part])
+            block.inner[rows, 512 * part : 512 * part + 512] = inner
+            active = gelu_both(inner)[0].astype(jnp.bfloat16)
+            total = total + product(active, weights[tile + 8 + part])
+        block.leave[rows, :] = after + total
+
+    each_block(block.length, feed)
+
+
+def block_back(block, grad, weights, gains, gain_sums, temps, put):
+    length, tile = block.length, block.tile
+    gain_attn = gains[block.gain_row : block.gain_row + 1, :]
+    gain_ffn = gains[block.gain_row + 1 : block.gain_row + 2, :]
+    turned, grad_inner, branch, upstream, turned_norm, key_sum, value_sum = temps
+    grad_low, grad_qkv = branch, grad_inner
+    all_rows = pl.ds(0, length)
+
+    def down(part):
+        def rows_step(rows):
+            low = grad[rows, :].astype(jnp.bfloat16)
+            columns = pl.ds(pl.multiple_of(part * 512, 512), 512)
+            active, slope = gelu_both(block.inner[rows, columns])
+            turned[:, rows] = turn(active)
+            grad_inner[rows, columns] = (product_nt(low, weights[tile + 8 + part]) * slope).astype(jnp.bfloat16)
+
+        each_block(length, rows_step)
+
+    def low_step(rows):
+        grad_low[rows, :] = grad[rows, :].astype(jnp.bfloat16)
+
+    each_block(length, low_step)
+
+    def down_step(part, carry):
+        down(part)
+        put(tile + 8 + part, part, lambda half: product(turned[half, all_rows], grad_low[all_rows, :]))
+        return carry
+
+    lax.fori_loop(0, 4, down_step, 0)
+
+    def middle(rows):
+        after = block.after[rows, :]
+        scale = root_scale(after)
+        turned_norm[:, rows] = turn(after * scale * gain_ffn)
+        turned[:, rows] = turn(block.attended[rows, :])
+        total = jnp.zeros_like(after)
+        for part in range(4):
+            total = total + product_nt(
+                grad_inner[rows, 512 * part : 512 * part + 512], weights[tile + 4 + part]
+            )
+        back, gain_part = norm_back(after, scale, gain_ffn, total)
+        row = block.gain_row + 1
+        gain_sums[row : row + 1, :] = gain_sums[row : row + 1, :] + gain_part
+        grad_after = grad[rows, :] + back
+        grad[rows, :] = grad_after
+        low = grad_after.astype(jnp.bfloat16)
+        branch[rows, :] = low
+        upstream[rows, :] = product_nt(low, weights[tile + 3]).astype(jnp.bfloat16)
+
+    each_block(length, middle)
+
+    def up_step(part, carry):
+        columns = pl.ds(pl.multiple_of(part * 512, 512), 512)
+        put(tile + 4 + part, part, lambda half: product(turned_norm[half, all_rows], grad_inner[all_rows, columns]))
+        return carry
+
+    lax.fori_loop(0, 4, up_step, 0)
+    put(tile + 3, 0, lambda half: product(turned[half, all_rows], branch[all_rows, :]))
+    attend_back(block, upstream, grad_qkv, key_sum, value_sum)
+
+    def enter(rows):
+        value = block.entry[rows, :]
+        scale = root_scale(value)
+        turned_norm[:, rows] = turn(value * scale * gain_attn)
+        total = jnp.zeros_like(value)
+        for part in range(3):
+            total = total + product_nt(grad_qkv[rows, 512 * part : 512 * part + 512], weights[tile + part])
+        back, gain_part = norm_back(value, scale, gain_attn, total)
+        row = block.gain_row
+        gain_sums[row : row + 1, :] = gain_sums[row : row + 1, :] + gain_part
+        grad[rows, :] = grad[rows, :] + back
+
+    each_block(length, enter)
+
+    def qkv_step(part, carry):
+        columns = pl.ds(pl.multiple_of(part * 512, 512), 512)
+        put(tile + part, part, lambda half: product(turned_norm[half, all_rows], grad_qkv[all_rows, columns]))
+        return carry
+
+    lax.fori_loop(0, 3, qkv_step, 0)
+
+
+def step_kernel(
+    micro_count, length_ref, tiles_ref, ids_ref, gains_ref, grads_ref, small_ref,
+    weights, load_sem, entry, qkv, logs, attended, after, inner, leave, grad,
+    seg_entry, seg_qkv, seg_logs, seg_attended, seg_after, seg_inner, seg_leave, seg_grad,
+    turned, grad_inner, branch, upstream, turned_norm, key_sum, value_sum,
+    ids_col, stage, stage_sem, counts, count_send, count_recv,
+):
+    dp, seq, _, _ = places()
+    length = entry.shape[0]
+    width = entry.shape[1]
+    segments = seg_entry.shape[0]
+    vocab = width // 2
+    root_width = width ** (-0.5)
+    column = [((dp + j) % 8, seq) for j in range(1, 8)]
+    meet(column)
+
+    def load(tile):
+        return pltpu.make_async_copy(tiles_ref.at[tile], weights.at[tile], load_sem.at[tile])
+
+    order = [25] + list(range(12)) + [24] + list(range(12, 24))
+    for tile in order:
+        load(tile).start()
+
+    def ready(tiles):
+        for tile in tiles:
+            load(tile).wait()
+
+    def count_copy(j):
+        return remote(counts.at[dp], counts.at[dp], count_send.at[j], count_recv.at[j], column[j])
+
+    def staged(tile, slot):
+        return pltpu.make_async_copy(stage.at[slot], grads_ref.at[tile], stage_sem.at[slot])
+
+    def put(tile, slot, half_of):
+        staged(tile, slot).wait()
+        for half in range(2):
+            stage[slot, 256 * half : 256 * half + 256, :] = half_of(pl.ds(256 * half, 256))
+        staged(tile, slot).start()
+
+    small_ref[...] = jnp.zeros_like(small_ref)
+    ids_col[...] = ids_ref[...].astype(jnp.float32).T
+    length_one = length_ref[0]
+    char = Block(length, 0, 0, entry, qkv, logs, attended, after, inner, leave)
+    seg = Block(
+        segments, 12, 2, seg_entry, seg_qkv, seg_logs, seg_attended, seg_after, seg_inner, seg_leave
+    )
+    temps = (turned, grad_inner, branch, upstream, turned_norm, key_sum, value_sum)
+
+    def hot_rows(rows, which, offset, count):
+        ids = ids_col[rows, which : which + 1] + float(offset)
+        lane = lax.broadcasted_iota(jnp.int32, (ROWS, count), 1).astype(jnp.float32)
+        return (ids == lane).astype(jnp.bfloat16)
+
+    def hot_turned(which, offset, count):
+        ids = ids_ref[which : which + 1, :] + offset
+        line = lax.broadcasted_iota(jnp.int32, (count, length), 0)
+        return (ids == line).astype(jnp.float32)
+
+    ready([25])
+
+    def embed(rows):
+        entry[rows, :] = product(hot_rows(rows, 0, 0, vocab), weights[25, 0:vocab, :])
+
+    each_block(length, embed)
+    ready(range(12))
+    block_run(char, weights, gains_ref)
+    ready([24])
+
+    def valid_rows(rows):
+        line = lax.broadcasted_iota(jnp.int32, (ROWS, 1), 0) + rows.start
+        return (line < length_one).astype(jnp.float32)
+
+    def boundary(rows):
+        low = leave[rows, :].astype(jnp.bfloat16)
+        reach = jnp.tanh(product(low, weights[24]))
+        logit = jnp.sum(reach * gains_ref[5:6, :], axis=1, keepdims=True) * root_width
+        return low, reach, 1.0 / (1.0 + jnp.exp(-logit))
+
+    def soft_step(number, total):
+        rows = pl.ds(pl.multiple_of(number * ROWS, ROWS), ROWS)
+        return total + jnp.sum(valid_rows(rows) * boundary(rows)[2], axis=0, keepdims=True)
+
+    soft_local = lax.fori_loop(0, length // ROWS, soft_step, jnp.zeros((1, 1), jnp.float32))
+    line = lax.broadcasted_iota(jnp.int32, (8, 128), 0)
+    length_float = length_one.astype(jnp.float32)
+    counts[dp] = jnp.where(line == 0, soft_local, jnp.where(line == 1, length_float, 0.0))
+    for j in range(7):
+        count_copy(j).start()
+
+    pool = hot_turned(2, 1, segments)
+    amounts = jnp.sum(pool, axis=1, keepdims=True)
+    divisor = jnp.maximum(amounts, 1.0)
+    seg_entry[...] = product(pool.astype(jnp.bfloat16), leave[...].astype(jnp.bfloat16)) / divisor
+    ready(range(12, 24))
+    block_run(seg, weights, gains_ref)
+
+    for j in range(7):
+        count_copy(j).wait_recv()
+    total = counts[0]
+    for j in range(1, 8):
+        total = total + counts[j]
+    soft_count, count_all = total[0:1, 0:1], total[1:2, 0:1]
+
+    def head(number, carry):
+        ce, head_sum = carry
+        rows = pl.ds(pl.multiple_of(number * ROWS, ROWS), ROWS)
+        lift = hot_rows(rows, 2, 0, segments)
+        merged = leave[rows, :] + product(lift, seg_leave[...].astype(jnp.bfloat16))
+        scale = root_scale(merged)
+        gain = gains_ref[4:5, :]
+        final_low = (merged * scale * gain).astype(jnp.bfloat16)
+        table = weights[25, vocab : 2 * vocab, :]
+        logits = product_nt(final_low, table)
+        peak = jnp.max(logits, axis=1, keepdims=True)
+        log_total = peak + jnp.log(jnp.sum(jnp.exp(logits - peak), axis=1, keepdims=True))
+        target = hot_rows(rows, 1, 0, vocab).astype(jnp.float32)
+        picked = jnp.sum(logits * target, axis=1, keepdims=True)
+        valid = valid_rows(rows)
+        ce = ce + jnp.sum(valid * (log_total - picked), axis=0, keepdims=True)
+        share = valid / (micro_count * count_all)
+        grad_logits = (jnp.exp(logits - log_total) - target) * share
+        head_sum = head_sum + product(turn(grad_logits), final_low)
+        back, gain_part = norm_back(merged, scale, gain, product(grad_logits.astype(jnp.bfloat16), table))
+        small_ref[4:5, :] = small_ref[4:5, :] + gain_part
+        grad[rows, :] = back
+        return ce, head_sum
+
+    ce_local, head_sum = lax.fori_loop(
+        0, length // ROWS, head, (jnp.zeros((1, 1), jnp.float32), jnp.zeros((vocab, width), jnp.float32))
+    )
+    stage[...] = jnp.zeros_like(stage)
+    for slot in range(4):
+        staged(slot, slot).start()
+    seg_grad[...] = exact_product(hot_turned(2, 0, segments).astype(jnp.bfloat16), grad[...])
+    block_back(seg, seg_grad, weights, gains_ref, small_ref, temps, put)
+    seg_grad[...] = seg_grad[...] / divisor
+
+    count_rest = count_all - soft_count
+    slope = (digamma(soft_count + 1.0) - digamma(count_rest + 1.0) + LOG_ODDS) / (count_all * micro_count)
+
+    def join(rows):
+        low, reach, chance = boundary(rows)
+        logit = valid_rows(rows) * slope * chance * (1.0 - chance)
+        gain = gains_ref[5:6, :]
+        small_ref[5:6, :] = small_ref[5:6, :] + jnp.sum(logit * reach, axis=0, keepdims=True) * root_width
+        pre = (logit * gain * root_width * (1.0 - reach * reach)).astype(jnp.bfloat16)
+        branch[rows, :] = pre
+        turned[:, rows] = turn(low)
+        spread = exact_product(hot_rows(rows, 2, 1, segments), seg_grad[...])
+        grad[rows, :] = (grad[rows, :] + spread) + product_nt(pre, weights[24])
+
+    each_block(length, join)
+    put(24, 0, lambda half: product(turned[half, :], branch[...]))
+    block_back(char, grad, weights, gains_ref, small_ref, temps, put)
+    staged(25, 3).wait()
+    stage[3, 0:vocab, :] = exact_product(hot_turned(0, 0, vocab).astype(jnp.bfloat16), grad[...])
+    stage[3, vocab : 2 * vocab, :] = head_sum
+    staged(25, 3).start()
+
+    lane = lax.broadcasted_iota(jnp.int32, (1, width), 1)
+    small_ref[6:7, :] = jnp.where(
+        lane == seq,
+        ce_local,
+        jnp.where(lane == seq + 8, soft_local, jnp.where(lane == seq + 16, length_float, 0.0)),
+    )
+    for slot in range(4):
+        staged(slot, slot).wait()
+    for j in range(7):
+        count_copy(j).wait_send()
+
+
+def step_call(length_one, tiles, ids, gains, micro_count):
+    tile_count, width, _ = tiles.shape
+    length = ids.shape[1]
+    segments = SEG_DEV * lax.axis_size("seq")
+    dma = pltpu.SemaphoreType.DMA
+    vmem = pl.BlockSpec(memory_space=pltpu.VMEM)
+    hbm = pl.BlockSpec(memory_space=pl.ANY)
+
+    def full(*shape):
+        return pltpu.VMEM(shape, jnp.float32)
+
+    def half(*shape):
+        return pltpu.VMEM(shape, jnp.bfloat16)
+
+    def kept(count):
+        return [
+            full(count, width), half(count, 3 * width), full(4, 2, count), half(count, width),
+            full(count, width), full(count, 4 * width), full(count, width), full(count, width),
+        ]
+
     return pl.pallas_call(
-        attention_forward_kernel,
+        functools.partial(step_kernel, micro_count),
         out_shape=(
-            jax.ShapeDtypeStruct((length, model_width), jnp.bfloat16),
-            jax.ShapeDtypeStruct((pairs, 2, length), jnp.float32),
+            jax.ShapeDtypeStruct((tile_count, width, width), jnp.float32),
+            jax.ShapeDtypeStruct((8, width), jnp.float32),
         ),
-        grid=(pairs,),
-        in_specs=attention_specs(length, lanes, pairs),
-        out_specs=(
-            pl.BlockSpec((length, lanes), lambda p: (0, p)),
-            pl.BlockSpec((1, 2, length), lambda p: (p, 0, 0)),
+        in_specs=[pl.BlockSpec(memory_space=pltpu.SMEM), hbm, vmem, vmem],
+        out_specs=(hbm, vmem),
+        scratch_shapes=[half(tile_count, width, width), dma((tile_count,))]
+        + kept(length)
+        + kept(segments)
+        + [
+            half(width, length), half(length, 4 * width), half(length, width), half(length, width),
+            half(width, length), full(length, 128),
+            full(length, 128), full(length, 8), full(4, width, width), dma((4,)),
+            full(lax.axis_size("dp"), 8, 128), dma((7,)), dma((7,)),
+        ],
+        name="step",
+        compiler_params=pltpu.CompilerParams(
+            collective_id=2, has_side_effects=True, vmem_limit_bytes=STEP_VMEM
         ),
-        scratch_shapes=[pltpu.VMEM((lanes, length), jnp.bfloat16)],
-        name="attention_forward",
-        compiler_params=pltpu.CompilerParams(vmem_limit_bytes=VMEM_LIMIT),
-    )(qkv_low, qkv_low, qkv_low)
-
-
-def attention_whole_back(qkv_low, grad_attended, log_totals, model_width, head_width):
-    length = qkv_low.shape[0]
-    lanes = 2 * head_width
-    pairs = model_width // lanes
-    grads = pl.pallas_call(
-        attention_backward_kernel,
-        out_shape=tuple(jax.ShapeDtypeStruct((length, model_width), jnp.bfloat16) for _ in range(3)),
-        grid=(pairs,),
-        in_specs=attention_specs(length, lanes, pairs)
-        + [
-            pl.BlockSpec((length, lanes), lambda p: (0, p)),
-            pl.BlockSpec((1, 2, length), lambda p: (p, 0, 0)),
-        ],
-        out_specs=tuple(pl.BlockSpec((length, lanes), lambda p: (0, p)) for _ in range(3)),
-        scratch_shapes=[
-            pltpu.VMEM((lanes, length), jnp.bfloat16),
-            pltpu.VMEM((length, lanes), jnp.float32),
-            pltpu.VMEM((length, lanes), jnp.float32),
-        ],
-        name="attention_backward",
-        compiler_params=pltpu.CompilerParams(vmem_limit_bytes=VMEM_LIMIT),
-    )(qkv_low, qkv_low, qkv_low, grad_attended, log_totals)
-    return jnp.concatenate(grads, axis=1)
-
-
-def whole_forward(hidden_in, tiles, gain_attn, gain_ffn):
-    model_width = hidden_in.shape[1]
-    head_width = model_width // HEADS
-    w_qkv, w_up, w_down = block_weights(tiles)
-    normed = rms_norm(hidden_in, gain_attn).astype(jnp.bfloat16)
-    qkv_low = product(normed, w_qkv).astype(jnp.bfloat16)
-    attended, log_totals = attention_whole(qkv_low, model_width, head_width)
-    after_attn = hidden_in + product(attended, tiles[3])
-    inner = product(rms_norm(after_attn, gain_ffn).astype(jnp.bfloat16), w_up)
-    block_out = after_attn + product(jax.nn.gelu(inner).astype(jnp.bfloat16), w_down)
-    return (block_out, (hidden_in, qkv_low, log_totals, attended, after_attn, inner))
-
-
-def whole_backward(grad_out, saved, tiles, gain_attn, gain_ffn):
-    hidden_in, qkv_low, log_totals, attended, after_attn, inner = saved
-    model_width = hidden_in.shape[1]
-    head_width = model_width // HEADS
-    w_qkv, w_up, w_down = block_weights(tiles)
-    grad_ffn = grad_out.astype(jnp.bfloat16)
-    activated, gelu_pull = jax.vjp(jax.nn.gelu, inner)
-    grad_down = product_tn(activated.astype(jnp.bfloat16), grad_ffn)
-    grad_inner = gelu_pull(product_nt(grad_ffn, w_down))[0].astype(jnp.bfloat16)
-    normed_ffn, ffn_pull = jax.vjp(rms_norm, after_attn, gain_ffn)
-    grad_up = product_tn(normed_ffn.astype(jnp.bfloat16), grad_inner)
-    grad_normed_in, grad_gain_ffn = ffn_pull(product_nt(grad_inner, w_up))
-    grad_after = grad_out + grad_normed_in
-    grad_branch = grad_after.astype(jnp.bfloat16)
-    grad_wout = product_tn(attended, grad_branch)
-    grad_attended = product_nt(grad_branch, tiles[3]).astype(jnp.bfloat16)
-    grad_qkv = attention_whole_back(qkv_low, grad_attended, log_totals, model_width, head_width)
-    normed_attn, attn_pull = jax.vjp(rms_norm, hidden_in, gain_attn)
-    grad_wqkv = product_tn(normed_attn.astype(jnp.bfloat16), grad_qkv)
-    grad_normed_x, grad_gain_attn = attn_pull(product_nt(grad_qkv, w_qkv))
-    grad_in = grad_after + grad_normed_x
-    pieces = [grad_wqkv[:, i * model_width : (i + 1) * model_width] for i in range(3)]
-    pieces = pieces + [grad_wout]
-    pieces = pieces + [grad_up[:, i * model_width : (i + 1) * model_width] for i in range(4)]
-    pieces = pieces + [grad_down[i * model_width : (i + 1) * model_width] for i in range(4)]
-    return (grad_in, pieces, grad_gain_attn, grad_gain_ffn)
+    )(length_one, tiles, ids, gains)
 
 
 def whole_step(char_ids, targets, seg_ids, lengths, owner_slot, master, gain_rows):
     micro_count = char_ids.shape[0]
-    seq_count = lax.axis_size("seq")
-    seq_me = lax.axis_index("seq")
-    model_width = master.shape[2]
-    vocab_size = model_width // 2
-    seg_total = SEG_DEV * seq_count
     ids = jnp.stack([char_ids[:, 0], targets[:, 0], seg_ids[:, 0]], axis=1)
     ids = jnp.pad(ids, ((0, 0), (0, 5), (0, 0)))
     tiles, ids = gather_tiles_kernel(master.astype(jnp.bfloat16), ids, owner_slot)
-    chars_row, target_row, segment_row = (ids[:, i].reshape(-1) for i in range(3))
-    length_one = lax.dynamic_index_in_dim(lengths[:, 0], seq_me, keepdims=False)
-    char_count = chars_row.shape[0]
-    is_valid = (jnp.arange(char_count) < length_one).astype(jnp.float32)
-    vocab_iota = jnp.arange(vocab_size)
-    char_hot = chars_row[:, None] == vocab_iota[None, :]
-    embed_low = tiles[25, :vocab_size]
-    head_low = tiles[25, vocab_size:]
-    start_hidden = product(char_hot.astype(jnp.bfloat16), embed_low)
-    char_out, char_saved = whole_forward(start_hidden, tiles[0:12], gain_rows[0], gain_rows[1])
-    char_low = char_out.astype(jnp.bfloat16)
-    boundary_hidden = jnp.tanh(product(char_low, tiles[24]))
-    root_width = model_width ** (-0.5)
-    boundary_prob = jax.nn.sigmoid(jnp.sum(boundary_hidden * gain_rows[5], axis=1) * root_width)
-    counts = jnp.stack([jnp.sum(is_valid * boundary_prob), length_one.astype(jnp.float32)])
-    counts = column_sum(jnp.pad(counts[:, None], ((0, 6), (0, 127))))
-    soft_count, count_all = counts[0, 0], counts[1, 0]
-    slot_iota = jnp.arange(seg_total)
-    pool_hot = segment_row[None, :] + 1 == slot_iota[:, None]
-    lift_hot = segment_row[:, None] == slot_iota[None, :]
-    row_counts = jnp.sum(pool_hot.astype(jnp.float32), axis=1)
-    divisor = jnp.maximum(row_counts, 1.0)[:, None]
-    pooled = product(pool_hot.astype(jnp.bfloat16), char_low) / divisor
-    seg_out, seg_saved = whole_forward(pooled, tiles[12:24], gain_rows[2], gain_rows[3])
-    merged = char_out + product(lift_hot.astype(jnp.bfloat16), seg_out.astype(jnp.bfloat16))
-    final_norm, final_pull = jax.vjp(rms_norm, merged, gain_rows[4])
-    final_low = final_norm.astype(jnp.bfloat16)
-    logits = product_nt(final_low, head_low)
-    peak = jnp.max(logits, axis=1, keepdims=True)
-    log_total = peak[:, 0] + jnp.log(jnp.sum(jnp.exp(logits - peak), axis=1))
-    target_hot = (target_row[:, None] == vocab_iota[None, :]).astype(jnp.float32)
-    picked = jnp.sum(logits * target_hot, axis=1)
-    ce_local = jnp.sum(is_valid * (log_total - picked))
-    weight_ce = is_valid / (micro_count * count_all)
-    grad_logits = ((jnp.exp(logits - log_total[:, None]) - target_hot) * weight_ce[:, None]).astype(
-        jnp.bfloat16
-    )
-    grad_head = product_tn(grad_logits, final_low)
-    grad_merged, grad_gain_final = final_pull(product(grad_logits, head_low))
-    grad_seg = exact_tn(lift_hot.astype(jnp.float32), grad_merged)
-    grad_pooled, seg_pieces, grad_gain_two, grad_gain_three = whole_backward(
-        grad_seg, seg_saved, tiles[12:24], gain_rows[2], gain_rows[3]
-    )
-    grad_char = grad_merged + exact_tn(pool_hot.astype(jnp.float32), grad_pooled / divisor)
-    prior_slope = (
-        lax.digamma(soft_count + 1.0)
-        - lax.digamma(count_all - soft_count + 1.0)
-        - jnp.log(PRIOR_RATE)
-        + jnp.log(1.0 - PRIOR_RATE)
-    ) / (count_all * micro_count)
-    grad_boundary_logit = is_valid * prior_slope * boundary_prob * (1.0 - boundary_prob)
-    grad_gain_boundary = (
-        jnp.sum(grad_boundary_logit[:, None] * boundary_hidden, axis=0) * root_width
-    )
-    grad_pre = (
-        grad_boundary_logit[:, None]
-        * gain_rows[5][None, :]
-        * root_width
-        * (1.0 - boundary_hidden * boundary_hidden)
-    ).astype(jnp.bfloat16)
-    grad_boundary = product_tn(char_low, grad_pre)
-    grad_char = grad_char + product_nt(grad_pre, tiles[24])
-    grad_start, char_pieces, grad_gain_zero, grad_gain_one = whole_backward(
-        grad_char, char_saved, tiles[0:12], gain_rows[0], gain_rows[1]
-    )
-    grad_embed = exact_tn(char_hot.astype(jnp.float32), grad_start)
-    tile_grads = jnp.stack(
-        char_pieces
-        + seg_pieces
-        + [grad_boundary, jnp.concatenate([grad_embed, grad_head], axis=0)]
-    )
-    gain_grads = jnp.stack(
-        [
-            grad_gain_zero,
-            grad_gain_one,
-            grad_gain_two,
-            grad_gain_three,
-            grad_gain_final,
-            grad_gain_boundary,
-        ]
-    )
-    prior_term = (
-        -(
-            lax.lgamma(count_all + 1.0)
-            - lax.lgamma(soft_count + 1.0)
-            - lax.lgamma(count_all - soft_count + 1.0)
-            + soft_count * jnp.log(PRIOR_RATE)
-            + (count_all - soft_count) * jnp.log(1.0 - PRIOR_RATE)
-        )
-        / count_all
-    )
-    loss_part = (ce_local / count_all + prior_term / lax.axis_size("dp")) / micro_count
-    return (tile_grads, gain_grads, loss_part)
+    ids = ids.transpose(1, 0, 2).reshape(8, -1)
+    length_one = lax.dynamic_slice_in_dim(lengths[:, 0], lax.axis_index("seq"), 1)
+    gains = jnp.pad(gain_rows, ((0, 2), (0, 0)))
+    return step_call(length_one, tiles, ids, gains, micro_count)
 
 
 def body(
@@ -1146,20 +1329,26 @@
     model_width = master.shape[2]
     slot_count = master.shape[0] * lax.axis_size("seq")
     if (micro_count, lax.axis_size("seq"), lax.axis_size("dp")) == (4, 4, 8):
-        tile_grads, gain_part, loss_part = whole_step(
+        tile_grads, small = whole_step(
             char_ids, targets, seg_ids, lengths, owner_slot, master, gain_rows
         )
         local = lax.axis_index("seq") * master.shape[0] + jnp.arange(master.shape[0])
         hot = local[:, None] == owner_slot[None, :]
         valid = jnp.any(hot, axis=1).astype(jnp.int32)
         source = jnp.sum(jnp.where(hot, jnp.arange(owner_slot.shape[0])[None, :], 0), axis=1)
-        small = jnp.concatenate(
-            [gain_part, jnp.pad(loss_part.reshape(1, 1), ((0, 1), (0, model_width - 1)))]
-        )
         shard_total, small, squares = reduce_tiles_kernel(
             tile_grads, small, source, valid, master.shape[0]
         )
-        gain_sum, loss_total, square_sum = small[0:6], small[6, 0], jnp.sum(squares)
+        gain_sum, square_sum = small[0:6], jnp.sum(squares)
+        entropy, soft, count = (small[6, 8 * i : 8 * i + micro_count] for i in range(3))
+        prior = -(
+            lax.lgamma(count + 1.0)
+            - lax.lgamma(soft + 1.0)
+            - lax.lgamma(count - soft + 1.0)
+            + soft * jnp.log(PRIOR_RATE)
+            + (count - soft) * jnp.log(1.0 - PRIOR_RATE)
+        )
+        loss_total = jnp.sum((entropy + prior) / count) / micro_count
     else:
         tile_total = jnp.zeros((owner_slot.shape[0], model_width, model_width), jnp.float32)
         gain_total = jnp.zeros_like(gain_rows)

time: 503 us -> 363 us (0.72); the launches traced: 495 us -> 362 us
  matrix products: 97.2 us -> 0 us
  local copies, waits for them, and re-layouts: 67.2 us -> 2.46 us
  Pallas kernels: 293 us -> 339 us
  between operations: 17 us -> 5.79 us
  other arithmetic: 20.2 us -> 14.7 us
    dot_general x35 -> x0, matrix products: 97.2 us -> none  [the longest x10 35.5 us: product_nt(): lax.dot_general(left, right, (((1,), (1,)), ((), ())), preferred_element_...]
    pallas_call x5 -> x1, Pallas kernels: 61.6 us -> 110 us  [step_call(): pl.pallas_call(functools.partial(step_kernel, micro_count), out_shape=(ja...]
    unnamed x211 -> x18, local copies, waits for them, and re-layouts: 40.6 us -> 0.65 us
    slice x10 -> x0, local copies, waits for them, and re-layouts: 13.5 us -> none  [the longest x2 4.41 us: whole_backward(): grad_down[i * model_width:(i + 1) * model_width]]
    squeeze x2 -> x0, local copies, waits for them, and re-layouts: 8.43 us -> none  [the longest x1 6.96 us: block_weights(): w_up = jnp.concatenate([tiles[4], tiles[5], tiles[6], tiles[7]], axis=1)]
where the time goes in v3:
time: 363 us; the launch traced here: 362 us
  Pallas kernels  339 us (93%)
  other arithmetic  14.7 us (4%)
  between operations  5.79 us (2%)
    pallas_call x1, Pallas kernels, gather_tiles_kernel(): pl.pallas_call(functools.partial(gather_kernel, chunks), out_shape=(jax.S...  128 us
    pallas_call x1, Pallas kernels, step_call(): pl.pallas_call(functools.partial(step_kernel, micro_count), out_shape=(ja...  110 us
    pallas_call x1, Pallas kernels, reduce_tiles_kernel(): pl.pallas_call(reduce_kernel, out_shape=(jax.ShapeDtypeStruct((held, rows...  101 us

profile of v3, /device:TPU:0, one launch (start us, length us, event | category | flops | bytes accessed | tf_op | source)
XLA Modules:
  0.0 362.0 jit_solution(5036486070182024271)
XLA Ops:
  0.6 0.0 copy-start
  0.7 0.0 copy-start.7
  0.7 0.0 copy-start.6
  0.7 0.0 copy-start.5
  0.7 0.6 copy-done
  1.3 0.6 constant_dynamic-slice_fusion
  1.9 0.0 copy-start.2
  1.9 2.3 convert_element_type.16.low_ref
  4.1 0.0 copy-done.7
  4.1 0.0 copy-done.6
  4.1 0.0 copy-done.5
  4.2 0.6 pad.8.ids_ref
  4.8 128.3 %gather_tiles.1 = (bf16[26,512,512]{2,1,0:T(8,128)(2,1)}, s32[4,8,256]{2,1,0:T(8,128)}) custom-call(s32[26]{0:T(128)} %slot_ref.1, bf16[10,64,512]{2,1,0:T(8,128)(2,1)} %convert_element_type.16.low_ref, s32[4,8,256]{2,1,0:T(8,128)} %pad.8.ids_ref), custom_call_target="tpu_custom_call" | custom-call | tf_op jit(solution)/shard_map/gather_tiles/pallas_call | solution.py:475
  133.1 0.0 copy-done.2
  133.1 0.6 pad.9.gains_ref
  133.7 0.0 copy-start.8
  133.7 109.7 %step.1 = (f32[26,512,512]{2,1,0:T(8,128)}, f32[8,512]{1,0:T(8,128)}) custom-call(s32[1]{0:T(128)} %bitcast.length_ref, bf16[26,512,512]{2,1,0:T(8,128)(2,1)} %get-tuple-element.16.tiles_ref, s32[8,1024]{1,0:T(8,128)} %bitcast.66, f32[8,512]{1,0:T(8,128)} %pad.9.gains_ref), custom_call_target="tpu_custom_call" | custom-call | tf_op jit(solution)/shard_map/step/pallas_call | solution.py:1279
  243.4 0.0 copy-done.8
  243.4 0.2 compare_reduce_fusion
  243.6 0.5 convert_element_type.15.valid_ref
  244.1 0.7 fusion.4.source_ref
  244.8 0.0 copy-start.3
  244.8 0.0 copy-start.4
  244.8 0.0 copy-start.1
  244.8 101.1 %reduce_tiles.1 = (f32[10,64,512]{2,1,0:T(8,128)}, f32[8,512]{1,0:T(8,128)}, f32[8,128]{1,0:T(8,128)}) custom-call(s32[10]{0:T(128)} %fusion.4.source_ref, s32[10]{0:T(128)} %convert_element_type.15.valid_ref, f32[26,4,2,2,2,16,512]{6,5,4,3,2,1,0:T(8,128)} %bitcast.65, f32[8,512]{1,0:T(8,128)} %get-tuple-element.19.small_ref), custom_call_target="tpu_custom_call" | custom-call | tf_op jit(solution)/shard_map/reduce_tiles/pallas_call | solution.py:796
  345.9 1.3 multiply_reduce_fusion
  347.2 1.3 reduce_sum.38
  350.6 0.0 copy-done.3
  350.6 0.0 copy-done.4
  350.7 1.4 multiply_subtract_fusion
  352.0 0.0 copy-done.1
  352.0 5.5 %fusion.21 = (bf16[10,64,512]{2,1,0:T(8,128)(2,1)}, f32[10,64,512]{2,1,0:T(8,128)}, f32[10,64,512]{2,1,0:T(8,128)}, f32[10,64,512]{2,1,0:T(8,128)}) fusion(f32[10,64,512]{2,1,0:T(8,128)S(1)} %copy-done.1, f32[]{:T(128)} %bitcast.10, f32[10,64,512]{2,1,0:T(8,128)} %param.20, f32[]{:T(128)} %bitcast.9, f32[10,64,512]{2,1,0:T(8,128)} %get-tuple-element.22, ...), kind=kLoop, calls=%fused_computation.77 | loop fusion | flops 6553600 | bytes 9830422 | tf_op jit(solution)/shard_map/convert_element_type | solution.py:1398
  357.5 1.6 fusion.19
  (2 shorter events, 0.0 us)
Async XLA Ops:
  0.6 0.7 copy-start
  0.7 3.5 copy-start.7
  0.7 3.5 copy-start.6
  0.7 3.5 copy-start.5
  1.9 131.2 %copy-start.2 = (f32[6,512]{1,0:T(8,128)S(1)}, f32[6,512]{1,0:T(8,128)}, u32[]{:S(2)}) copy-start(f32[6,512]{1,0:T(8,128)} %param.21) | copy-start | bytes 36868
  133.7 109.7 %copy-start.8 = (s32[26]{0:T(128)S(1)}, s32[26]{0:T(128)}, u32[]{:S(2)}) copy-start(s32[26]{0:T(128)} %slot_ref.1) | copy-start | bytes 316
  244.8 105.8 %copy-start.3 = (f32[6,512]{1,0:T(8,128)S(1)}, f32[6,512]{1,0:T(8,128)}, u32[]{:S(2)}) copy-start(f32[6,512]{1,0:T(8,128)} %param.23) | copy-start | bytes 36868
  244.8 105.8 %copy-start.4 = (f32[6,512]{1,0:T(8,128)S(1)}, f32[6,512]{1,0:T(8,128)}, u32[]{:S(2)}) copy-start(f32[6,512]{1,0:T(8,128)} %param.22) | copy-start | bytes 36868
  244.8 107.2 %copy-start.1 = (f32[10,64,512]{2,1,0:T(8,128)S(1)}, f32[10,64,512]{2,1,0:T(8,128)}, u32[]{:S(2)}) copy-start(f32[10,64,512]{2,1,0:T(8,128)} %param.18) | copy-start | bytes 3932164

commit v4 on v3

--- a/solution.py
+++ b/solution.py
@@ -360,142 +360,6 @@
     for peer in peers:
         pl.semaphore_signal(barrier, inc=1, device_id=peer, device_id_type=MESH)
     pl.semaphore_wait(barrier, len(peers))
-
-
-def gather_kernel(
-    chunks, slot_ref, low_ref, ids_ref, full_ref, ids_out, slots, own, x_send, x_recv, own_sem,
-    n_send, n_recv, f_send, f_recv, c_send, c_recv, i_send, i_recv, i_own,
-):
-    dp, seq, z, core = places()
-    held, rows, _ = low_ref.shape
-    tile_count = full_ref.shape[0]
-    half = tile_count // 2
-    step_rows = rows // chunks
-    sibling = (z * 2 + 1 - core, seq)
-    up, down = ((z + 1) % 4 * 2 + core, seq), ((z + 3) % 4 * 2 + core, seq)
-    side = [(dp, seq_peer(seq, j)) for j in (1, 2, 3)]
-    meet([sibling, up, down] + side)
-
-    def rows_of(owner_z, chunk):
-        return pl.ds(pl.multiple_of((owner_z * 2 + core) * rows + chunk * step_rows, step_rows), step_rows)
-
-    def part(chunk):
-        return pl.ds(chunk * step_rows, step_rows)
-
-    side_copies = []
-    for chunk in range(chunks):
-        for j in range(3):
-            copy = remote(
-                low_ref.at[:, part(chunk)], slots[chunk].at[pl.ds(held * seq, held)],
-                x_send.at[chunk, j], x_recv.at[chunk, j], side[j],
-            )
-            copy.start()
-            side_copies.append(copy)
-        for j in range(3):
-            if chunk == 0:
-                copy = remote(
-                    ids_ref.at[side[j][1]], ids_out.at[seq], i_send.at[j], i_recv.at[j], side[j]
-                )
-                copy.start()
-                side_copies.append(copy)
-        slots[chunk][pl.ds(held * seq, held)] = low_ref[:, part(chunk), :]
-    ids_copy = pltpu.make_async_copy(ids_ref.at[seq], ids_out.at[seq], i_own)
-    ids_copy.start()
-
-    def near(chunk):
-        for j in range(3):
-            remote(
-                low_ref.at[:, part(chunk)], slots[chunk].at[pl.ds(held * seq, held)],
-                x_send.at[chunk, j], x_recv.at[chunk, j], side[j],
-            ).wait_recv()
-
-        def pick(tile, carry):
-            own[chunk, tile] = slots[chunk][slot_ref[tile]]
-            return carry
-
-        lax.fori_loop(0, tile_count, pick, 0)
-        place = full_ref.at[:, rows_of(z, chunk)]
-        for way, peer in enumerate((up, down)):
-            copy = remote(own.at[chunk], place, n_send.at[chunk, way], n_recv.at[chunk, way], peer)
-            copy.start()
-        copy = remote(own.at[chunk], place, c_send.at[chunk, 0], c_recv.at[chunk, 0], sibling)
-        copy.start()
-        copy = pltpu.make_async_copy(own.at[chunk], place, own_sem.at[chunk])
-        copy.start()
-
-    def far(chunk):
-        for way, peer in enumerate((up, down)):
-            origin = (z + 3) % 4 if way == 0 else (z + 1) % 4
-            place = full_ref.at[:, rows_of(origin, chunk)]
-            remote(own.at[chunk], place, n_send.at[chunk, way], n_recv.at[chunk, way], peer).wait_recv()
-            portion = full_ref.at[pl.ds(way * half, half), rows_of(origin, chunk)]
-            copy = remote(portion, portion, f_send.at[chunk, way], f_recv.at[chunk, way], peer)
-            copy.start()
-            copy = remote(place, place, c_send.at[chunk, 1 + way], c_recv.at[chunk, 1 + way], sibling)
-            copy.start()
-
-    def last(chunk):
-        for way, peer in enumerate((up, down)):
-            portion = full_ref.at[pl.ds(way * half, half), rows_of((z + 2) % 4, chunk)]
-            remote(portion, portion, f_send.at[chunk, way], f_recv.at[chunk, way], peer).wait_recv()
-            copy = remote(portion, portion, c_send.at[chunk, 3 + way], c_recv.at[chunk, 3 + way], sibling)
-            copy.start()
-
-    for tick in range(chunks + 2):
-        if tick < chunks:
-            near(tick)
-        if 0 <= tick - 1 < chunks:
-            far(tick - 1)
-        if 0 <= tick - 2 < chunks:
-            last(tick - 2)
-    for copy in side_copies:
-        copy.wait_send()
-    for j in range(3):
-        remote(ids_ref.at[side[j][1]], ids_out.at[seq], i_send.at[j], i_recv.at[j], side[j]).wait_recv()
-    ids_copy.wait()
-    for chunk in range(chunks):
-        place = full_ref.at[:, rows_of(z, chunk)]
-        for way, peer in enumerate((up, down)):
-            remote(own.at[chunk], place, n_send.at[chunk, way], n_recv.at[chunk, way], peer).wait_send()
-            portion = full_ref.at[pl.ds(way * half, half), rows_of(z, chunk)]
-            remote(portion, portion, f_send.at[chunk, way], f_recv.at[chunk, way], peer).wait_send()
-        pltpu.make_async_copy(own.at[chunk], place, own_sem.at[chunk]).wait()
-        for turn in range(5):
-            piece = full_ref.at[:, rows_of(z, chunk)] if turn < 3 else full_ref.at[pl.ds(0, half), rows_of(z, chunk)]
-            remote(piece, piece, c_send.at[chunk, turn], c_recv.at[chunk, turn], sibling).wait()
-
-
-def gather_tiles_kernel(low, ids, owner_slot):
-    held, rows, width = low.shape
-    tile_count = owner_slot.shape[0]
-    seq_count, dp_count = lax.axis_size("seq"), lax.axis_size("dp")
-    chunks = 4
-    step_rows = rows // chunks
-    dma = pltpu.SemaphoreType.DMA
-    return pl.pallas_call(
-        functools.partial(gather_kernel, chunks),
-        out_shape=(
-            jax.ShapeDtypeStruct((tile_count, dp_count * rows, width), low.dtype),
-            jax.ShapeDtypeStruct(ids.shape, ids.dtype),
-        ),
-        in_specs=[
-            pl.BlockSpec(memory_space=pltpu.SMEM),
-            pl.BlockSpec(memory_space=pltpu.VMEM),
-            pl.BlockSpec(memory_space=pltpu.VMEM),
-        ],
-        out_specs=(pl.BlockSpec(memory_space=pl.ANY), pl.BlockSpec(memory_space=pltpu.VMEM)),
-        scratch_shapes=[
-            [pltpu.VMEM((seq_count * held, step_rows, width), low.dtype)] * chunks,
-            pltpu.VMEM((chunks, tile_count, step_rows, width), low.dtype),
-            dma((chunks, 3)), dma((chunks, 3)), dma((chunks,)),
-            dma((chunks, 2)), dma((chunks, 2)), dma((chunks, 2)), dma((chunks, 2)),
-            dma((chunks, 5)), dma((chunks, 5)), dma((3,)), dma((3,)), dma,
-        ],
-        name="gather_tiles",
-        compiler_params=pltpu.CompilerParams(
-            collective_id=0, has_side_effects=True, vmem_limit_bytes=VMEM_LIMIT
-        ),
-    )(owner_slot, low, ids)
 
 
 CODE_TOP = 32000.0
@@ -845,6 +709,8 @@
 
 
 ROWS = 256
+LAG = 2
+START = 10
 
 
 def split_three(value):
@@ -903,13 +769,13 @@
 
 
 class Block:
-    def __init__(self, length, first_tile, gain_row, entry, qkv, logs, attended, after, inner, leave):
-        self.length, self.tile, self.gain_row = length, first_tile, gain_row
+    def __init__(self, length, first_tile, place, gain_row, entry, qkv, logs, attended, after, inner, leave):
+        self.length, self.tile, self.place, self.gain_row = length, first_tile, place, gain_row
         self.entry, self.qkv, self.logs, self.attended = entry, qkv, logs, attended
         self.after, self.inner, self.leave = after, inner, leave
 
 
-def attend(block):
+def attend(block, pump):
     length = block.length
 
     def pair_step(pair, carry):
@@ -929,6 +795,7 @@
                 outs.append(product_tn(weights, block.qkv[0:span, lanes[2]]))
             merged = jnp.where(head_mask(outs[0].shape, 0), outs[0], outs[1])
             block.attended[first:span, lanes[0]] = merged.astype(jnp.bfloat16)
+        pump(pair)
         return carry
 
     lax.fori_loop(0, 4, pair_step, 0)
@@ -972,8 +839,8 @@
     lax.fori_loop(0, 4, pair_step, 0)
 
 
-def block_run(block, weights, gains):
-    tile = block.tile
+def block_run(block, matrix, gains, pumps):
+    place = block.place
     gain_attn = gains[block.gain_row : block.gain_row + 1, :]
     gain_ffn = gains[block.gain_row + 1 : block.gain_row + 2, :]
 
@@ -981,30 +848,33 @@
         value = block.entry[rows, :]
         normed = (value * root_scale(value) * gain_attn).astype(jnp.bfloat16)
         for part in range(3):
-            block.qkv[rows, 512 * part : 512 * part + 512] = product(normed, weights[tile + part]).astype(
+            block.qkv[rows, 512 * part : 512 * part + 512] = product(normed, matrix(place + part)).astype(
                 jnp.bfloat16
             )
 
     each_block(block.length, project)
-    attend(block)
+    pumps[0]()
+    attend(block, pumps[1])
+    pumps[2]()
 
     def feed(rows):
-        after = block.entry[rows, :] + product(block.attended[rows, :], weights[tile + 3])
+        after = block.entry[rows, :] + product(block.attended[rows, :], matrix(place + 3))
         block.after[rows, :] = after
         normed = (after * root_scale(after) * gain_ffn).astype(jnp.bfloat16)
         total = jnp.zeros_like(after)
         for part in range(4):
-            inner = product(normed, weights[tile + 4 + part])
+            inner = product(normed, matrix(place + 4 + part))
             block.inner[rows, 512 * part : 512 * part + 512] = inner
             active = gelu_both(inner)[0].astype(jnp.bfloat16)
-            total = total + product(active, weights[tile + 8 + part])
+            total = total + product(active, matrix(place + 8 + part))
         block.leave[rows, :] = after + total
+        pumps[3](rows.start // ROWS)
 
     each_block(block.length, feed)
 
 
-def block_back(block, grad, weights, gains, gain_sums, temps, put):
-    length, tile = block.length, block.tile
+def block_back(block, grad, matrix, gains, gain_sums, temps, put):
+    length, tile, place = block.length, block.tile, block.place
     gain_attn = gains[block.gain_row : block.gain_row + 1, :]
     gain_ffn = gains[block.gain_row + 1 : block.gain_row + 2, :]
     turned, grad_inner, branch, upstream, turned_norm, key_sum, value_sum = temps
@@ -1017,7 +887,7 @@
             columns = pl.ds(pl.multiple_of(part * 512, 512), 512)
             active, slope = gelu_both(block.inner[rows, columns])
             turned[:, rows] = turn(active)
-            grad_inner[rows, columns] = (product_nt(low, weights[tile + 8 + part]) * slope).astype(jnp.bfloat16)
+            grad_inner[rows, columns] = (product_nt(low, matrix(place + 8 + part)) * slope).astype(jnp.bfloat16)
 
         each_block(length, rows_step)
 
@@ -1041,7 +911,7 @@
         total = jnp.zeros_like(after)
         for part in range(4):
             total = total + product_nt(
-                grad_inner[rows, 512 * part : 512 * part + 512], weights[tile + 4 + part]
+                grad_inner[rows, 512 * part : 512 * part + 512], matrix(place + 4 + part)
             )
         back, gain_part = norm_back(after, scale, gain_ffn, total)
         row = block.gain_row + 1
@@ -1050,7 +920,7 @@
         grad[rows, :] = grad_after
         low = grad_after.astype(jnp.bfloat16)
         branch[rows, :] = low
-        upstream[rows, :] = product_nt(low, weights[tile + 3]).astype(jnp.bfloat16)
+        upstream[rows, :] = product_nt(low, matrix(place + 3)).astype(jnp.bfloat16)
 
     each_block(length, middle)
 
@@ -1069,7 +939,7 @@
         turned_norm[:, rows] = turn(value * scale * gain_attn)
         total = jnp.zeros_like(value)
         for part in range(3):
-            total = total + product_nt(grad_qkv[rows, 512 * part : 512 * part + 512], weights[tile + part])
+            total = total + product_nt(grad_qkv[rows, 512 * part : 512 * part + 512], matrix(place + part))
         back, gain_part = norm_back(value, scale, gain_attn, total)
         row = block.gain_row
         gain_sums[row : row + 1, :] = gain_sums[row : row + 1, :] + gain_part
@@ -1086,31 +956,140 @@
 
 
 def step_kernel(
-    micro_count, length_ref, tiles_ref, ids_ref, gains_ref, grads_ref, small_ref,
-    weights, load_sem, entry, qkv, logs, attended, after, inner, leave, grad,
+    micro_count, length_ref, local_ref, valid_ref, master_ref, ids_ref, gains_ref, grads_ref, small_ref,
+    weights, entry, qkv, logs, attended, after, inner, leave, grad,
     seg_entry, seg_qkv, seg_logs, seg_attended, seg_after, seg_inner, seg_leave, seg_grad,
     turned, grad_inner, branch, upstream, turned_norm, key_sum, value_sum,
-    ids_col, stage, stage_sem, counts, count_send, count_recv,
+    ids_row, ids_col, stage, stage_sem, counts, count_send, count_recv, i_send, i_recv, i_own,
+    p_send, p_recv, z_send, z_recv, s_send, s_recv, d_send, d_recv, c_send, c_recv,
 ):
-    dp, seq, _, _ = places()
+    dp, seq, z, core = places()
+    across, along = seq % 2, seq // 2
     length = entry.shape[0]
     width = entry.shape[1]
     segments = seg_entry.shape[0]
     vocab = width // 2
     root_width = width ** (-0.5)
+    groups = weights.shape[0] // 2
+    sibling = (z * 2 + 1 - core, seq)
+    beside = [along * 2 + 1 - across, (1 - along) * 2 + across]
+    side = [seq_peer(seq, j) for j in (1, 2, 3)]
     column = [((dp + j) % 8, seq) for j in range(1, 8)]
-    meet(column)
-
-    def load(tile):
-        return pltpu.make_async_copy(tiles_ref.at[tile], weights.at[tile], load_sem.at[tile])
-
-    order = [25] + list(range(12)) + [24] + list(range(12, 24))
-    for tile in order:
-        load(tile).start()
-
-    def ready(tiles):
-        for tile in tiles:
-            load(tile).wait()
+    tower = [((z + j) % 4 * 2 + core, seq) for j in (1, 2, 3)]
+    meet([(dp, peer) for peer in side] + column)
+
+    def ids_copy(j):
+        part = pl.ds(pl.multiple_of(seq * ids_ref.shape[2], 256), ids_ref.shape[2])
+        return remote(ids_ref.at[side[j]], ids_row.at[:, part], i_send.at[j], i_recv.at[j], (dp, side[j]))
+
+    def own_ids():
+        part = pl.ds(pl.multiple_of(seq * ids_ref.shape[2], 256), ids_ref.shape[2])
+        return pltpu.make_async_copy(ids_ref.at[seq], ids_row.at[:, part], i_own)
+
+    def part_of(which):
+        return pl.ds(pl.multiple_of(which * width, width), width)
+
+    def peer_copy(group, j):
+        return remote(
+            grad_inner.at[pl.ds(pl.multiple_of(group * 32, 32), 32), part_of(side[j])],
+            grad_inner.at[pl.ds(pl.multiple_of(512 + group * 32, 32), 32), part_of(j)],
+            p_send.at[j, group], p_recv.at[j, group], (dp, side[j]),
+        )
+
+    def tower_copy(group, j):
+        spot = weights.at[pl.ds(group * 2, 2), z, core, seq]
+        return remote(spot, spot, z_send.at[j, group], z_recv.at[j, group], tower[j])
+
+    def side_copy(group, way):
+        spot = weights.at[pl.ds(group * 2, 2), :, core, seq]
+        return remote(spot, spot, s_send.at[way, group], s_recv.at[way, group], (dp, beside[way]))
+
+    def corner_copy(group, way):
+        spot = weights.at[group * 2 + way, :, core, beside[way]]
+        return remote(spot, spot, d_send.at[way, group], d_recv.at[way, group], (dp, beside[1 - way]))
+
+    def core_copy(group):
+        spot = weights.at[pl.ds(group * 2, 2), :, core]
+        return remote(spot, spot, c_send.at[group], c_recv.at[group], sibling)
+
+    def offer(group):
+        for j in (2, 0, 1):
+            peer_copy(group, j).start()
+
+    def combine(group):
+        for j in range(3):
+            peer_copy(group, j).wait_recv()
+        for number in range(2):
+            row = group * 32 + number * 16
+            value = grad_inner[pl.ds(pl.multiple_of(row, 16), 16), part_of(seq)]
+            for j in range(3):
+                value = value + grad_inner[pl.ds(pl.multiple_of(512 + row, 16), 16), pl.ds(j * width, width)]
+            weights[group * 2 + number, z, core, seq] = value
+        for j in range(3):
+            tower_copy(group, j).start()
+
+    def widen(group):
+        for j in range(3):
+            tower_copy(group, j).wait_recv()
+        for way in range(2):
+            side_copy(group, way).start()
+
+    def corner(group):
+        for way in range(2):
+            side_copy(group, way).wait_recv()
+        for way in range(2):
+            corner_copy(group, way).start()
+
+    def share(group):
+        for way in range(2):
+            corner_copy(group, way).wait_recv()
+        core_copy(group).start()
+
+    stages = (offer, combine, widen, corner, share)
+
+    def tick(number):
+        for order, stage_of in enumerate(stages):
+            group = number - LAG * order
+
+            @pl.when(jnp.logical_and(group >= 0, group < groups))
+            def _():
+                stage_of(group)
+
+    def ticks(start, stop):
+        def body(number, carry):
+            tick(number)
+            return carry
+
+        lax.fori_loop(start, stop, body, 0)
+
+    def arrived(first, last):
+        def body(group, carry):
+            core_copy(group).wait_recv()
+            return carry
+
+        lax.fori_loop(first, last, body, 0)
+
+    for j in range(3):
+        ids_copy(j).start()
+    own_ids().start()
+
+    def pick(place, carry):
+        value = master_ref[local_ref[place]]
+        value = jnp.where(valid_ref[place] > 0, value, jnp.zeros_like(value)).astype(jnp.bfloat16)
+        for quarter in range(4):
+            grad_inner[pl.ds(pl.multiple_of(place * 16, 16), 16), quarter * width : quarter * width + width] = value[
+                16 * quarter : 16 * quarter + 16
+            ]
+        return carry
+
+    lax.fori_loop(0, groups * 2, pick, 0)
+    ticks(0, START)
+
+    def matrix(place):
+        return weights[place].reshape(width, width)
+
+    def matrix_half(which):
+        return weights[0, 2 * which : 2 * which + 2].reshape(vocab, width)
 
     def count_copy(j):
         return remote(counts.at[dp], counts.at[dp], count_send.at[j], count_recv.at[j], column[j])
@@ -1125,11 +1104,14 @@
         staged(tile, slot).start()
 
     small_ref[...] = jnp.zeros_like(small_ref)
-    ids_col[...] = ids_ref[...].astype(jnp.float32).T
+    own_ids().wait()
+    for j in range(3):
+        ids_copy(j).wait_recv()
+    ids_col[...] = ids_row[...].astype(jnp.float32).T
     length_one = length_ref[0]
-    char = Block(length, 0, 0, entry, qkv, logs, attended, after, inner, leave)
+    char = Block(length, 0, 1, 0, entry, qkv, logs, attended, after, inner, leave)
     seg = Block(
-        segments, 12, 2, seg_entry, seg_qkv, seg_logs, seg_attended, seg_after, seg_inner, seg_leave
+        segments, 12, 14, 2, seg_entry, seg_qkv, seg_logs, seg_attended, seg_after, seg_inner, seg_leave
     )
     temps = (turned, grad_inner, branch, upstream, turned_norm, key_sum, value_sum)
 
@@ -1139,19 +1121,29 @@
         return (ids == lane).astype(jnp.bfloat16)
 
     def hot_turned(which, offset, count):
-        ids = ids_ref[which : which + 1, :] + offset
+        ids = ids_row[which : which + 1, :] + offset
         line = lax.broadcasted_iota(jnp.int32, (count, length), 0)
         return (ids == line).astype(jnp.float32)
 
-    ready([25])
+    arrived(0, 2)
 
     def embed(rows):
-        entry[rows, :] = product(hot_rows(rows, 0, 0, vocab), weights[25, 0:vocab, :])
+        entry[rows, :] = product(hot_rows(rows, 0, 0, vocab), matrix_half(0))
 
     each_block(length, embed)
-    ready(range(12))
-    block_run(char, weights, gains_ref)
-    ready([24])
+    tick(START)
+    block_run(
+        char,
+        matrix,
+        gains_ref,
+        (
+            lambda: tick(START + 1),
+            lambda pair: tick(START + 2 + pair),
+            lambda: arrived(2, 7),
+            lambda number: tick(START + 6 + number),
+        ),
+    )
+    ticks(START + 10, groups + LAG * (len(stages) - 1))
 
     def valid_rows(rows):
         line = lax.broadcasted_iota(jnp.int32, (ROWS, 1), 0) + rows.start
@@ -1159,7 +1151,7 @@
 
     def boundary(rows):
         low = leave[rows, :].astype(jnp.bfloat16)
-        reach = jnp.tanh(product(low, weights[24]))
+        reach = jnp.tanh(product(low, matrix(13)))
         logit = jnp.sum(reach * gains_ref[5:6, :], axis=1, keepdims=True) * root_width
         return low, reach, 1.0 / (1.0 + jnp.exp(-logit))
 
@@ -1178,8 +1170,8 @@
     amounts = jnp.sum(pool, axis=1, keepdims=True)
     divisor = jnp.maximum(amounts, 1.0)
     seg_entry[...] = product(pool.astype(jnp.bfloat16), leave[...].astype(jnp.bfloat16)) / divisor
-    ready(range(12, 24))
-    block_run(seg, weights, gains_ref)
+    arrived(7, groups)
+    block_run(seg, matrix, gains_ref, (lambda: None, lambda pair: None, lambda: None, lambda number: None))
 
     for j in range(7):
         count_copy(j).wait_recv()
@@ -1196,7 +1188,7 @@
         scale = root_scale(merged)
         gain = gains_ref[4:5, :]
         final_low = (merged * scale * gain).astype(jnp.bfloat16)
-        table = weights[25, vocab : 2 * vocab, :]
+        table = matrix_half(1)
         logits = product_nt(final_low, table)
         peak = jnp.max(logits, axis=1, keepdims=True)
         log_total = peak + jnp.log(jnp.sum(jnp.exp(logits - peak), axis=1, keepdims=True))
@@ -1219,7 +1211,18 @@
     for slot in range(4):
         staged(slot, slot).start()
     seg_grad[...] = exact_product(hot_turned(2, 0, segments).astype(jnp.bfloat16), grad[...])
-    block_back(seg, seg_grad, weights, gains_ref, small_ref, temps, put)
+    def sent(group, carry):
+        for j in range(3):
+            peer_copy(group, j).wait_send()
+            tower_copy(group, j).wait_send()
+        for way in range(2):
+            side_copy(group, way).wait_send()
+            corner_copy(group, way).wait_send()
+        core_copy(group).wait_send()
+        return carry
+
+    lax.fori_loop(0, groups, sent, 0)
+    block_back(seg, seg_grad, matrix, gains_ref, small_ref, temps, put)
     seg_grad[...] = seg_grad[...] / divisor
 
     count_rest = count_all - soft_count
@@ -1234,11 +1237,11 @@
         branch[rows, :] = pre
         turned[:, rows] = turn(low)
         spread = exact_product(hot_rows(rows, 2, 1, segments), seg_grad[...])
-        grad[rows, :] = (grad[rows, :] + spread) + product_nt(pre, weights[24])
+        grad[rows, :] = (grad[rows, :] + spread) + product_nt(pre, matrix(13))
 
     each_block(length, join)
     put(24, 0, lambda half: product(turned[half, :], branch[...]))
-    block_back(char, grad, weights, gains_ref, small_ref, temps, put)
+    block_back(char, grad, matrix, gains_ref, small_ref, temps, put)
     staged(25, 3).wait()
     stage[3, 0:vocab, :] = exact_product(hot_turned(0, 0, vocab).astype(jnp.bfloat16), grad[...])
     stage[3, vocab : 2 * vocab, :] = head_sum
@@ -1254,15 +1257,24 @@
         staged(slot, slot).wait()
     for j in range(7):
         count_copy(j).wait_send()
-
-
-def step_call(length_one, tiles, ids, gains, micro_count):
-    tile_count, width, _ = tiles.shape
-    length = ids.shape[1]
-    segments = SEG_DEV * lax.axis_size("seq")
+    for j in range(3):
+        ids_copy(j).wait_send()
+
+
+def step_call(length_one, owner_slot, master, ids, gains, micro_count):
+    held, _, width = master.shape
+    tile_count = owner_slot.shape[0]
+    seq_count, dp_count = lax.axis_size("seq"), lax.axis_size("dp")
+    groups = tile_count // 2
+    length = seq_count * ids.shape[2]
+    segments = SEG_DEV * seq_count
     dma = pltpu.SemaphoreType.DMA
     vmem = pl.BlockSpec(memory_space=pltpu.VMEM)
+    smem = pl.BlockSpec(memory_space=pltpu.SMEM)
     hbm = pl.BlockSpec(memory_space=pl.ANY)
+    local = jnp.concatenate([owner_slot[25:], owner_slot[:12], owner_slot[24:25], owner_slot[12:24]])
+    local = local - lax.axis_index("seq") * held
+    valid = jnp.logical_and(local >= 0, local < held).astype(jnp.int32)
 
     def full(*shape):
         return pltpu.VMEM(shape, jnp.float32)
@@ -1282,33 +1294,34 @@
             jax.ShapeDtypeStruct((tile_count, width, width), jnp.float32),
             jax.ShapeDtypeStruct((8, width), jnp.float32),
         ),
-        in_specs=[pl.BlockSpec(memory_space=pltpu.SMEM), hbm, vmem, vmem],
+        in_specs=[smem, smem, smem, vmem, vmem, vmem],
         out_specs=(hbm, vmem),
-        scratch_shapes=[half(tile_count, width, width), dma((tile_count,))]
+        scratch_shapes=[half(tile_count, 4, 2, 4, 16, width)]
         + kept(length)
         + kept(segments)
         + [
             half(width, length), half(length, 4 * width), half(length, width), half(length, width),
-            half(width, length), full(length, 128),
-            full(length, 128), full(length, 8), full(4, width, width), dma((4,)),
-            full(lax.axis_size("dp"), 8, 128), dma((7,)), dma((7,)),
+            half(width, length), full(length, 128), full(length, 128),
+            pltpu.VMEM((8, length), jnp.int32), full(length, 8), full(4, width, width), dma((4,)),
+            full(dp_count, 8, 128), dma((7,)), dma((7,)), dma((3,)), dma((3,)), dma,
+            dma((3, groups)), dma((3, groups)), dma((3, groups)), dma((3, groups)),
+            dma((2, groups)), dma((2, groups)), dma((2, groups)), dma((2, groups)),
+            dma((groups,)), dma((groups,)),
         ],
         name="step",
         compiler_params=pltpu.CompilerParams(
             collective_id=2, has_side_effects=True, vmem_limit_bytes=STEP_VMEM
         ),
-    )(length_one, tiles, ids, gains)
+    )(length_one, jnp.where(valid > 0, local, 0), valid, master, ids, gains)
 
 
 def whole_step(char_ids, targets, seg_ids, lengths, owner_slot, master, gain_rows):
     micro_count = char_ids.shape[0]
     ids = jnp.stack([char_ids[:, 0], targets[:, 0], seg_ids[:, 0]], axis=1)
     ids = jnp.pad(ids, ((0, 0), (0, 5), (0, 0)))
-    tiles, ids = gather_tiles_kernel(master.astype(jnp.bfloat16), ids, owner_slot)
-    ids = ids.transpose(1, 0, 2).reshape(8, -1)
     length_one = lax.dynamic_slice_in_dim(lengths[:, 0], lax.axis_index("seq"), 1)
     gains = jnp.pad(gain_rows, ((0, 2), (0, 0)))
-    return step_call(length_one, tiles, ids, gains, micro_count)
+    return step_call(length_one, owner_slot, master, ids, gains, micro_count)
 
 
 def body(

time: 363 us -> 298 us (0.82)
  Pallas kernels: 339 us -> 271 us
    pallas_call x1 -> x0, Pallas kernels: 128 us -> none  [gather_tiles_kernel(): pl.pallas_call(functools.partial(gather_kernel, chunks), out_shape=(jax.S...]
    pallas_call x1, Pallas kernels: 110 us -> 167 us  [step_call(): pl.pallas_call(functools.partial(step_kernel, micro_count), out_shape=(ja...]
where the time goes in v4:
time: 298 us; the launch traced here: 297 us
  Pallas kernels  271 us (91%)
  other arithmetic  15.3 us (5%)
  between operations  5.76 us (2%)
  local copies, waits for them, and re-layouts  4.7 us (2%)
    pallas_call x1, Pallas kernels, step_call(): pl.pallas_call(functools.partial(step_kernel, micro_count), out_shape=(ja...  167 us
    pallas_call x1, Pallas kernels, reduce_tiles_kernel(): pl.pallas_call(reduce_kernel, out_shape=(jax.ShapeDtypeStruct((held, rows...  104 us

profile of v4, /device:TPU:0, one launch (start us, length us, event | category | flops | bytes accessed | tf_op | source)
XLA Modules:
  0.0 297.0 jit_solution(8116439262283841049)
XLA Ops:
  0.6 0.0 copy-start
  0.7 0.0 copy-start.6
  0.7 1.3 fusion.22
  2.0 0.8 fusion.23
  2.8 1.9 and_convert_fusion
  4.7 0.5 compare_select_fusion.7.local_ref
  5.2 0.0 copy-done
  5.2 0.6 constant_dynamic-slice_fusion
  5.8 0.7 pad_add_fusion
  6.5 0.6 pad.8.ids_ref
  7.2 1.3 pad.9.gains_ref
  8.5 167.1 %step.1 = (f32[26,512,512]{2,1,0:T(8,128)}, f32[8,512]{1,0:T(8,128)}) custom-call(s32[1]{0:T(128)} %bitcast.length_ref, s32[26]{0:T(128)} %compare_select_fusion.7.local_ref, s32[26]{0:T(128)} %get-tuple-element.24.valid_ref, f32[10,64,512]{2,1,0:T(8,128)} %master_ref.1, s32[4,8,256]{2,1,0:T(8,128)} %pad.8.ids_ref, f32[8,512]{1,0:T(8,128)} %pad.9.gains_ref), custom_call_target="tpu_custom_call" | custom-call | tf_op jit(solution)/shard_map/step/pallas_call | solution.py:1291
  175.6 0.0 copy-done.6
  175.6 0.2 compare_reduce_fusion
  175.8 0.5 convert_element_type.15.valid_ref
  176.3 0.7 fusion.4.source_ref
  177.0 0.0 copy-start.3
  177.0 0.0 copy-start.4
  177.0 0.0 copy-start.5
  177.0 0.0 copy-start.1
  177.0 0.0 copy-start.2
  177.0 104.1 %reduce_tiles.1 = (f32[10,64,512]{2,1,0:T(8,128)}, f32[8,512]{1,0:T(8,128)}, f32[8,128]{1,0:T(8,128)}) custom-call(s32[10]{0:T(128)} %fusion.4.source_ref, s32[10]{0:T(128)} %convert_element_type.15.valid_ref, f32[26,4,2,2,2,16,512]{6,5,4,3,2,1,0:T(8,128)} %bitcast.62, f32[8,512]{1,0:T(8,128)} %get-tuple-element.15.small_ref), custom_call_target="tpu_custom_call" | custom-call | tf_op jit(solution)/shard_map/reduce_tiles/pallas_call | solution.py:660
  281.2 1.3 multiply_reduce_fusion
  282.5 1.3 reduce_sum.38
  285.9 0.0 copy-done.3
  285.9 0.0 copy-done.4
  285.9 0.0 copy-done.5
  285.9 1.4 multiply_subtract_fusion
  287.3 0.0 copy-done.1
  287.3 0.0 copy-done.2
  287.3 5.2 %fusion.21 = (bf16[10,64,512]{2,1,0:T(8,128)(2,1)}, f32[10,64,512]{2,1,0:T(8,128)}, f32[10,64,512]{2,1,0:T(8,128)}, f32[10,64,512]{2,1,0:T(8,128)}) fusion(f32[10,64,512]{2,1,0:T(8,128)S(1)} %copy-done.1, f32[]{:T(128)} %bitcast.8, f32[10,64,512]{2,1,0:T(8,128)S(1)} %copy-done.2, f32[]{:T(128)} %bitcast.7, f32[10,64,512]{2,1,0:T(8,128)} %get-tuple-element.18, ...), kind=kLoop, calls=%fused_computation.80 | loop fusion | flops 6553600 | bytes 9830422 | tf_op jit(solution)/shard_map/convert_element_type | solution.py:1411
  292.5 1.6 fusion.19
  (1 shorter events, 0.0 us)
Async XLA Ops:
  0.6 4.6 %copy-start = (s32[4,1]{0,1:T(1,128)S(1)}, s32[4,1]{0,1:T(1,128)}, u32[]{:S(2)}) copy-start(s32[4,1]{0,1:T(1,128)} %param.15) | copy-start | bytes 52
  0.7 174.9 %copy-start.6 = (s32[26]{0:T(128)S(1)}, s32[26]{0:T(128)}, u32[]{:S(2)}) copy-start(s32[26]{0:T(128)} %param.16) | copy-start | bytes 316
  177.0 108.9 %copy-start.3 = (f32[6,512]{1,0:T(8,128)S(1)}, f32[6,512]{1,0:T(8,128)}, u32[]{:S(2)}) copy-start(f32[6,512]{1,0:T(8,128)} %param.21) | copy-start | bytes 36868
  177.0 108.9 %copy-start.4 = (f32[6,512]{1,0:T(8,128)S(1)}, f32[6,512]{1,0:T(8,128)}, u32[]{:S(2)}) copy-start(f32[6,512]{1,0:T(8,128)} %param.23) | copy-start | bytes 36868
  177.0 108.9 %copy-start.5 = (f32[6,512]{1,0:T(8,128)S(1)}, f32[6,512]{1,0:T(8,128)}, u32[]{:S(2)}) copy-start(f32[6,512]{1,0:T(8,128)} %param.22) | copy-start | bytes 36868
  177.0 110.3 %copy-start.1 = (f32[10,64,512]{2,1,0:T(8,128)S(1)}, f32[10,64,512]{2,1,0:T(8,128)}, u32[]{:S(2)}) copy-start(f32[10,64,512]{2,1,0:T(8,128)} %master_ref.1) | copy-start | bytes 3932164
  177.0 110.3 %copy-start.2 = (f32[10,64,512]{2,1,0:T(8,128)S(1)}, f32[10,64,512]{2,1,0:T(8,128)}, u32[]{:S(2)}) copy-start(f32[10,64,512]{2,1,0:T(8,128)} %param.20) | copy-start | bytes 3932164

commit v5 on v4

--- a/solution.py
+++ b/solution.py
@@ -381,319 +381,6 @@
     return jnp.concatenate([value[0:8, :] * unit, value[8:16, :] * unit], axis=0)
 
 
-def reduce_kernel(
-    source_ref, valid_ref, grads_ref, small_ref, out_ref, small_out, square_out,
-    own, other, b1_out, b1_in, b2_out, b2_in, c_out, c_in, d_out, d_in,
-    b1_unit_out, b1_unit_in, b2_unit_out, b2_unit_in, c_unit_out, c_unit_in, d_unit_out, d_unit_in,
-    final, small_dp, small_seq, square_dp, square_seq,
-    l_sem, a_send, a_recv, b1_send, b1_recv, b2_send, b2_recv, c_send, c_recv, d_send, d_recv,
-    p_send, p_recv, q_send, q_recv, r_send, r_recv, s_send, s_recv,
-):
-    dp, seq, z, core = places()
-    across, along = seq % 2, seq // 2
-    held = out_ref.shape[0]
-    tile_count = grads_ref.shape[0]
-    pairs = tile_count // 2
-    sibling = (z * 2 + 1 - core, seq)
-    beside = [(dp, along * 2 + 1 - across), (dp, (1 - along) * 2 + across)]
-    side = [(dp, seq_peer(seq, j)) for j in (1, 2, 3)]
-    column = [((dp + j) % 8, seq) for j in range(1, 8)]
-    tower = [((z + j) % 4 * 2 + core, seq) for j in (1, 2, 3)]
-    meet(side + column)
-    lane = lax.broadcasted_iota(jnp.int32, (8, 128), 1)
-
-    def core_copy(pair):
-        two = pl.ds(pair * 2, 2)
-        return remote(grads_ref.at[two, :, 1 - core], other.at[two], a_send.at[pair], a_recv.at[pair], sibling)
-
-    def local_copy(pair):
-        two = pl.ds(pair * 2, 2)
-        return pltpu.make_async_copy(grads_ref.at[two, :, core], own.at[two], l_sem.at[pair])
-
-    def with_units(values, units, send, recv, peer):
-        return [
-            remote(values[0], values[1], send.at[0], recv.at[0], peer),
-            remote(units[0], units[1], send.at[1], recv.at[1], peer),
-        ]
-
-    def first_copies(pair, order):
-        tile = pair * 2 + order
-        return with_units(
-            (b1_out.at[tile], b1_in.at[tile]), (b1_unit_out.at[tile], b1_unit_in.at[tile]),
-            b1_send.at[tile], b1_recv.at[tile], beside[order],
-        )
-
-    def second_copies(pair, order):
-        tile = pair * 2 + order
-        return with_units(
-            (b2_out.at[tile], b2_in.at[tile]), (b2_unit_out.at[tile], b2_unit_in.at[tile]),
-            b2_send.at[tile], b2_recv.at[tile], beside[1 - order],
-        )
-
-    def tower_copies(pair, j):
-        two = pl.ds(pair * 2, 2)
-        return with_units(
-            (c_out.at[j, two], c_in.at[j, two]), (c_unit_out.at[j, pair], c_unit_in.at[j, pair]),
-            c_send.at[j, pair], c_recv.at[j, pair], tower[j],
-        )
-
-    def share_copies(pair, j):
-        two = pl.ds(pair * 2, 2)
-        return with_units(
-            (d_out.at[two], d_in.at[j, two]), (d_unit_out.at[pair], d_unit_in.at[j, pair]),
-            d_send.at[j, pair], d_recv.at[j, pair], side[j],
-        )
-
-    def start_all(copies):
-        for copy in copies:
-            copy.start()
-
-    def arrive_all(copies):
-        for copy in copies:
-            copy.wait_recv()
-
-    def sent_all(copies):
-        for copy in copies:
-            copy.wait_send()
-
-    def small_copy(j):
-        return remote(small_ref, small_dp.at[dp], p_send.at[j], p_recv.at[j], column[j])
-
-    def small_side(j):
-        return remote(small_seq.at[seq], small_seq.at[seq], q_send.at[j], q_recv.at[j], side[j])
-
-    def square_copy(j):
-        return remote(square_dp.at[dp], square_dp.at[dp], r_send.at[j], r_recv.at[j], column[j])
-
-    def square_side(j):
-        return remote(square_seq.at[seq], square_seq.at[seq], s_send.at[j], s_recv.at[j], side[j])
-
-    for j in range(7):
-        small_copy(j).start()
-
-    def launch(pair, carry):
-        core_copy(pair).start()
-        local_copy(pair).start()
-        return carry
-
-    lax.fori_loop(0, pairs, launch, 0)
-
-    def cell(tile, order, floor, line, mine):
-        if order == 0:
-            return (tile, floor, line, across if mine else 1 - across)
-        return (tile, floor, along if mine else 1 - along, line)
-
-    def stage_one(pair):
-        core_copy(pair).wait_recv()
-        local_copy(pair).wait()
-
-        def add(step, carry):
-            tile, floor = pair * 2 + step // 4, step % 4
-            own[tile, floor] = own[tile, floor] + other[tile, floor]
-            return carry
-
-        lax.fori_loop(0, 8, add, 0)
-        for order in range(2):
-            tile = pair * 2 + order
-            units = jnp.zeros((8, 128), jnp.float32)
-            for floor in range(4):
-                for line in range(2):
-                    coded, unit = encode(own[cell(tile, order, floor, line, False)])
-                    b1_out[tile, floor * 2 + line] = coded
-                    units = jnp.where(lane == floor * 2 + line, unit, units)
-            b1_unit_out[tile] = units
-            start_all(first_copies(pair, order))
-
-    def stage_two(pair):
-        for order in range(2):
-            tile = pair * 2 + order
-            arrive_all(first_copies(pair, order))
-            got = b1_unit_in[tile]
-            units = jnp.zeros((8, 128), jnp.float32)
-            keep = along if order == 0 else across
-            for floor in range(4):
-                for line in range(2):
-                    block = floor * 2 + line
-                    spot = cell(tile, order, floor, line, True)
-                    own[spot] = own[spot] + decode(b1_in[tile, block], got[:, block : block + 1])
-                spot = cell(tile, order, floor, 1 - keep, True)
-                coded, unit = encode(own[spot])
-                b2_out[tile, floor] = coded
-                units = jnp.where(lane == floor, unit, units)
-            b2_unit_out[tile] = units
-            start_all(second_copies(pair, order))
-
-    def stage_three(pair):
-        for order in range(2):
-            tile = pair * 2 + order
-            arrive_all(second_copies(pair, order))
-            got = b2_unit_in[tile]
-            for floor in range(4):
-                spot = (tile, floor, along, across)
-                own[spot] = own[spot] + decode(b2_in[tile, floor], got[:, floor : floor + 1])
-        for j in range(3):
-            units = jnp.zeros((8, 128), jnp.float32)
-            for order in range(2):
-                tile = pair * 2 + order
-                coded, unit = encode(own[tile, (z + j + 1) % 4, along, across])
-                c_out[j, tile] = coded
-                units = jnp.where(lane == order, unit, units)
-            c_unit_out[j, pair] = units
-            start_all(tower_copies(pair, j))
-
-    def stage_four(pair):
-        for j in range(3):
-            arrive_all(tower_copies(pair, j))
-        units = jnp.zeros((8, 128), jnp.float32)
-        for order in range(2):
-            tile = pair * 2 + order
-            total = own[tile, z, along, across]
-            for j in range(3):
-                total = total + decode(c_in[j, tile], c_unit_in[j, pair][:, order : order + 1])
-            final[tile, seq] = total
-            coded, unit = encode(total)
-            d_out[tile] = coded
-            units = jnp.where(lane == order, unit, units)
-        d_unit_out[pair] = units
-        for j in range(3):
-            start_all(share_copies(pair, j))
-
-    def stage_five(pair):
-        for j in range(3):
-            arrive_all(share_copies(pair, j))
-            for order in range(2):
-                tile = pair * 2 + order
-                final[tile, side[j][1]] = decode(d_in[j, tile], d_unit_in[j, pair][:, order : order + 1])
-
-    stages = (stage_one, stage_two, stage_three, stage_four, stage_five)
-    lag = 2
-
-    def tick(step, carry):
-        for number, stage in enumerate(stages):
-            pair = step - lag * number
-
-            @pl.when(jnp.logical_and(pair >= 0, pair < pairs))
-            def _():
-                stage(pair)
-
-        return carry
-
-    lax.fori_loop(0, 4, tick, 0)
-    small_dp[dp] = small_ref[...]
-    for j in range(7):
-        small_copy(j).wait_recv()
-    total = small_dp[0]
-    for j in range(1, 8):
-        total = total + small_dp[j]
-    small_seq[seq] = total
-    for j in range(3):
-        small_side(j).start()
-    lax.fori_loop(4, pairs + lag * 4, tick, 0)
-
-    def collect(slot, square):
-        keep = valid_ref[slot] > 0
-        for quarter in range(4):
-            value = final[source_ref[slot], quarter]
-            value = jnp.where(keep, value, jnp.zeros_like(value))
-            out_ref[slot, quarter * 16 : quarter * 16 + 16, :] = value
-            square = square + value * value
-        return square
-
-    square = lax.fori_loop(0, held, collect, jnp.zeros((16, out_ref.shape[2]), jnp.float32))
-    folded = square[0:8, 0:128]
-    for r in range(2):
-        for w in range(out_ref.shape[2] // 128):
-            if r or w:
-                folded = folded + square[8 * r : 8 * r + 8, 128 * w : 128 * w + 128]
-    square_dp[dp] = folded
-    for j in range(7):
-        square_copy(j).start()
-    for j in range(3):
-        small_side(j).wait_recv()
-    small_out[...] = (small_seq[0] + small_seq[1]) + (small_seq[2] + small_seq[3])
-    for j in range(7):
-        square_copy(j).wait_recv()
-    total = square_dp[0]
-    for j in range(1, 8):
-        total = total + square_dp[j]
-    square_seq[seq] = total
-    for j in range(3):
-        square_side(j).start()
-    for j in range(3):
-        square_side(j).wait_recv()
-    square_out[...] = (square_seq[0] + square_seq[1]) + (square_seq[2] + square_seq[3])
-    for j in range(7):
-        small_copy(j).wait_send()
-        square_copy(j).wait_send()
-    for j in range(3):
-        small_side(j).wait_send()
-        square_side(j).wait_send()
-
-    def drain(pair, carry):
-        core_copy(pair).wait_send()
-        for order in range(2):
-            sent_all(first_copies(pair, order))
-            sent_all(second_copies(pair, order))
-        for j in range(3):
-            sent_all(tower_copies(pair, j))
-            sent_all(share_copies(pair, j))
-        return carry
-
-    lax.fori_loop(0, pairs, drain, 0)
-
-
-def reduce_tiles_kernel(grads, small, source, valid, held):
-    tile_count, height, width = grads.shape
-    seq_count, dp_count = lax.axis_size("seq"), lax.axis_size("dp")
-    rows = height // dp_count
-    pairs = tile_count // 2
-    dma = pltpu.SemaphoreType.DMA
-    vmem = pl.BlockSpec(memory_space=pltpu.VMEM)
-    smem = pl.BlockSpec(memory_space=pltpu.SMEM)
-
-    def buffer(*shape):
-        return pltpu.VMEM(shape, jnp.float32)
-
-    def codes(*shape):
-        return pltpu.VMEM(shape + (16, width), jnp.int16)
-
-    return pl.pallas_call(
-        reduce_kernel,
-        out_shape=(
-            jax.ShapeDtypeStruct((held, rows, width), jnp.float32),
-            jax.ShapeDtypeStruct(small.shape, jnp.float32),
-            jax.ShapeDtypeStruct((8, 128), jnp.float32),
-        ),
-        in_specs=[smem, smem, pl.BlockSpec(memory_space=pl.ANY), vmem],
-        out_specs=(vmem, vmem, vmem),
-        scratch_shapes=[
-            buffer(tile_count, 4, 2, 2, 16, width),
-            buffer(tile_count, 4, 2, 2, 16, width),
-            codes(tile_count, 8), codes(tile_count, 8),
-            codes(tile_count, 4), codes(tile_count, 4),
-            codes(3, tile_count), codes(3, tile_count),
-            codes(tile_count), codes(3, tile_count),
-            buffer(tile_count, 8, 128), buffer(tile_count, 8, 128),
-            buffer(tile_count, 8, 128), buffer(tile_count, 8, 128),
-            buffer(3, pairs, 8, 128), buffer(3, pairs, 8, 128),
-            buffer(pairs, 8, 128), buffer(3, pairs, 8, 128),
-            buffer(tile_count, 4, 16, width),
-            buffer(dp_count, *small.shape),
-            buffer(seq_count, *small.shape),
-            buffer(dp_count, 8, 128),
-            buffer(seq_count, 8, 128),
-            dma((pairs,)), dma((pairs,)), dma((pairs,)),
-            dma((tile_count, 2)), dma((tile_count, 2)), dma((tile_count, 2)), dma((tile_count, 2)),
-            dma((3, pairs, 2)), dma((3, pairs, 2)), dma((3, pairs, 2)), dma((3, pairs, 2)),
-            dma((7,)), dma((7,)), dma((3,)), dma((3,)), dma((7,)), dma((7,)), dma((3,)), dma((3,)),
-        ],
-        name="reduce_tiles",
-        compiler_params=pltpu.CompilerParams(
-            collective_id=1, has_side_effects=True, vmem_limit_bytes=VMEM_LIMIT
-        ),
-    )(source, valid, grads.reshape(tile_count, 4, 2, 2, 2, 16, width), small)
-
-
 def head_mask(shape, head):
     lane = lax.broadcasted_iota(jnp.int32, shape, 1)
     return (lane >= 64) if head else (lane < 64)
@@ -769,10 +456,10 @@
 
 
 class Block:
-    def __init__(self, length, first_tile, place, gain_row, entry, qkv, logs, attended, after, inner, leave):
-        self.length, self.tile, self.place, self.gain_row = length, first_tile, place, gain_row
+    def __init__(self, length, order, place, gain_row, entry, qkv, logs, attended, after, leave):
+        self.length, self.order, self.place, self.gain_row = length, order, place, gain_row
         self.entry, self.qkv, self.logs, self.attended = entry, qkv, logs, attended
-        self.after, self.inner, self.leave = after, inner, leave
+        self.after, self.leave = after, leave
 
 
 def attend(block, pump):
@@ -801,7 +488,7 @@
     lax.fori_loop(0, 4, pair_step, 0)
 
 
-def attend_back(block, upstream, grad_qkv, key_sum, value_sum):
+def attend_back(block, upstream, grad_qkv, key_sum, value_sum, pump):
     length = block.length
 
     def pair_step(pair, carry):
@@ -834,6 +521,7 @@
                 value_sum[0:span, :] = value_sum[0:span, :] + (values[0] + values[1])
         grad_qkv[0:length, lanes[1]] = key_sum[0:length, :].astype(jnp.bfloat16)
         grad_qkv[0:length, lanes[2]] = value_sum[0:length, :].astype(jnp.bfloat16)
+        pump(pair)
         return carry
 
     lax.fori_loop(0, 4, pair_step, 0)
@@ -845,7 +533,7 @@
     gain_ffn = gains[block.gain_row + 1 : block.gain_row + 2, :]
 
     def project(rows):
-        value = block.entry[rows, :]
+        value = block.entry(rows)
         normed = (value * root_scale(value) * gain_attn).astype(jnp.bfloat16)
         for part in range(3):
             block.qkv[rows, 512 * part : 512 * part + 512] = product(normed, matrix(place + part)).astype(
@@ -858,13 +546,12 @@
     pumps[2]()
 
     def feed(rows):
-        after = block.entry[rows, :] + product(block.attended[rows, :], matrix(place + 3))
+        after = block.entry(rows) + product(block.attended[rows, :], matrix(place + 3))
         block.after[rows, :] = after
         normed = (after * root_scale(after) * gain_ffn).astype(jnp.bfloat16)
         total = jnp.zeros_like(after)
         for part in range(4):
             inner = product(normed, matrix(place + 4 + part))
-            block.inner[rows, 512 * part : 512 * part + 512] = inner
             active = gelu_both(inner)[0].astype(jnp.bfloat16)
             total = total + product(active, matrix(place + 8 + part))
         block.leave[rows, :] = after + total
@@ -873,19 +560,21 @@
     each_block(block.length, feed)
 
 
-def block_back(block, grad, matrix, gains, gain_sums, temps, put):
-    length, tile, place = block.length, block.tile, block.place
+def block_back(block, grad, matrix, gains, gain_sums, temps, put, pumps):
+    length, order, place = block.length, block.order, block.place
     gain_attn = gains[block.gain_row : block.gain_row + 1, :]
     gain_ffn = gains[block.gain_row + 1 : block.gain_row + 2, :]
-    turned, grad_inner, branch, upstream, turned_norm, key_sum, value_sum = temps
-    grad_low, grad_qkv = branch, grad_inner
+    turned, grad_inner, branch, turned_norm, key_sum, value_sum = temps
+    grad_low, grad_qkv, upstream = branch, grad_inner, block.attended
     all_rows = pl.ds(0, length)
 
     def down(part):
         def rows_step(rows):
             low = grad[rows, :].astype(jnp.bfloat16)
             columns = pl.ds(pl.multiple_of(part * 512, 512), 512)
-            active, slope = gelu_both(block.inner[rows, columns])
+            after = block.after[rows, :]
+            normed = (after * root_scale(after) * gain_ffn).astype(jnp.bfloat16)
+            active, slope = gelu_both(product(normed, matrix(place + 4 + part)))
             turned[:, rows] = turn(active)
             grad_inner[rows, columns] = (product_nt(low, matrix(place + 8 + part)) * slope).astype(jnp.bfloat16)
 
@@ -898,7 +587,8 @@
 
     def down_step(part, carry):
         down(part)
-        put(tile + 8 + part, part, lambda half: product(turned[half, all_rows], grad_low[all_rows, :]))
+        put(order[0] + part, lambda half: product(turned[half, all_rows], grad_low[all_rows, :]))
+        pumps[0](part)
         return carry
 
     lax.fori_loop(0, 4, down_step, 0)
@@ -926,15 +616,16 @@
 
     def up_step(part, carry):
         columns = pl.ds(pl.multiple_of(part * 512, 512), 512)
-        put(tile + 4 + part, part, lambda half: product(turned_norm[half, all_rows], grad_inner[all_rows, columns]))
+        put(order[1] + part, lambda half: product(turned_norm[half, all_rows], grad_inner[all_rows, columns]))
+        pumps[1](part)
         return carry
 
     lax.fori_loop(0, 4, up_step, 0)
-    put(tile + 3, 0, lambda half: product(turned[half, all_rows], branch[all_rows, :]))
-    attend_back(block, upstream, grad_qkv, key_sum, value_sum)
+    put(order[2], lambda half: product(turned[half, all_rows], branch[all_rows, :]))
+    attend_back(block, upstream, grad_qkv, key_sum, value_sum, pumps[2])
 
     def enter(rows):
-        value = block.entry[rows, :]
+        value = block.entry(rows)
         scale = root_scale(value)
         turned_norm[:, rows] = turn(value * scale * gain_attn)
         total = jnp.zeros_like(value)
@@ -949,24 +640,327 @@
 
     def qkv_step(part, carry):
         columns = pl.ds(pl.multiple_of(part * 512, 512), 512)
-        put(tile + part, part, lambda half: product(turned_norm[half, all_rows], grad_qkv[all_rows, columns]))
+        put(order[3] + part, lambda half: product(turned_norm[half, all_rows], grad_qkv[all_rows, columns]))
         return carry
 
     lax.fori_loop(0, 3, qkv_step, 0)
 
 
+class Reducer:
+    pairs = 13
+    offsets = (1, 2, 4, 6, 8)
+    gap_first, gap = 10, 5
+    last_tick = pairs + gap + offsets[-1]
+
+    def __init__(self, place, own_far, other_far, pair_copy, beside, side, tower, refs):
+        self.dp, self.seq, self.z, self.core = place
+        self.across, self.along = self.seq % 2, self.seq // 2
+        self.own_far, self.other_far, self.pair_copy = own_far, other_far, pair_copy
+        self.beside, self.side, self.tower = beside, side, tower
+        (
+            self.own, self.other, self.one, self.two, self.three, self.final,
+            self.b1_out, self.b1_in, self.b2_out, self.b2_in, self.c_out, self.c_in, self.d_out, self.d_in,
+            self.b1_unit_out, self.b1_unit_in, self.b2_unit_out, self.b2_unit_in,
+            self.c_unit_out, self.c_unit_in, self.d_unit_out, self.d_unit_in,
+            self.l_sem, self.b1_send, self.b1_recv, self.b2_send, self.b2_recv,
+            self.c_send, self.c_recv, self.d_send, self.d_recv,
+        ) = refs[:31]
+        self.lane = lax.broadcasted_iota(jnp.int32, (8, 128), 1)
+
+    def loads(self, pair):
+        two = pl.ds(pair * 2, 2)
+        return [
+            pltpu.make_async_copy(self.own_far.at[two], self.own, self.l_sem.at[0]),
+            pltpu.make_async_copy(self.other_far.at[two], self.other, self.l_sem.at[1]),
+        ]
+
+    def first_copies(self, pair, order):
+        tile, slot, peer = pair * 2 + order, pair % 3, self.beside[order]
+        send, recv = self.b1_send, self.b1_recv
+        return [
+            remote(self.b1_out.at[slot, order], self.b1_in.at[tile], send.at[0, slot, order], recv.at[0, tile], peer),
+            remote(
+                self.b1_unit_out.at[slot, order], self.b1_unit_in.at[tile], send.at[1, slot, order], recv.at[1, tile], peer
+            ),
+        ]
+
+    def second_copies(self, pair, order):
+        tile, slot, peer = pair * 2 + order, pair % 3, self.beside[1 - order]
+        send, recv = self.b2_send, self.b2_recv
+        return [
+            remote(self.b2_out.at[slot, order], self.b2_in.at[tile], send.at[0, slot, order], recv.at[0, tile], peer),
+            remote(
+                self.b2_unit_out.at[slot, order], self.b2_unit_in.at[tile], send.at[1, slot, order], recv.at[1, tile], peer
+            ),
+        ]
+
+    def tower_copies(self, pair, j):
+        two, slot, peer = pl.ds(pair * 2, 2), pair % 3, self.tower[j]
+        send, recv = self.c_send, self.c_recv
+        return [
+            remote(self.c_out.at[slot, j], self.c_in.at[j, two], send.at[0, slot, j], recv.at[0, j, pair], peer),
+            remote(self.c_unit_out.at[slot, j], self.c_unit_in.at[j, pair], send.at[1, slot, j], recv.at[1, j, pair], peer),
+        ]
+
+    def share_copies(self, pair, j):
+        two, slot, peer = pl.ds(pair * 2, 2), pair % 3, self.side[j]
+        send, recv = self.d_send, self.d_recv
+        return [
+            remote(self.d_out.at[slot], self.d_in.at[j, two], send.at[0, slot, j], recv.at[0, j, pair], peer),
+            remote(self.d_unit_out.at[slot], self.d_unit_in.at[j, pair], send.at[1, slot, j], recv.at[1, j, pair], peer),
+        ]
+
+    def after_sends(self, pair, copies, count):
+        @pl.when(pair >= 3)
+        def _():
+            for number in range(count):
+                for copy in copies(pair - 3, number):
+                    copy.wait_send()
+
+    def load(self, pair):
+        for order in range(2):
+            self.pair_copy(pair * 2 + order).wait_recv()
+        for copy in self.loads(pair):
+            copy.start()
+
+    def send_first(self, pair):
+        for copy in self.loads(pair):
+            copy.wait()
+        self.after_sends(pair, self.first_copies, 2)
+        slot, kept = pair % 3, pair % 2
+        for order in range(2):
+
+            units = jnp.zeros((8, 128), jnp.float32)
+            for block in range(8):
+                floor, line = block // 2, block % 2
+                if order == 0:
+                    mine = (order, floor, line, self.across)
+                    away = (order, floor, line, 1 - self.across)
+                else:
+                    mine = (order, floor, self.along, line)
+                    away = (order, floor, 1 - self.along, line)
+                self.one[kept, order, block] = self.own[mine] + self.other[mine]
+                coded, unit = encode(self.own[away] + self.other[away])
+                self.b1_out[slot, order, block] = coded
+                units = jnp.where(self.lane == block, unit, units)
+            self.b1_unit_out[slot, order] = units
+            for copy in self.first_copies(pair, order):
+                copy.start()
+
+    def send_second(self, pair):
+        slot, kept = pair % 3, pair % 2
+        self.after_sends(pair, self.second_copies, 2)
+        for order in range(2):
+            for copy in self.first_copies(pair, order):
+                copy.wait_recv()
+            tile = pair * 2 + order
+            got = self.b1_unit_in[tile]
+            keep = self.along if order == 0 else self.across
+
+            units = jnp.zeros((8, 128), jnp.float32)
+            for floor in range(4):
+                stay, leave = floor * 2 + keep, floor * 2 + 1 - keep
+                even, odd = got[:, 2 * floor : 2 * floor + 1], got[:, 2 * floor + 1 : 2 * floor + 2]
+                self.two[kept, order, floor] = self.one[kept, order, stay] + decode(
+                    self.b1_in[tile, stay], jnp.where(keep == 0, even, odd)
+                )
+                coded, unit = encode(
+                    self.one[kept, order, leave] + decode(self.b1_in[tile, leave], jnp.where(keep == 0, odd, even))
+                )
+                self.b2_out[slot, order, floor] = coded
+                units = jnp.where(self.lane == floor, unit, units)
+            self.b2_unit_out[slot, order] = units
+            for copy in self.second_copies(pair, order):
+                copy.start()
+
+    def send_tower(self, pair):
+        slot, kept = pair % 3, pair % 2
+        self.after_sends(pair, self.tower_copies, 3)
+        for order in range(2):
+            for copy in self.second_copies(pair, order):
+                copy.wait_recv()
+
+        for order in range(2):
+            tile = pair * 2 + order
+            got = self.b2_unit_in[tile]
+            for floor in range(4):
+                self.two[kept, order, floor] = self.two[kept, order, floor] + decode(
+                    self.b2_in[tile, floor], got[:, floor : floor + 1]
+                )
+            self.three[kept, order] = self.two[kept, order, self.z]
+        for j in range(3):
+            units = jnp.zeros((8, 128), jnp.float32)
+            for order in range(2):
+                coded, unit = encode(self.two[kept, order, (self.z + j + 1) % 4])
+                self.c_out[slot, j, order] = coded
+                units = jnp.where(self.lane == order, unit, units)
+            self.c_unit_out[slot, j] = units
+        for j in range(3):
+            for copy in self.tower_copies(pair, j):
+                copy.start()
+
+    def send_share(self, pair):
+        slot = pair % 3
+        self.after_sends(pair, self.share_copies, 3)
+        for j in range(3):
+            for copy in self.tower_copies(pair, j):
+                copy.wait_recv()
+        units = jnp.zeros((8, 128), jnp.float32)
+        for order in range(2):
+            tile = pair * 2 + order
+            total = self.three[pair % 2, order]
+            for j in range(3):
+                total = total + decode(self.c_in[j, tile], self.c_unit_in[j, pair][:, order : order + 1])
+            self.final[tile] = total
+            coded, unit = encode(total)
+            self.d_out[slot, order] = coded
+            units = jnp.where(self.lane == order, unit, units)
+        self.d_unit_out[slot] = units
+        for j in range(3):
+            for copy in self.share_copies(pair, j):
+                copy.start()
+
+    def tick(self, number):
+        stages = (self.load, self.send_first, self.send_second, self.send_tower, self.send_share)
+        for offset, stage_of in reversed(list(zip(self.offsets, stages))):
+            turn_of = jnp.int32(number) - offset
+            late = (turn_of >= self.gap_first + self.gap).astype(jnp.int32)
+            pair = turn_of - self.gap * late
+            fits = jnp.logical_and(turn_of >= 0, pair < self.pairs)
+            fits = jnp.logical_and(fits, jnp.logical_or(late > 0, turn_of < self.gap_first))
+
+            @pl.when(fits)
+            def _():
+                stage_of(pair)
+
+    def ticks(self, start, stop):
+        def body(number, carry):
+            self.tick(number)
+            return carry
+
+        lax.fori_loop(start, stop, body, 0)
+
+    def collect(self, source_ref, parity_ref, owned_ref, stage):
+        def arrive(pair, carry):
+            for j in range(3):
+                for copy in self.share_copies(pair, j):
+                    copy.wait_recv()
+            return carry
+
+        lax.fori_loop(0, self.pairs, arrive, 0)
+        for order in range(self.pairs * 2 - 4, self.pairs * 2):
+            self.pair_copy(order).wait_send()
+        width = self.final.shape[2]
+
+        def step(slot, square):
+            keep = owned_ref[slot] > 0
+            tile = source_ref[slot]
+            places_of = [self.seq] + [peer[1] for peer in self.side]
+            for number, quarter in enumerate(places_of):
+                if number == 0:
+                    value = self.final[tile]
+                else:
+                    units = self.d_unit_in[number - 1, parity_ref[slot]]
+                    unit = jnp.where(parity_ref[slot + 16] > 0, units[:, 1:2], units[:, 0:1])
+                    value = decode(self.d_in[number - 1, tile], unit)
+                value = jnp.where(keep, value, jnp.zeros_like(value))
+                stage[slot // 8, slot % 8 // 2, slot % 2, quarter // 2, quarter % 2] = value
+                square = square + value * value
+            return square
+
+        square = lax.fori_loop(0, source_ref.shape[0], step, jnp.zeros((16, width), jnp.float32))
+        folded = jnp.zeros((8, 128), jnp.float32)
+        for r in range(2):
+            for w in range(width // 128):
+                folded = folded + square[8 * r : 8 * r + 8, 128 * w : 128 * w + 128]
+        return folded
+
+    def finish(self):
+        for pair in range(self.pairs - 3, self.pairs):
+            for order in range(2):
+                for copy in self.first_copies(pair, order) + self.second_copies(pair, order):
+                    copy.wait_send()
+            for j in range(3):
+                for copy in self.tower_copies(pair, j) + self.share_copies(pair, j):
+                    copy.wait_send()
+
+
+class Sums:
+    def __init__(self, place, column, side, small, small_out, square_out, refs):
+        self.dp, self.seq, _, _ = place
+        self.column, self.side = column, side
+        self.small, self.small_out, self.square_out = small, small_out, square_out
+        self.small_dp, self.small_seq, self.square_dp, self.square_seq, self.sems = refs[31:]
+
+    def copies(self, which):
+        sends, recvs = self.sems[2 * which], self.sems[2 * which + 1]
+        if which == 0:
+            return [remote(self.small, self.small_dp.at[self.dp], sends.at[j], recvs.at[j], self.column[j]) for j in range(7)]
+        if which == 1:
+            spot = self.small_seq.at[self.seq]
+            return [remote(spot, spot, sends.at[j], recvs.at[j], self.side[j]) for j in range(3)]
+        if which == 2:
+            spot = self.square_dp.at[self.dp]
+            return [remote(spot, spot, sends.at[j], recvs.at[j], self.column[j]) for j in range(7)]
+        spot = self.square_seq.at[self.seq]
+        return [remote(spot, spot, sends.at[j], recvs.at[j], self.side[j]) for j in range(3)]
+
+    def start(self, which):
+        for copy in self.copies(which):
+            copy.start()
+
+    def arrive(self, which):
+        for copy in self.copies(which):
+            copy.wait_recv()
+
+    def start_small(self):
+        self.start(0)
+        self.small_dp[self.dp] = self.small[...]
+
+    def pass_small(self):
+        self.arrive(0)
+        total = self.small_dp[0]
+        for j in range(1, 8):
+            total = total + self.small_dp[j]
+        self.small_seq[self.seq] = total
+        self.start(1)
+
+    def squares(self, folded):
+        self.square_dp[self.dp] = folded
+        self.start(2)
+        self.arrive(1)
+        self.small_out[...] = (self.small_seq[0] + self.small_seq[1]) + (self.small_seq[2] + self.small_seq[3])
+        self.arrive(2)
+        total = self.square_dp[0]
+        for j in range(1, 8):
+            total = total + self.square_dp[j]
+        self.square_seq[self.seq] = total
+        self.start(3)
+        self.arrive(3)
+        self.square_out[...] = (self.square_seq[0] + self.square_seq[1]) + (self.square_seq[2] + self.square_seq[3])
+
+    def finish(self):
+        for which in range(4):
+            for copy in self.copies(which):
+                copy.wait_send()
+
+
+GRAD_ORDER = (20, 21, 22, 23, 16, 17, 18, 19, 15, 12, 13, 14, 24, 8, 9, 10, 11, 4, 5, 6, 7, 3, 0, 1, 2, 25)
+
+
 def step_kernel(
-    micro_count, length_ref, local_ref, valid_ref, master_ref, ids_ref, gains_ref, grads_ref, small_ref,
-    weights, entry, qkv, logs, attended, after, inner, leave, grad,
-    seg_entry, seg_qkv, seg_logs, seg_attended, seg_after, seg_inner, seg_leave, seg_grad,
-    turned, grad_inner, branch, upstream, turned_norm, key_sum, value_sum,
-    ids_row, ids_col, stage, stage_sem, counts, count_send, count_recv, i_send, i_recv, i_own,
+    micro_count, length_ref, local_ref, valid_ref, source_ref, parity_ref, owned_ref, master_ref, ids_ref, gains_ref,
+    own_far, other_far, out_ref, small_out, square_out,
+    weights, qkv, logs, attended, after, leave, grad,
+    seg_entry, seg_qkv, seg_logs, seg_attended, seg_after, seg_leave, seg_grad,
+    turned, grad_inner, branch, turned_norm, key_sum, value_sum, head_grad, small_ref,
+    ids_row, ids_col, stage, stage_sem, counts, count_send, count_recv, i_send, i_recv, i_own, g_send, g_recv, out_sem,
     p_send, p_recv, z_send, z_recv, s_send, s_recv, d_send, d_recv, c_send, c_recv,
+    reduce_refs,
 ):
     dp, seq, z, core = places()
     across, along = seq % 2, seq // 2
-    length = entry.shape[0]
-    width = entry.shape[1]
+    length, width = leave.shape
     segments = seg_entry.shape[0]
     vocab = width // 2
     root_width = width ** (-0.5)
@@ -1094,14 +1088,28 @@
     def count_copy(j):
         return remote(counts.at[dp], counts.at[dp], count_send.at[j], count_recv.at[j], column[j])
 
-    def staged(tile, slot):
-        return pltpu.make_async_copy(stage.at[slot], grads_ref.at[tile], stage_sem.at[slot])
-
-    def put(tile, slot, half_of):
-        staged(tile, slot).wait()
+    def own_copy(order):
+        return pltpu.make_async_copy(stage.at[order % 4, :, core], own_far.at[order], stage_sem.at[order % 2])
+
+    def pair_copy(order):
+        return remote(
+            stage.at[order % 4, :, 1 - core], other_far.at[order], g_send.at[order % 4], g_recv.at[order], sibling
+        )
+
+    def put(order, half_of):
+        @pl.when(jnp.int32(order) >= 4)
+        def _():
+            pair_copy(order - 4).wait_send()
+
+        @pl.when(jnp.int32(order) >= 1)
+        def _():
+            own_copy(order - 1).wait()
+
         for half in range(2):
-            stage[slot, 256 * half : 256 * half + 256, :] = half_of(pl.ds(256 * half, 256))
-        staged(tile, slot).start()
+            value = half_of(pl.ds(256 * half, 256))
+            stage[order % 4, 2 * half : 2 * half + 2] = value.reshape(2, 2, 2, 2, 16, width)
+        own_copy(order).start()
+        pair_copy(order).start()
 
     small_ref[...] = jnp.zeros_like(small_ref)
     own_ids().wait()
@@ -1109,11 +1117,7 @@
         ids_copy(j).wait_recv()
     ids_col[...] = ids_row[...].astype(jnp.float32).T
     length_one = length_ref[0]
-    char = Block(length, 0, 1, 0, entry, qkv, logs, attended, after, inner, leave)
-    seg = Block(
-        segments, 12, 14, 2, seg_entry, seg_qkv, seg_logs, seg_attended, seg_after, seg_inner, seg_leave
-    )
-    temps = (turned, grad_inner, branch, upstream, turned_norm, key_sum, value_sum)
+    temps = (turned, grad_inner, branch, turned_norm, key_sum, value_sum)
 
     def hot_rows(rows, which, offset, count):
         ids = ids_col[rows, which : which + 1] + float(offset)
@@ -1128,9 +1132,13 @@
     arrived(0, 2)
 
     def embed(rows):
-        entry[rows, :] = product(hot_rows(rows, 0, 0, vocab), matrix_half(0))
-
-    each_block(length, embed)
+        return product(hot_rows(rows, 0, 0, vocab), matrix_half(0))
+
+    char = Block(length, (13, 17, 21, 22), 1, 0, embed, qkv, logs, attended, after, leave)
+    seg = Block(
+        segments, (0, 4, 8, 9), 14, 2, lambda rows: seg_entry[rows, :],
+        seg_qkv, seg_logs, seg_attended, seg_after, seg_leave,
+    )
     tick(START)
     block_run(
         char,
@@ -1207,9 +1215,7 @@
     ce_local, head_sum = lax.fori_loop(
         0, length // ROWS, head, (jnp.zeros((1, 1), jnp.float32), jnp.zeros((vocab, width), jnp.float32))
     )
-    stage[...] = jnp.zeros_like(stage)
-    for slot in range(4):
-        staged(slot, slot).start()
+    head_grad[...] = head_sum
     seg_grad[...] = exact_product(hot_turned(2, 0, segments).astype(jnp.bfloat16), grad[...])
     def sent(group, carry):
         for j in range(3):
@@ -1222,7 +1228,13 @@
         return carry
 
     lax.fori_loop(0, groups, sent, 0)
-    block_back(seg, seg_grad, matrix, gains_ref, small_ref, temps, put)
+    reducer = Reducer(
+        places(), own_far, other_far, pair_copy, [(dp, peer) for peer in beside], [(dp, peer) for peer in side], tower, reduce_refs
+    )
+    block_back(
+        seg, seg_grad, matrix, gains_ref, small_ref, temps, put,
+        (lambda part: None, lambda part: reducer.tick(part), lambda pair: None),
+    )
     seg_grad[...] = seg_grad[...] / divisor
 
     count_rest = count_all - soft_count
@@ -1240,12 +1252,18 @@
         grad[rows, :] = (grad[rows, :] + spread) + product_nt(pre, matrix(13))
 
     each_block(length, join)
-    put(24, 0, lambda half: product(turned[half, :], branch[...]))
-    block_back(char, grad, matrix, gains_ref, small_ref, temps, put)
-    staged(25, 3).wait()
-    stage[3, 0:vocab, :] = exact_product(hot_turned(0, 0, vocab).astype(jnp.bfloat16), grad[...])
-    stage[3, vocab : 2 * vocab, :] = head_sum
-    staged(25, 3).start()
+    put(12, lambda half: product(turned[half, :], branch[...]))
+    block_back(
+        char, grad, matrix, gains_ref, small_ref, temps, put,
+        (
+            lambda part: reducer.tick(4 + part),
+            lambda part: None,
+            lambda pair: reducer.ticks(8 + 2 * pair, 10 + 2 * pair),
+        ),
+    )
+    embed_grad = exact_product(hot_turned(0, 0, vocab).astype(jnp.bfloat16), grad[...])
+    put(25, lambda half: embed_grad if half.start == 0 else head_grad[...])
+    own_copy(25).wait()
 
     lane = lax.broadcasted_iota(jnp.int32, (1, width), 1)
     small_ref[6:7, :] = jnp.where(
@@ -1253,16 +1271,31 @@
         ce_local,
         jnp.where(lane == seq + 8, soft_local, jnp.where(lane == seq + 16, length_float, 0.0)),
     )
-    for slot in range(4):
-        staged(slot, slot).wait()
     for j in range(7):
         count_copy(j).wait_send()
     for j in range(3):
         ids_copy(j).wait_send()
+    sums = Sums(places(), column, [(dp, peer) for peer in side], small_ref, small_out, square_out, reduce_refs)
+    sums.start_small()
+    reducer.ticks(16, reducer.last_tick)
+    sums.pass_small()
+    square = reducer.collect(source_ref, parity_ref, owned_ref, stage)
+    held = out_ref.shape[0]
+    for slot in range(held):
+        pltpu.make_async_copy(
+            stage.at[slot // 8, slot % 8 // 2, slot % 2], out_ref.at[slot], out_sem.at[slot]
+        ).start()
+    sums.squares(square)
+    for slot in range(held):
+        pltpu.make_async_copy(
+            stage.at[slot // 8, slot % 8 // 2, slot % 2], out_ref.at[slot], out_sem.at[slot]
+        ).wait()
+    sums.finish()
+    reducer.finish()
 
 
 def step_call(length_one, owner_slot, master, ids, gains, micro_count):
-    held, _, width = master.shape
+    held, rows, width = master.shape
     tile_count = owner_slot.shape[0]
     seq_count, dp_count = lax.axis_size("seq"), lax.axis_size("dp")
     groups = tile_count // 2
@@ -1272,9 +1305,16 @@
     vmem = pl.BlockSpec(memory_space=pltpu.VMEM)
     smem = pl.BlockSpec(memory_space=pltpu.SMEM)
     hbm = pl.BlockSpec(memory_space=pl.ANY)
-    local = jnp.concatenate([owner_slot[25:], owner_slot[:12], owner_slot[24:25], owner_slot[12:24]])
-    local = local - lax.axis_index("seq") * held
+    local = owner_slot - lax.axis_index("seq") * held
     valid = jnp.logical_and(local >= 0, local < held).astype(jnp.int32)
+    hot = jnp.arange(held)[:, None] == jnp.take(local, jnp.array(GRAD_ORDER))[None, :]
+    source = jnp.sum(jnp.where(hot, jnp.arange(tile_count)[None, :], 0), axis=1)
+    owned = jnp.any(hot, axis=1).astype(jnp.int32)
+    parity = jnp.concatenate([jnp.pad(source // 2, (0, 16 - held)), source % 2])
+    local = jnp.where(valid > 0, local, 0)
+
+    def used(values):
+        return jnp.concatenate([values[25:], values[:12], values[24:25], values[12:24]])
 
     def full(*shape):
         return pltpu.VMEM(shape, jnp.float32)
@@ -1282,37 +1322,57 @@
     def half(*shape):
         return pltpu.VMEM(shape, jnp.bfloat16)
 
+    def codes(*shape):
+        return pltpu.VMEM(shape + (16, width), jnp.int16)
+
     def kept(count):
         return [
-            full(count, width), half(count, 3 * width), full(4, 2, count), half(count, width),
-            full(count, width), full(count, 4 * width), full(count, width), full(count, width),
+            half(count, 3 * width), full(4, 2, count), half(count, width), full(count, width),
+            full(count, width), full(count, width),
         ]
 
+    reduce_refs = [
+        full(2, 4, 2, 2, 16, width), full(2, 4, 2, 2, 16, width),
+        full(2, 2, 8, 16, width), full(2, 2, 4, 16, width), full(2, 2, 16, width), full(tile_count, 16, width),
+        codes(3, 2, 8), codes(tile_count, 8), codes(3, 2, 4), codes(tile_count, 4),
+        codes(3, 3, 2), codes(3, tile_count), codes(3, 2), codes(3, tile_count),
+        full(3, 2, 8, 128), full(tile_count, 8, 128), full(3, 2, 8, 128), full(tile_count, 8, 128),
+        full(3, 3, 8, 128), full(3, groups, 8, 128), full(3, 8, 128), full(3, groups, 8, 128),
+        dma((2,)), dma((2, 3, 2)), dma((2, tile_count)), dma((2, 3, 2)), dma((2, tile_count)),
+        dma((2, 3, 3)), dma((2, 3, groups)), dma((2, 3, 3)), dma((2, 3, groups)),
+        full(dp_count, 8, width), full(seq_count, 8, width), full(dp_count, 8, 128), full(seq_count, 8, 128),
+        [dma((7,)), dma((7,)), dma((3,)), dma((3,)), dma((7,)), dma((7,)), dma((3,)), dma((3,))],
+    ]
     return pl.pallas_call(
         functools.partial(step_kernel, micro_count),
         out_shape=(
-            jax.ShapeDtypeStruct((tile_count, width, width), jnp.float32),
+            jax.ShapeDtypeStruct((tile_count, 4, 2, 2, 16, width), jnp.float32),
+            jax.ShapeDtypeStruct((tile_count, 4, 2, 2, 16, width), jnp.float32),
+            jax.ShapeDtypeStruct((held, 2, 2, 16, width), jnp.float32),
             jax.ShapeDtypeStruct((8, width), jnp.float32),
+            jax.ShapeDtypeStruct((8, 128), jnp.float32),
         ),
-        in_specs=[smem, smem, smem, vmem, vmem, vmem],
-        out_specs=(hbm, vmem),
+        in_specs=[smem] * 6 + [vmem] * 3,
+        out_specs=(hbm, hbm, hbm, vmem, vmem),
         scratch_shapes=[half(tile_count, 4, 2, 4, 16, width)]
         + kept(length)
+        + [full(segments, width)]
         + kept(segments)
         + [
-            half(width, length), half(length, 4 * width), half(length, width), half(length, width),
-            half(width, length), full(length, 128), full(length, 128),
-            pltpu.VMEM((8, length), jnp.int32), full(length, 8), full(4, width, width), dma((4,)),
+            half(width, length), half(length, 4 * width), half(length, width), half(width, length),
+            full(length, 128), full(length, 128), full(width // 2, width), full(8, width),
+            pltpu.VMEM((8, length), jnp.int32), full(length, 8), full(4, 4, 2, 2, 2, 16, width), dma((2,)),
             full(dp_count, 8, 128), dma((7,)), dma((7,)), dma((3,)), dma((3,)), dma,
+            dma((4,)), dma((tile_count,)), dma((held,)),
             dma((3, groups)), dma((3, groups)), dma((3, groups)), dma((3, groups)),
             dma((2, groups)), dma((2, groups)), dma((2, groups)), dma((2, groups)),
-            dma((groups,)), dma((groups,)),
+            dma((groups,)), dma((groups,)), reduce_refs,
         ],
         name="step",
         compiler_params=pltpu.CompilerParams(
             collective_id=2, has_side_effects=True, vmem_limit_bytes=STEP_VMEM
         ),
-    )(length_one, jnp.where(valid > 0, local, 0), valid, master, ids, gains)
+    )(length_one, used(local), used(valid), source, parity, owned, master, ids, gains)[2:]
 
 
 def whole_step(char_ids, targets, seg_ids, lengths, owner_slot, master, gain_rows):
@@ -1342,16 +1402,10 @@
     model_width = master.shape[2]
     slot_count = master.shape[0] * lax.axis_size("seq")
     if (micro_count, lax.axis_size("seq"), lax.axis_size("dp")) == (4, 4, 8):
-        tile_grads, small = whole_step(
+        shard_total, small, squares = whole_step(
             char_ids, targets, seg_ids, lengths, owner_slot, master, gain_rows
         )
-        local = lax.axis_index("seq") * master.shape[0] + jnp.arange(master.shape[0])
-        hot = local[:, None] == owner_slot[None, :]
-        valid = jnp.any(hot, axis=1).astype(jnp.int32)
-        source = jnp.sum(jnp.where(hot, jnp.arange(owner_slot.shape[0])[None, :], 0), axis=1)
-        shard_total, small, squares = reduce_tiles_kernel(
-            tile_grads, small, source, valid, master.shape[0]
-        )
+        shard_total = shard_total.reshape(master.shape)
         gain_sum, square_sum = small[0:6], jnp.sum(squares)
         entropy, soft, count = (small[6, 8 * i : 8 * i + micro_count] for i in range(3))
         prior = -(

time: 298 us -> 277 us (0.930)
  Pallas kernels: 271 us -> 247 us
  other arithmetic: 15.3 us -> 18.6 us
    pallas_call x1 -> x0, Pallas kernels: 104 us -> none  [reduce_tiles_kernel(): pl.pallas_call(reduce_kernel, out_shape=(jax.ShapeDtypeStruct((held, rows...]
    pallas_call x1, Pallas kernels: 167 us -> 247 us  [step_call(): pl.pallas_call(functools.partial(step_kernel, micro_count), out_shape=(ja...]
    concatenate x0 -> x2, other arithmetic: none -> 3.76 us  [the longest x1 1.88 us: step_call(): parity = jnp.concatenate([jnp.pad(source // 2, (0, 16 - held)), source % 2])]
where the time goes in v5:
time: 277 us; the launch traced here: 276 us
  Pallas kernels  247 us (89%)
  other arithmetic  18.6 us (7%)
  between operations  5.79 us (2%)
  local copies, waits for them, and re-layouts  4.86 us (2%)
    pallas_call x1, Pallas kernels, step_call(): pl.pallas_call(functools.partial(step_kernel, micro_count), out_shape=(ja...  247 us

profile of v5, /device:TPU:0, one launch (start us, length us, event | category | flops | bytes accessed | tf_op | source)
XLA Modules:
  0.0 276.2 jit_solution(11249995942553229759)
XLA Ops:
  0.6 0.0 copy-start
  0.7 0.0 copy-start.3
  0.7 0.0 copy-start.5
  0.7 0.0 copy-start.4
  0.7 0.7 and_convert_fusion
  1.4 0.7 pad_clamp_fusion
  2.0 0.7 gather_fusion
  2.7 0.1 select_reduce_fusion.source_ref
  2.8 0.0 copy-start.6
  2.9 0.6 fusion.25
  3.5 0.1 fusion.26
  3.5 1.9 pad_add_fusion.1
  5.4 0.6 fusion.23
  6.0 0.1 fusion.24
  6.1 1.9 pad_add_fusion.3.valid_ref
  8.0 0.0 copy-done
  8.0 0.6 constant_dynamic-slice_fusion
  8.5 0.1 fusion.5
  8.7 0.5 convert_element_type.16.owned_ref
  9.2 0.7 pad_add_fusion
  9.9 0.6 pad.13.ids_ref
  10.5 1.3 pad.14.gains_ref
  11.9 0.0 copy-done.6
  11.9 246.9 %step.1 = (f32[26,4,2,2,16,512]{5,4,3,2,1,0:T(8,128)}, f32[26,4,2,2,16,512]{5,4,3,2,1,0:T(8,128)}, f32[10,2,2,16,512]{4,3,2,1,0:T(8,128)}, f32[8,512]{1,0:T(8,128)}, f32[8,128]{1,0:T(8,128)}) custom-call(s32[1]{0:T(128)} %bitcast.length_ref, s32[26]{0:T(128)} %get-tuple-element.35.local_ref, s32[26]{0:T(128)} %pad_add_fusion.3.valid_ref, s32[10]{0:T(128)} %copy-done.6, ...), custom_call_target="tpu_custom_call" | custom-call | tf_op jit(solution)/shard_map/step/pallas_call | solution.py:1346
  258.8 1.3 multiply_reduce_fusion
  260.1 1.3 reduce_sum.38
  263.5 0.0 copy-done.3
  263.5 0.0 copy-done.5
  263.6 0.0 copy-done.4
  263.6 1.4 multiply_subtract_fusion
  264.9 0.0 copy-start.7
  264.9 0.0 copy-start.1
  264.9 0.0 copy-start.2
  264.9 1.6 broadcast_multiply_fusion
  266.6 0.0 copy-done.7
  266.6 0.2 compare_reduce_fusion
  266.8 0.0 copy-done.1
  266.8 0.3 copy-done.2
  267.0 4.7 %fusion.22 = (bf16[10,64,512]{2,1,0:T(8,128)(2,1)}, f32[10,64,512]{2,1,0:T(8,128)}, f32[10,64,512]{2,1,0:T(8,128)}, f32[10,64,512]{2,1,0:T(8,128)}) fusion(f32[10,64,512]{2,1,0:T(8,128)S(1)} %copy-done.1, f32[]{:T(128)} %bitcast.8, f32[10,64,512]{2,1,0:T(8,128)S(1)} %copy-done.2, f32[]{:T(128)} %bitcast.7, ...), kind=kLoop, calls=%fused_computation.93 | loop fusion | flops 6225920 | bytes 9830418 | tf_op jit(solution)/shard_map/convert_element_type | solution.py:1465
  271.8 1.6 fusion.20
  (3 shorter events, 0.0 us)
Async XLA Ops:
  0.6 7.3 %copy-start = (s32[4,1]{0,1:T(1,128)S(1)}, s32[4,1]{0,1:T(1,128)}, u32[]{:S(2)}) copy-start(s32[4,1]{0,1:T(1,128)} %param.16) | copy-start | bytes 52
  0.7 262.9 %copy-start.3 = (f32[6,512]{1,0:T(8,128)S(1)}, f32[6,512]{1,0:T(8,128)}, u32[]{:S(2)}) copy-start(f32[6,512]{1,0:T(8,128)} %param.22) | copy-start | bytes 36868
  0.7 262.9 %copy-start.5 = (f32[6,512]{1,0:T(8,128)S(1)}, f32[6,512]{1,0:T(8,128)}, u32[]{:S(2)}) copy-start(f32[6,512]{1,0:T(8,128)} %param.23) | copy-start | bytes 36868
  0.7 262.9 %copy-start.4 = (f32[6,512]{1,0:T(8,128)S(1)}, f32[6,512]{1,0:T(8,128)}, u32[]{:S(2)}) copy-start(f32[6,512]{1,0:T(8,128)} %param.24) | copy-start | bytes 36868
  2.8 9.0 %copy-start.6 = (s32[10]{0:T(128)}, s32[10]{0:T(128)S(1)}, u32[]{:S(2)}) copy-start(s32[10]{0:T(128)S(1)} %select_reduce_fusion.source_ref) | copy-start | bytes 124
  264.9 1.6 copy-start.7
  264.9 1.8 copy-start.1
  264.9 2.1 copy-start.2

commit v6 on v5

--- a/solution.py
+++ b/solution.py
@@ -445,6 +445,17 @@
     for number in range(8):
         total = total - 1.0 / (value + float(number))
     return total
+
+
+def log_gamma(value):
+    moved = value + 8.0
+    inverse = 1.0 / moved
+    square = inverse * inverse
+    series = inverse * (1.0 / 12.0 - square * (1.0 / 360.0 - square * (1.0 / 1260.0)))
+    gone = value
+    for number in range(1, 8):
+        gone = gone * (value + float(number))
+    return ((moved - 0.5) * jnp.log(moved) - moved) + (0.9189385332046727 + series) - jnp.log(gone)
 
 
 def each_block(length, body):
@@ -622,6 +633,7 @@
 
     lax.fori_loop(0, 4, up_step, 0)
     put(order[2], lambda half: product(turned[half, all_rows], branch[all_rows, :]))
+    pumps[3]()
     attend_back(block, upstream, grad_qkv, key_sum, value_sum, pumps[2])
 
     def enter(rows):
@@ -646,11 +658,15 @@
     lax.fori_loop(0, 3, qkv_step, 0)
 
 
+def total_of(value):
+    return jnp.sum(jnp.sum(value, axis=1, keepdims=True), axis=0, keepdims=True)
+
+
 class Reducer:
     pairs = 13
     offsets = (1, 2, 4, 6, 8)
-    gap_first, gap = 10, 5
-    last_tick = pairs + gap + offsets[-1]
+    gaps = ((11, 4),)
+    last_tick = pairs + sum(count for _, count in gaps) + offsets[-1]
 
     def __init__(self, place, own_far, other_far, pair_copy, beside, side, tower, refs):
         self.dp, self.seq, self.z, self.core = place
@@ -824,10 +840,12 @@
         stages = (self.load, self.send_first, self.send_second, self.send_tower, self.send_share)
         for offset, stage_of in reversed(list(zip(self.offsets, stages))):
             turn_of = jnp.int32(number) - offset
-            late = (turn_of >= self.gap_first + self.gap).astype(jnp.int32)
-            pair = turn_of - self.gap * late
-            fits = jnp.logical_and(turn_of >= 0, pair < self.pairs)
-            fits = jnp.logical_and(fits, jnp.logical_or(late > 0, turn_of < self.gap_first))
+            pair = turn_of
+            fits = turn_of >= 0
+            for first, count in self.gaps:
+                pair = pair - jnp.minimum(jnp.maximum(turn_of - first + 1, 0), count)
+                fits = jnp.logical_and(fits, jnp.logical_or(turn_of < first, turn_of >= first + count))
+            fits = jnp.logical_and(fits, pair < self.pairs)
 
             @pl.when(fits)
             def _():
@@ -840,7 +858,7 @@
 
         lax.fori_loop(start, stop, body, 0)
 
-    def collect(self, source_ref, parity_ref, owned_ref, stage):
+    def collect(self, source_ref, pair_ref, parity_ref, owned_ref, stage):
         def arrive(pair, carry):
             for j in range(3):
                 for copy in self.share_copies(pair, j):
@@ -860,8 +878,8 @@
                 if number == 0:
                     value = self.final[tile]
                 else:
-                    units = self.d_unit_in[number - 1, parity_ref[slot]]
-                    unit = jnp.where(parity_ref[slot + 16] > 0, units[:, 1:2], units[:, 0:1])
+                    units = self.d_unit_in[number - 1, pair_ref[slot]]
+                    unit = jnp.where(parity_ref[slot] > 0, units[:, 1:2], units[:, 0:1])
                     value = decode(self.d_in[number - 1, tile], unit)
                 value = jnp.where(keep, value, jnp.zeros_like(value))
                 stage[slot // 8, slot % 8 // 2, slot % 2, quarter // 2, quarter % 2] = value
@@ -886,10 +904,10 @@
 
 
 class Sums:
-    def __init__(self, place, column, side, small, small_out, square_out, refs):
+    def __init__(self, place, column, side, small, refs):
         self.dp, self.seq, _, _ = place
         self.column, self.side = column, side
-        self.small, self.small_out, self.square_out = small, small_out, square_out
+        self.small = small
         self.small_dp, self.small_seq, self.square_dp, self.square_seq, self.sems = refs[31:]
 
     def copies(self, which):
@@ -929,7 +947,7 @@
         self.square_dp[self.dp] = folded
         self.start(2)
         self.arrive(1)
-        self.small_out[...] = (self.small_seq[0] + self.small_seq[1]) + (self.small_seq[2] + self.small_seq[3])
+        small = (self.small_seq[0] + self.small_seq[1]) + (self.small_seq[2] + self.small_seq[3])
         self.arrive(2)
         total = self.square_dp[0]
         for j in range(1, 8):
@@ -937,7 +955,7 @@
         self.square_seq[self.seq] = total
         self.start(3)
         self.arrive(3)
-        self.square_out[...] = (self.square_seq[0] + self.square_seq[1]) + (self.square_seq[2] + self.square_seq[3])
+        return small, (self.square_seq[0] + self.square_seq[1]) + (self.square_seq[2] + self.square_seq[3])
 
     def finish(self):
         for which in range(4):
@@ -949,12 +967,14 @@
 
 
 def step_kernel(
-    micro_count, length_ref, local_ref, valid_ref, source_ref, parity_ref, owned_ref, master_ref, ids_ref, gains_ref,
-    own_far, other_far, out_ref, small_out, square_out,
+    micro_count, lengths_ref, owner_ref, step_ref, master_ref, chars_ref, targets_ref, segs_ref,
+    gains_ref, gain_first_ref, gain_second_ref, first_far, second_far,
+    own_far, other_far, master_out, first_out, second_out, low_out, gains_out, gain_first_out, gain_second_out,
+    loss_out, norm_out,
     weights, qkv, logs, attended, after, leave, grad,
     seg_entry, seg_qkv, seg_logs, seg_attended, seg_after, seg_leave, seg_grad,
     turned, grad_inner, branch, turned_norm, key_sum, value_sum, head_grad, small_ref,
-    ids_row, ids_col, stage, stage_sem, counts, count_send, count_recv, i_send, i_recv, i_own, g_send, g_recv, out_sem,
+    ids_in, ids_row, ids_col, source_ref, pair_ref, parity_ref, owned_ref, stage, stage_sem, counts, count_send, count_recv, i_send, i_recv, g_send, g_recv, out_sem, m_sem,
     p_send, p_recv, z_send, z_recv, s_send, s_recv, d_send, d_recv, c_send, c_recv,
     reduce_refs,
 ):
@@ -972,13 +992,12 @@
     tower = [((z + j) % 4 * 2 + core, seq) for j in (1, 2, 3)]
     meet([(dp, peer) for peer in side] + column)
 
-    def ids_copy(j):
-        part = pl.ds(pl.multiple_of(seq * ids_ref.shape[2], 256), ids_ref.shape[2])
-        return remote(ids_ref.at[side[j]], ids_row.at[:, part], i_send.at[j], i_recv.at[j], (dp, side[j]))
-
-    def own_ids():
-        part = pl.ds(pl.multiple_of(seq * ids_ref.shape[2], 256), ids_ref.shape[2])
-        return pltpu.make_async_copy(ids_ref.at[seq], ids_row.at[:, part], i_own)
+    all_ids = (chars_ref, targets_ref, segs_ref)
+
+    def ids_copy(j, which):
+        return remote(
+            all_ids[which].at[side[j]], ids_in.at[which, seq], i_send.at[j, which], i_recv.at[j, which], (dp, side[j])
+        )
 
     def part_of(which):
         return pl.ds(pl.multiple_of(which * width, width), width)
@@ -1063,13 +1082,20 @@
 
         lax.fori_loop(first, last, body, 0)
 
-    for j in range(3):
-        ids_copy(j).start()
-    own_ids().start()
+    for which in range(3):
+        ids_in[which, seq] = all_ids[which][seq]
+        for j in range(3):
+            ids_copy(j, which).start()
+
+    held = master_ref.shape[0]
 
     def pick(place, carry):
-        value = master_ref[local_ref[place]]
-        value = jnp.where(valid_ref[place] > 0, value, jnp.zeros_like(value)).astype(jnp.bfloat16)
+        late = (place > 13).astype(jnp.int32)
+        tile = jnp.where(place == 0, 25, jnp.where(place == 13, 24, place - 1 - late))
+        slot = owner_ref[tile] - held * seq
+        keep = jnp.logical_and(slot >= 0, slot < held)
+        value = master_ref[jnp.minimum(jnp.maximum(slot, 0), held - 1)]
+        value = jnp.where(keep, value, jnp.zeros_like(value)).astype(jnp.bfloat16)
         for quarter in range(4):
             grad_inner[pl.ds(pl.multiple_of(place * 16, 16), 16), quarter * width : quarter * width + width] = value[
                 16 * quarter : 16 * quarter + 16
@@ -1101,7 +1127,7 @@
         def _():
             pair_copy(order - 4).wait_send()
 
-        @pl.when(jnp.int32(order) >= 1)
+        @pl.when(jnp.logical_and(jnp.int32(order) >= 1, jnp.int32(order) != 22))
         def _():
             own_copy(order - 1).wait()
 
@@ -1112,11 +1138,24 @@
         pair_copy(order).start()
 
     small_ref[...] = jnp.zeros_like(small_ref)
-    own_ids().wait()
-    for j in range(3):
-        ids_copy(j).wait_recv()
+    for which in range(3):
+        for j in range(3):
+            ids_copy(j, which).wait_recv()
+        for peer in range(4):
+            ids_row[which : which + 1, 256 * peer : 256 * peer + 256] = ids_in[which, peer]
+    for slot in range(held):
+        zero = jnp.int32(0)
+        source, pair, parity, owned = zero, zero, zero, zero
+        for order, tile in enumerate(GRAD_ORDER):
+            here = (owner_ref[tile] == held * seq + slot).astype(jnp.int32)
+            source, pair, parity = source + here * order, pair + here * (order // 2), parity + here * (order % 2)
+            owned = owned + here
+        source_ref[slot] = jnp.minimum(source, 2 * groups - 1)
+        pair_ref[slot] = jnp.minimum(pair, groups - 1)
+        parity_ref[slot], owned_ref[slot] = parity, owned
+    ids_row[3:8, :] = jnp.zeros((5, length), jnp.int32)
     ids_col[...] = ids_row[...].astype(jnp.float32).T
-    length_one = length_ref[0]
+    length_one = lengths_ref[seq, 0]
     temps = (turned, grad_inner, branch, turned_norm, key_sum, value_sum)
 
     def hot_rows(rows, which, offset, count):
@@ -1233,8 +1272,9 @@
     )
     block_back(
         seg, seg_grad, matrix, gains_ref, small_ref, temps, put,
-        (lambda part: None, lambda part: reducer.tick(part), lambda pair: None),
-    )
+        (lambda part: None, lambda part: reducer.tick(part), lambda pair: None, lambda: None),
+    )
+
     seg_grad[...] = seg_grad[...] / divisor
 
     count_rest = count_all - soft_count
@@ -1259,6 +1299,7 @@
             lambda part: reducer.tick(4 + part),
             lambda part: None,
             lambda pair: reducer.ticks(8 + 2 * pair, 10 + 2 * pair),
+            lambda: own_copy(21).wait(),
         ),
     )
     embed_grad = exact_product(hot_turned(0, 0, vocab).astype(jnp.bfloat16), grad[...])
@@ -1273,48 +1314,102 @@
     )
     for j in range(7):
         count_copy(j).wait_send()
-    for j in range(3):
-        ids_copy(j).wait_send()
-    sums = Sums(places(), column, [(dp, peer) for peer in side], small_ref, small_out, square_out, reduce_refs)
+    for which in range(3):
+        for j in range(3):
+            ids_copy(j, which).wait_send()
+    moments = [
+        pltpu.make_async_copy(first_far, leave.at[pl.ds(0, held * 64)], m_sem.at[0]),
+        pltpu.make_async_copy(second_far, after.at[pl.ds(0, held * 64)], m_sem.at[1]),
+    ]
+    for copy in moments:
+        copy.start()
+    sums = Sums(places(), column, [(dp, peer) for peer in side], small_ref, reduce_refs)
     sums.start_small()
     reducer.ticks(16, reducer.last_tick)
     sums.pass_small()
-    square = reducer.collect(source_ref, parity_ref, owned_ref, stage)
-    held = out_ref.shape[0]
-    for slot in range(held):
-        pltpu.make_async_copy(
-            stage.at[slot // 8, slot % 8 // 2, slot % 2], out_ref.at[slot], out_sem.at[slot]
-        ).start()
-    sums.squares(square)
-    for slot in range(held):
-        pltpu.make_async_copy(
-            stage.at[slot // 8, slot % 8 // 2, slot % 2], out_ref.at[slot], out_sem.at[slot]
-        ).wait()
+    square = reducer.collect(source_ref, pair_ref, parity_ref, owned_ref, stage)
+    for copy in moments:
+        copy.wait()
+    small_sum, square_sum = sums.squares(square)
+    gain_sum = small_sum[0:6, :]
+    grad_norm = jnp.sqrt(total_of(square_sum) + total_of(gain_sum * gain_sum))
+    clip = jnp.minimum(1.0, CLIP_NORM / (grad_norm + 1e-06))
+    steps = jnp.full((1, 1), step_ref[0], jnp.int32).astype(jnp.float32)
+    corrections = [1.0 / (1.0 - jnp.exp(steps * math.log(beta))) for beta in (BETA_ONE, BETA_TWO)]
+
+    def renew(param, moment_a, moment_b, grad_in, rate, decay):
+        new_first = BETA_ONE * moment_a + (1.0 - BETA_ONE) * grad_in
+        new_second = BETA_TWO * moment_b + (1.0 - BETA_TWO) * grad_in * grad_in
+        move = (new_first * corrections[0]) / (jnp.sqrt(new_second * corrections[1]) + ADAM_EPS)
+        return param - rate * (move + decay * param), new_first, new_second
+
+    def leaving(slot):
+        rows = pl.ds(pl.multiple_of(slot * 64, 64), 64)
+        return [
+            pltpu.make_async_copy(source.at[rows], target.at[rows], out_sem.at[number, slot])
+            for number, (source, target) in enumerate(
+                ((grad, master_out), (leave, first_out), (after, second_out), (attended, low_out))
+            )
+        ]
+
+    def update(slot, carry):
+        rows = pl.ds(pl.multiple_of(slot * 64, 64), 64)
+        param, moment_a, moment_b = master_ref[slot], leave[rows, :], after[rows, :]
+        reduced = stage[slot // 8, slot % 8 // 2, slot % 2].reshape(64, width)
+        new_param, new_first, new_second = renew(
+            param, moment_a, moment_b, reduced * clip, RATE_TILES, WEIGHT_DECAY
+        )
+        keep = owned_ref[slot] > 0
+        new_param = jnp.where(keep, new_param, param)
+        grad[rows, :] = new_param
+        leave[rows, :] = jnp.where(keep, new_first, moment_a)
+        after[rows, :] = jnp.where(keep, new_second, moment_b)
+        attended[rows, :] = new_param.astype(jnp.bfloat16)
+        for copy in leaving(slot):
+            copy.start()
+        return carry
+
+    lax.fori_loop(0, held, update, 0)
+    gains_out[...], gain_first_out[...], gain_second_out[...] = renew(
+        gains_ref[...], gain_first_ref[...], gain_second_ref[...], gain_sum * clip, RATE_GAINS, 0.0
+    )
+    loss = jnp.zeros((1, 1), jnp.float32)
+    row = small_sum[6:7, :]
+    for micro in range(micro_count):
+        entropy, soft, count = (total_of(jnp.where(lane == micro + 8 * part, row, 0.0)) for part in range(3))
+        prior = -(
+            log_gamma(count + 1.0)
+            - log_gamma(soft + 1.0)
+            - log_gamma(count - soft + 1.0)
+            + soft * math.log(PRIOR_RATE)
+            + (count - soft) * math.log(1.0 - PRIOR_RATE)
+        )
+        loss = loss + (entropy + prior) / count
+    loss_out[0] = jnp.sum(loss) / micro_count
+    norm_out[0] = jnp.sum(grad_norm)
     sums.finish()
     reducer.finish()
 
-
-def step_call(length_one, owner_slot, master, ids, gains, micro_count):
+    def left(slot, carry):
+        for copy in leaving(slot):
+            copy.wait()
+        return carry
+
+    lax.fori_loop(0, held, left, 0)
+
+
+def step_call(char_ids, targets, seg_ids, lengths, owner_slot, step_count, master, first, second, *gains):
     held, rows, width = master.shape
     tile_count = owner_slot.shape[0]
+    micro_count = char_ids.shape[0]
     seq_count, dp_count = lax.axis_size("seq"), lax.axis_size("dp")
     groups = tile_count // 2
-    length = seq_count * ids.shape[2]
+    length = seq_count * char_ids.shape[2]
     segments = SEG_DEV * seq_count
     dma = pltpu.SemaphoreType.DMA
     vmem = pl.BlockSpec(memory_space=pltpu.VMEM)
     smem = pl.BlockSpec(memory_space=pltpu.SMEM)
     hbm = pl.BlockSpec(memory_space=pl.ANY)
-    local = owner_slot - lax.axis_index("seq") * held
-    valid = jnp.logical_and(local >= 0, local < held).astype(jnp.int32)
-    hot = jnp.arange(held)[:, None] == jnp.take(local, jnp.array(GRAD_ORDER))[None, :]
-    source = jnp.sum(jnp.where(hot, jnp.arange(tile_count)[None, :], 0), axis=1)
-    owned = jnp.any(hot, axis=1).astype(jnp.int32)
-    parity = jnp.concatenate([jnp.pad(source // 2, (0, 16 - held)), source % 2])
-    local = jnp.where(valid > 0, local, 0)
-
-    def used(values):
-        return jnp.concatenate([values[25:], values[:12], values[24:25], values[12:24]])
 
     def full(*shape):
         return pltpu.VMEM(shape, jnp.float32)
@@ -1343,17 +1438,18 @@
         full(dp_count, 8, width), full(seq_count, 8, width), full(dp_count, 8, 128), full(seq_count, 8, 128),
         [dma((7,)), dma((7,)), dma((3,)), dma((3,)), dma((7,)), dma((7,)), dma((3,)), dma((3,))],
     ]
-    return pl.pallas_call(
+    flat = jax.ShapeDtypeStruct((held * rows, width), jnp.float32)
+    gain_shape = jax.ShapeDtypeStruct(gains[0].shape, jnp.float32)
+    one = jax.ShapeDtypeStruct((1,), jnp.float32)
+    far = jax.ShapeDtypeStruct((tile_count, 4, 2, 2, 16, width), jnp.float32)
+    results = pl.pallas_call(
         functools.partial(step_kernel, micro_count),
         out_shape=(
-            jax.ShapeDtypeStruct((tile_count, 4, 2, 2, 16, width), jnp.float32),
-            jax.ShapeDtypeStruct((tile_count, 4, 2, 2, 16, width), jnp.float32),
-            jax.ShapeDtypeStruct((held, 2, 2, 16, width), jnp.float32),
-            jax.ShapeDtypeStruct((8, width), jnp.float32),
-            jax.ShapeDtypeStruct((8, 128), jnp.float32),
+            far, far, flat, flat, flat, jax.ShapeDtypeStruct(flat.shape, jnp.bfloat16),
+            gain_shape, gain_shape, gain_shape, one, one,
         ),
-        in_specs=[smem] * 6 + [vmem] * 3,
-        out_specs=(hbm, hbm, hbm, vmem, vmem),
+        in_specs=[smem] * 3 + [vmem] * 7 + [hbm] * 2,
+        out_specs=(hbm,) * 6 + (vmem,) * 3 + (smem,) * 2,
         scratch_shapes=[half(tile_count, 4, 2, 4, 16, width)]
         + kept(length)
         + [full(segments, width)]
@@ -1361,9 +1457,10 @@
         + [
             half(width, length), half(length, 4 * width), half(length, width), half(width, length),
             full(length, 128), full(length, 128), full(width // 2, width), full(8, width),
-            pltpu.VMEM((8, length), jnp.int32), full(length, 8), full(4, 4, 2, 2, 2, 16, width), dma((2,)),
-            full(dp_count, 8, 128), dma((7,)), dma((7,)), dma((3,)), dma((3,)), dma,
-            dma((4,)), dma((tile_count,)), dma((held,)),
+            pltpu.VMEM((3, 4, 1, length // 4), jnp.int32), pltpu.VMEM((8, length), jnp.int32), full(length, 8),
+            pltpu.SMEM((held,), jnp.int32), pltpu.SMEM((held,), jnp.int32), pltpu.SMEM((held,), jnp.int32), pltpu.SMEM((held,), jnp.int32), full(4, 4, 2, 2, 2, 16, width), dma((2,)),
+            full(dp_count, 8, 128), dma((7,)), dma((7,)), dma((3, 3)), dma((3, 3)),
+            dma((4,)), dma((tile_count,)), dma((4, held)), dma((2,)),
             dma((3, groups)), dma((3, groups)), dma((3, groups)), dma((3, groups)),
             dma((2, groups)), dma((2, groups)), dma((2, groups)), dma((2, groups)),
             dma((groups,)), dma((groups,)), reduce_refs,
@@ -1372,16 +1469,12 @@
         compiler_params=pltpu.CompilerParams(
             collective_id=2, has_side_effects=True, vmem_limit_bytes=STEP_VMEM
         ),
-    )(length_one, used(local), used(valid), source, parity, owned, master, ids, gains)[2:]
-
-
-def whole_step(char_ids, targets, seg_ids, lengths, owner_slot, master, gain_rows):
-    micro_count = char_ids.shape[0]
-    ids = jnp.stack([char_ids[:, 0], targets[:, 0], seg_ids[:, 0]], axis=1)
-    ids = jnp.pad(ids, ((0, 0), (0, 5), (0, 0)))
-    length_one = lax.dynamic_slice_in_dim(lengths[:, 0], lax.axis_index("seq"), 1)
-    gains = jnp.pad(gain_rows, ((0, 2), (0, 0)))
-    return step_call(length_one, owner_slot, master, ids, gains, micro_count)
+    )(
+        lengths, owner_slot, step_count, master, char_ids, targets, seg_ids, *gains,
+        first.reshape(flat.shape), second.reshape(flat.shape),
+    )
+    master_new, first_new, second_new, low_new = (value.reshape(master.shape) for value in results[2:6])
+    return (results[9], results[10], master_new, first_new, second_new, low_new) + tuple(results[6:9])
 
 
 def body(
@@ -1402,40 +1495,29 @@
     model_width = master.shape[2]
     slot_count = master.shape[0] * lax.axis_size("seq")
     if (micro_count, lax.axis_size("seq"), lax.axis_size("dp")) == (4, 4, 8):
-        shard_total, small, squares = whole_step(
-            char_ids, targets, seg_ids, lengths, owner_slot, master, gain_rows
+        return step_call(
+            char_ids, targets, seg_ids, lengths, owner_slot, step_count, master, tile_first, tile_second,
+            gain_rows, gain_first, gain_second,
         )
-        shard_total = shard_total.reshape(master.shape)
-        gain_sum, square_sum = small[0:6], jnp.sum(squares)
-        entropy, soft, count = (small[6, 8 * i : 8 * i + micro_count] for i in range(3))
-        prior = -(
-            lax.lgamma(count + 1.0)
-            - lax.lgamma(soft + 1.0)
-            - lax.lgamma(count - soft + 1.0)
-            + soft * jnp.log(PRIOR_RATE)
-            + (count - soft) * jnp.log(1.0 - PRIOR_RATE)
+    tile_total = jnp.zeros((owner_slot.shape[0], model_width, model_width), jnp.float32)
+    gain_total = jnp.zeros_like(gain_rows)
+    loss_total = jnp.zeros((), jnp.float32)
+    for micro in range(micro_count):
+        tiles = gather_tiles(master, owner_slot)
+        tile_part, gain_part, loss_part = micro_step(
+            tiles,
+            gain_rows,
+            char_ids[micro, 0],
+            targets[micro, 0],
+            seg_ids[micro, 0],
+            lengths[micro, 0],
+            micro_count,
         )
-        loss_total = jnp.sum((entropy + prior) / count) / micro_count
-    else:
-        tile_total = jnp.zeros((owner_slot.shape[0], model_width, model_width), jnp.float32)
-        gain_total = jnp.zeros_like(gain_rows)
-        loss_total = jnp.zeros((), jnp.float32)
-        for micro in range(micro_count):
-            tiles = gather_tiles(master, owner_slot)
-            tile_part, gain_part, loss_part = micro_step(
-                tiles,
-                gain_rows,
-                char_ids[micro, 0],
-                targets[micro, 0],
-                seg_ids[micro, 0],
-                lengths[micro, 0],
-                micro_count,
-            )
-            tile_total = tile_total + tile_part
-            gain_total = gain_total + gain_part
-            loss_total = loss_total + loss_part
-        shard_total = reduce_tiles(tile_total, owner_slot, slot_count)
-        gain_sum, square_sum = lax.psum((gain_total, jnp.sum(shard_total * shard_total)), ("dp", "seq"))
+        tile_total = tile_total + tile_part
+        gain_total = gain_total + gain_part
+        loss_total = loss_total + loss_part
+    shard_total = reduce_tiles(tile_total, owner_slot, slot_count)
+    gain_sum, square_sum = lax.psum((gain_total, jnp.sum(shard_total * shard_total)), ("dp", "seq"))
     grad_norm = jnp.sqrt(square_sum + jnp.sum(gain_sum * gain_sum))
     clip_factor = jnp.minimum(1.0, CLIP_NORM / (grad_norm + 1e-06))
     step_float = step_count[0].astype(jnp.float32)

time: 277 us -> 262 us (0.946)
  other arithmetic: 18.6 us -> 0 us
  local copies, waits for them, and re-layouts: 4.86 us -> 9.87 us
    unnamed x16 -> x20, local copies, waits for them, and re-layouts: 0.32 us -> 9.87 us
    convert_element_type x3 -> x0, other arithmetic: 5.91 us -> none  [the longest x1 4.71 us: body(): master_new.astype(jnp.bfloat16)]
    reduce_sum x4 -> x0, other arithmetic: 4.29 us -> none  [the longest x1 1.56 us: body(): loss_total = jnp.sum((entropy + prior) / count) / micro_count]
    concatenate x2 -> x0, other arithmetic: 3.76 us -> none  [the longest x1 1.88 us: step_call(): parity = jnp.concatenate([jnp.pad(source // 2, (0, 16 - held)), source % 2])]
where the time goes in v6:
time: 262 us; the launch traced here: 261 us
  Pallas kernels  247 us (94%)
  local copies, waits for them, and re-layouts  9.87 us (4%)
  between operations  4.77 us (2%)
    pallas_call x1, Pallas kernels, step_call(): pl.pallas_call(functools.partial(step_kernel, micro_count), out_shape=(fa...  247 us
    unnamed x20, local copies, waits for them, and re-layouts  9.87 us

profile of v6, /device:TPU:0, one launch (start us, length us, event | category | flops | bytes accessed | tf_op | source)
XLA Modules:
  0.0 261.4 jit_solution(17587995782327314062)
XLA Ops:
  1.3 1.3 copy.21.lengths_ref
  2.6 246.8 %step.1 = (f32[26,4,2,2,16,512]{5,4,3,2,1,0:T(8,128)}, f32[26,4,2,2,16,512]{5,4,3,2,1,0:T(8,128)}, f32[640,512]{1,0:T(8,128)}, f32[640,512]{1,0:T(8,128)}, f32[6...) custom-call(s32[4,1]{1,0:T(4,128)} %copy.21.lengths_ref, ...), custom_call_target="tpu_custom_call" | custom-call | tf_op jit(solution)/shard_map/step/pallas_call | solution.py:1445
  250.6 0.0 copy-start.1
  250.6 2.6 copy.34
  253.2 0.0 copy-done.1
  253.2 0.0 copy-start
  253.2 1.1 copy.35
  254.3 0.7 copy-done
  255.0 0.0 copy-start.2
  255.0 1.1 copy.36
  256.0 0.5 copy-done.2
  256.5 0.0 copy-start.5
  256.5 0.0 copy-start.4
  256.5 0.0 copy-start.3
  256.5 0.8 copy.37
  257.4 0.0 copy-done.5
  257.4 0.6 copy.38
  258.0 0.0 copy-done.4
  258.0 0.6 copy.39
  258.6 0.0 copy-done.3
  258.6 0.6 copy.40
Async XLA Ops:
  250.6 2.6 copy-start.1
  253.2 1.8 copy-start
  255.0 1.5 copy-start.2
  256.5 0.8 copy-start.5
  256.5 1.5 copy-start.4
  256.5 2.1 copy-start.3

commit v7 on v6

--- a/solution.py
+++ b/solution.py
@@ -336,7 +336,7 @@
 
 MESH = pl.DeviceIdType.MESH
 VMEM_LIMIT = 60 * 1024 * 1024
-STEP_VMEM = 63 * 1024 * 1024
+STEP_VMEM = 66_900_000
 
 
 def remote(src, dst, send_sem, recv_sem, peer):
@@ -397,7 +397,7 @@
 
 ROWS = 256
 LAG = 2
-START = 10
+START = 8
 
 
 def split_three(value):
@@ -538,6 +538,14 @@
     lax.fori_loop(0, 4, pair_step, 0)
 
 
+def put_rows(blocks, rows, value):
+    blocks[pl.ds(rows.start // 16, value.shape[0] // 16)] = value.reshape(-1, 16, value.shape[1])
+
+
+def whole_rows(blocks, length):
+    return blocks[0 : length // 16].reshape(length, blocks.shape[2])
+
+
 def block_run(block, matrix, gains, pumps):
     place = block.place
     gain_attn = gains[block.gain_row : block.gain_row + 1, :]
@@ -592,13 +600,13 @@
         each_block(length, rows_step)
 
     def low_step(rows):
-        grad_low[rows, :] = grad[rows, :].astype(jnp.bfloat16)
+        put_rows(grad_low, rows, grad[rows, :].astype(jnp.bfloat16))
 
     each_block(length, low_step)
 
     def down_step(part, carry):
         down(part)
-        put(order[0] + part, lambda half: product(turned[half, all_rows], grad_low[all_rows, :]))
+        put(order[0] + part, lambda half: product(turned[half, all_rows], whole_rows(grad_low, length)))
         pumps[0](part)
         return carry
 
@@ -620,7 +628,7 @@
         grad_after = grad[rows, :] + back
         grad[rows, :] = grad_after
         low = grad_after.astype(jnp.bfloat16)
-        branch[rows, :] = low
+        put_rows(branch, rows, low)
         upstream[rows, :] = product_nt(low, matrix(place + 3)).astype(jnp.bfloat16)
 
     each_block(length, middle)
@@ -632,7 +640,7 @@
         return carry
 
     lax.fori_loop(0, 4, up_step, 0)
-    put(order[2], lambda half: product(turned[half, all_rows], branch[all_rows, :]))
+    put(order[2], lambda half: product(turned[half, all_rows], whole_rows(branch, length)))
     pumps[3]()
     attend_back(block, upstream, grad_qkv, key_sum, value_sum, pumps[2])
 
@@ -674,14 +682,15 @@
         self.own_far, self.other_far, self.pair_copy = own_far, other_far, pair_copy
         self.beside, self.side, self.tower = beside, side, tower
         (
-            self.own, self.other, self.one, self.two, self.three, self.final,
+            self.own, self.other, self.one, self.two, self.three, self.final, self.square,
             self.b1_out, self.b1_in, self.b2_out, self.b2_in, self.c_out, self.c_in, self.d_out, self.d_in,
             self.b1_unit_out, self.b1_unit_in, self.b2_unit_out, self.b2_unit_in,
             self.c_unit_out, self.c_unit_in, self.d_unit_out, self.d_unit_in,
             self.l_sem, self.b1_send, self.b1_recv, self.b2_send, self.b2_recv,
             self.c_send, self.c_recv, self.d_send, self.d_recv,
-        ) = refs[:31]
+        ) = refs[:32]
         self.lane = lax.broadcasted_iota(jnp.int32, (8, 128), 1)
+        self.square[...] = jnp.zeros_like(self.square)
 
     def loads(self, pair):
         two = pl.ds(pair * 2, 2)
@@ -828,6 +837,7 @@
             for j in range(3):
                 total = total + decode(self.c_in[j, tile], self.c_unit_in[j, pair][:, order : order + 1])
             self.final[tile] = total
+            self.square[...] = self.square[...] + total * total
             coded, unit = encode(total)
             self.d_out[slot, order] = coded
             units = jnp.where(self.lane == order, unit, units)
@@ -858,7 +868,7 @@
 
         lax.fori_loop(start, stop, body, 0)
 
-    def collect(self, source_ref, pair_ref, parity_ref, owned_ref, stage):
+    def collect(self, source_ref, pair_ref, parity_ref, stage):
         def arrive(pair, carry):
             for j in range(3):
                 for copy in self.share_copies(pair, j):
@@ -868,10 +878,8 @@
         lax.fori_loop(0, self.pairs, arrive, 0)
         for order in range(self.pairs * 2 - 4, self.pairs * 2):
             self.pair_copy(order).wait_send()
-        width = self.final.shape[2]
-
-        def step(slot, square):
-            keep = owned_ref[slot] > 0
+
+        def step(slot, carry):
             tile = source_ref[slot]
             places_of = [self.seq] + [peer[1] for peer in self.side]
             for number, quarter in enumerate(places_of):
@@ -881,12 +889,13 @@
                     units = self.d_unit_in[number - 1, pair_ref[slot]]
                     unit = jnp.where(parity_ref[slot] > 0, units[:, 1:2], units[:, 0:1])
                     value = decode(self.d_in[number - 1, tile], unit)
-                value = jnp.where(keep, value, jnp.zeros_like(value))
                 stage[slot // 8, slot % 8 // 2, slot % 2, quarter // 2, quarter % 2] = value
-                square = square + value * value
-            return square
-
-        square = lax.fori_loop(0, source_ref.shape[0], step, jnp.zeros((16, width), jnp.float32))
+            return carry
+
+        lax.fori_loop(0, source_ref.shape[0], step, 0)
+
+    def folded_square(self):
+        square, width = self.square[...], self.square.shape[1]
         folded = jnp.zeros((8, 128), jnp.float32)
         for r in range(2):
             for w in range(width // 128):
@@ -908,7 +917,7 @@
         self.dp, self.seq, _, _ = place
         self.column, self.side = column, side
         self.small = small
-        self.small_dp, self.small_seq, self.square_dp, self.square_seq, self.sems = refs[31:]
+        self.small_dp, self.small_seq, self.square_dp, self.square_seq, self.sems = refs[32:]
 
     def copies(self, which):
         sends, recvs = self.sems[2 * which], self.sems[2 * which + 1]
@@ -943,18 +952,22 @@
         self.small_seq[self.seq] = total
         self.start(1)
 
-    def squares(self, folded):
+    def start_squares(self, folded):
         self.square_dp[self.dp] = folded
         self.start(2)
-        self.arrive(1)
-        small = (self.small_seq[0] + self.small_seq[1]) + (self.small_seq[2] + self.small_seq[3])
+
+    def pass_squares(self):
         self.arrive(2)
         total = self.square_dp[0]
         for j in range(1, 8):
             total = total + self.square_dp[j]
         self.square_seq[self.seq] = total
         self.start(3)
+
+    def results(self):
+        self.arrive(1)
         self.arrive(3)
+        small = (self.small_seq[0] + self.small_seq[1]) + (self.small_seq[2] + self.small_seq[3])
         return small, (self.square_seq[0] + self.square_seq[1]) + (self.square_seq[2] + self.square_seq[3])
 
     def finish(self):
@@ -967,14 +980,12 @@
 
 
 def step_kernel(
-    micro_count, lengths_ref, owner_ref, step_ref, master_ref, chars_ref, targets_ref, segs_ref,
-    gains_ref, gain_first_ref, gain_second_ref, first_far, second_far,
-    own_far, other_far, master_out, first_out, second_out, low_out, gains_out, gain_first_out, gain_second_out,
-    loss_out, norm_out,
+    micro_count, lengths_ref, owner_ref, master_ref, chars_ref, targets_ref, segs_ref, gains_ref,
+    own_far, other_far, reduced_out, small_out, square_out, owned_out,
     weights, qkv, logs, attended, after, leave, grad,
     seg_entry, seg_qkv, seg_logs, seg_attended, seg_after, seg_leave, seg_grad,
     turned, grad_inner, branch, turned_norm, key_sum, value_sum, head_grad, small_ref,
-    ids_in, ids_row, ids_col, source_ref, pair_ref, parity_ref, owned_ref, stage, stage_sem, counts, count_send, count_recv, i_send, i_recv, g_send, g_recv, out_sem, m_sem,
+    slots, ids_in, ids_row, ids_col, source_ref, pair_ref, parity_ref, owned_ref, stage, stage_sem, counts, count_send, count_recv, i_send, i_recv, g_send, g_recv, out_sem,
     p_send, p_recv, z_send, z_recv, s_send, s_recv, d_send, d_recv, c_send, c_recv,
     reduce_refs,
 ):
@@ -992,6 +1003,7 @@
     tower = [((z + j) % 4 * 2 + core, seq) for j in (1, 2, 3)]
     meet([(dp, peer) for peer in side] + column)
 
+    held = master_ref.shape[0]
     all_ids = (chars_ref, targets_ref, segs_ref)
 
     def ids_copy(j, which):
@@ -999,14 +1011,9 @@
             all_ids[which].at[side[j]], ids_in.at[which, seq], i_send.at[j, which], i_recv.at[j, which], (dp, side[j])
         )
 
-    def part_of(which):
-        return pl.ds(pl.multiple_of(which * width, width), width)
-
-    def peer_copy(group, j):
+    def peer_copy(j):
         return remote(
-            grad_inner.at[pl.ds(pl.multiple_of(group * 32, 32), 32), part_of(side[j])],
-            grad_inner.at[pl.ds(pl.multiple_of(512 + group * 32, 32), 32), part_of(j)],
-            p_send.at[j, group], p_recv.at[j, group], (dp, side[j]),
+            branch.at[pl.ds(held * side[j], held)], slots.at[pl.ds(held * seq, held)], p_send.at[j], p_recv.at[j], (dp, side[j])
         )
 
     def tower_copy(group, j):
@@ -1025,19 +1032,12 @@
         spot = weights.at[pl.ds(group * 2, 2), :, core]
         return remote(spot, spot, c_send.at[group], c_recv.at[group], sibling)
 
-    def offer(group):
-        for j in (2, 0, 1):
-            peer_copy(group, j).start()
-
-    def combine(group):
-        for j in range(3):
-            peer_copy(group, j).wait_recv()
+    def pick(group):
         for number in range(2):
-            row = group * 32 + number * 16
-            value = grad_inner[pl.ds(pl.multiple_of(row, 16), 16), part_of(seq)]
-            for j in range(3):
-                value = value + grad_inner[pl.ds(pl.multiple_of(512 + row, 16), 16), pl.ds(j * width, width)]
-            weights[group * 2 + number, z, core, seq] = value
+            place = group * 2 + number
+            late = (place > 13).astype(jnp.int32)
+            tile = jnp.where(place == 0, 25, jnp.where(place == 13, 24, place - 1 - late))
+            weights[place, z, core, seq] = slots[owner_ref[tile]]
         for j in range(3):
             tower_copy(group, j).start()
 
@@ -1058,11 +1058,11 @@
             corner_copy(group, way).wait_recv()
         core_copy(group).start()
 
-    stages = (offer, combine, widen, corner, share)
+    stages = (pick, widen, corner, share)
 
     def tick(number):
         for order, stage_of in enumerate(stages):
-            group = number - LAG * order
+            group = jnp.int32(number) - LAG * order
 
             @pl.when(jnp.logical_and(group >= 0, group < groups))
             def _():
@@ -1087,22 +1087,18 @@
         for j in range(3):
             ids_copy(j, which).start()
 
-    held = master_ref.shape[0]
-
-    def pick(place, carry):
-        late = (place > 13).astype(jnp.int32)
-        tile = jnp.where(place == 0, 25, jnp.where(place == 13, 24, place - 1 - late))
-        slot = owner_ref[tile] - held * seq
-        keep = jnp.logical_and(slot >= 0, slot < held)
-        value = master_ref[jnp.minimum(jnp.maximum(slot, 0), held - 1)]
-        value = jnp.where(keep, value, jnp.zeros_like(value)).astype(jnp.bfloat16)
+    def lower(slot, carry):
+        value = master_ref[slot].astype(jnp.bfloat16)
         for quarter in range(4):
-            grad_inner[pl.ds(pl.multiple_of(place * 16, 16), 16), quarter * width : quarter * width + width] = value[
-                16 * quarter : 16 * quarter + 16
-            ]
+            branch[quarter * held + slot] = value[16 * quarter : 16 * quarter + 16]
         return carry
 
-    lax.fori_loop(0, groups * 2, pick, 0)
+    lax.fori_loop(0, held, lower, 0)
+    for j in (2, 0, 1):
+        peer_copy(j).start()
+    slots[pl.ds(held * seq, held)] = branch[pl.ds(held * seq, held)]
+    for j in range(3):
+        peer_copy(j).wait_recv()
     ticks(0, START)
 
     def matrix(place):
@@ -1258,7 +1254,6 @@
     seg_grad[...] = exact_product(hot_turned(2, 0, segments).astype(jnp.bfloat16), grad[...])
     def sent(group, carry):
         for j in range(3):
-            peer_copy(group, j).wait_send()
             tower_copy(group, j).wait_send()
         for way in range(2):
             side_copy(group, way).wait_send()
@@ -1267,6 +1262,8 @@
         return carry
 
     lax.fori_loop(0, groups, sent, 0)
+    for j in range(3):
+        peer_copy(j).wait_send()
     reducer = Reducer(
         places(), own_far, other_far, pair_copy, [(dp, peer) for peer in beside], [(dp, peer) for peer in side], tower, reduce_refs
     )
@@ -1286,13 +1283,13 @@
         gain = gains_ref[5:6, :]
         small_ref[5:6, :] = small_ref[5:6, :] + jnp.sum(logit * reach, axis=0, keepdims=True) * root_width
         pre = (logit * gain * root_width * (1.0 - reach * reach)).astype(jnp.bfloat16)
-        branch[rows, :] = pre
+        put_rows(branch, rows, pre)
         turned[:, rows] = turn(low)
         spread = exact_product(hot_rows(rows, 2, 1, segments), seg_grad[...])
         grad[rows, :] = (grad[rows, :] + spread) + product_nt(pre, matrix(13))
 
     each_block(length, join)
-    put(12, lambda half: product(turned[half, :], branch[...]))
+    put(12, lambda half: product(turned[half, :], whole_rows(branch, length)))
     block_back(
         char, grad, matrix, gains_ref, small_ref, temps, put,
         (
@@ -1317,88 +1314,34 @@
     for which in range(3):
         for j in range(3):
             ids_copy(j, which).wait_send()
-    moments = [
-        pltpu.make_async_copy(first_far, leave.at[pl.ds(0, held * 64)], m_sem.at[0]),
-        pltpu.make_async_copy(second_far, after.at[pl.ds(0, held * 64)], m_sem.at[1]),
-    ]
-    for copy in moments:
-        copy.start()
     sums = Sums(places(), column, [(dp, peer) for peer in side], small_ref, reduce_refs)
     sums.start_small()
     reducer.ticks(16, reducer.last_tick)
+    sums.start_squares(reducer.folded_square())
     sums.pass_small()
-    square = reducer.collect(source_ref, pair_ref, parity_ref, owned_ref, stage)
-    for copy in moments:
-        copy.wait()
-    small_sum, square_sum = sums.squares(square)
-    gain_sum = small_sum[0:6, :]
-    grad_norm = jnp.sqrt(total_of(square_sum) + total_of(gain_sum * gain_sum))
-    clip = jnp.minimum(1.0, CLIP_NORM / (grad_norm + 1e-06))
-    steps = jnp.full((1, 1), step_ref[0], jnp.int32).astype(jnp.float32)
-    corrections = [1.0 / (1.0 - jnp.exp(steps * math.log(beta))) for beta in (BETA_ONE, BETA_TWO)]
-
-    def renew(param, moment_a, moment_b, grad_in, rate, decay):
-        new_first = BETA_ONE * moment_a + (1.0 - BETA_ONE) * grad_in
-        new_second = BETA_TWO * moment_b + (1.0 - BETA_TWO) * grad_in * grad_in
-        move = (new_first * corrections[0]) / (jnp.sqrt(new_second * corrections[1]) + ADAM_EPS)
-        return param - rate * (move + decay * param), new_first, new_second
+    sums.pass_squares()
+    reducer.collect(source_ref, pair_ref, parity_ref, stage)
+    for slot in range(held):
+        pltpu.make_async_copy(
+            stage.at[slot // 8, slot % 8 // 2, slot % 2], reduced_out.at[slot], out_sem.at[slot]
+        ).start()
+    small_sum, square_sum = sums.results()
+    small_out[...] = small_sum
+    square_out[...] = square_sum
 
     def leaving(slot):
-        rows = pl.ds(pl.multiple_of(slot * 64, 64), 64)
-        return [
-            pltpu.make_async_copy(source.at[rows], target.at[rows], out_sem.at[number, slot])
-            for number, (source, target) in enumerate(
-                ((grad, master_out), (leave, first_out), (after, second_out), (attended, low_out))
-            )
-        ]
-
-    def update(slot, carry):
-        rows = pl.ds(pl.multiple_of(slot * 64, 64), 64)
-        param, moment_a, moment_b = master_ref[slot], leave[rows, :], after[rows, :]
-        reduced = stage[slot // 8, slot % 8 // 2, slot % 2].reshape(64, width)
-        new_param, new_first, new_second = renew(
-            param, moment_a, moment_b, reduced * clip, RATE_TILES, WEIGHT_DECAY
+        return pltpu.make_async_copy(
+            stage.at[slot // 8, slot % 8 // 2, slot % 2], reduced_out.at[slot], out_sem.at[slot]
         )
-        keep = owned_ref[slot] > 0
-        new_param = jnp.where(keep, new_param, param)
-        grad[rows, :] = new_param
-        leave[rows, :] = jnp.where(keep, new_first, moment_a)
-        after[rows, :] = jnp.where(keep, new_second, moment_b)
-        attended[rows, :] = new_param.astype(jnp.bfloat16)
-        for copy in leaving(slot):
-            copy.start()
-        return carry
-
-    lax.fori_loop(0, held, update, 0)
-    gains_out[...], gain_first_out[...], gain_second_out[...] = renew(
-        gains_ref[...], gain_first_ref[...], gain_second_ref[...], gain_sum * clip, RATE_GAINS, 0.0
-    )
-    loss = jnp.zeros((1, 1), jnp.float32)
-    row = small_sum[6:7, :]
-    for micro in range(micro_count):
-        entropy, soft, count = (total_of(jnp.where(lane == micro + 8 * part, row, 0.0)) for part in range(3))
-        prior = -(
-            log_gamma(count + 1.0)
-            - log_gamma(soft + 1.0)
-            - log_gamma(count - soft + 1.0)
-            + soft * math.log(PRIOR_RATE)
-            + (count - soft) * math.log(1.0 - PRIOR_RATE)
-        )
-        loss = loss + (entropy + prior) / count
-    loss_out[0] = jnp.sum(loss) / micro_count
-    norm_out[0] = jnp.sum(grad_norm)
+
+    for slot in range(held):
+        owned_out[slot] = owned_ref[slot]
+        leaving(slot).wait()
     sums.finish()
     reducer.finish()
 
-    def left(slot, carry):
-        for copy in leaving(slot):
-            copy.wait()
-        return carry
-
-    lax.fori_loop(0, held, left, 0)
-
-
-def step_call(char_ids, targets, seg_ids, lengths, owner_slot, step_count, master, first, second, *gains):
+
+def step_call(char_ids, targets, seg_ids, lengths, owner_slot, master, gains):
     held, rows, width = master.shape
     tile_count = owner_slot.shape[0]
     micro_count = char_ids.shape[0]
@@ -1428,7 +1371,7 @@
 
     reduce_refs = [
         full(2, 4, 2, 2, 16, width), full(2, 4, 2, 2, 16, width),
-        full(2, 2, 8, 16, width), full(2, 2, 4, 16, width), full(2, 2, 16, width), full(tile_count, 16, width),
+        full(2, 2, 8, 16, width), full(2, 2, 4, 16, width), full(2, 2, 16, width), full(tile_count, 16, width), full(16, width),
         codes(3, 2, 8), codes(tile_count, 8), codes(3, 2, 4), codes(tile_count, 4),
         codes(3, 3, 2), codes(3, tile_count), codes(3, 2), codes(3, tile_count),
         full(3, 2, 8, 128), full(tile_count, 8, 128), full(3, 2, 8, 128), full(tile_count, 8, 128),
@@ -1438,30 +1381,29 @@
         full(dp_count, 8, width), full(seq_count, 8, width), full(dp_count, 8, 128), full(seq_count, 8, 128),
         [dma((7,)), dma((7,)), dma((3,)), dma((3,)), dma((7,)), dma((7,)), dma((3,)), dma((3,))],
     ]
-    flat = jax.ShapeDtypeStruct((held * rows, width), jnp.float32)
-    gain_shape = jax.ShapeDtypeStruct(gains[0].shape, jnp.float32)
-    one = jax.ShapeDtypeStruct((1,), jnp.float32)
     far = jax.ShapeDtypeStruct((tile_count, 4, 2, 2, 16, width), jnp.float32)
-    results = pl.pallas_call(
+    return pl.pallas_call(
         functools.partial(step_kernel, micro_count),
         out_shape=(
-            far, far, flat, flat, flat, jax.ShapeDtypeStruct(flat.shape, jnp.bfloat16),
-            gain_shape, gain_shape, gain_shape, one, one,
+            far, far, jax.ShapeDtypeStruct((held, 2, 2, 16, width), jnp.float32),
+            jax.ShapeDtypeStruct((8, width), jnp.float32), jax.ShapeDtypeStruct((8, 128), jnp.float32),
+            jax.ShapeDtypeStruct((held,), jnp.int32),
         ),
-        in_specs=[smem] * 3 + [vmem] * 7 + [hbm] * 2,
-        out_specs=(hbm,) * 6 + (vmem,) * 3 + (smem,) * 2,
+        in_specs=[smem] * 2 + [vmem] * 5,
+        out_specs=(hbm,) * 3 + (vmem,) * 2 + (smem,),
         scratch_shapes=[half(tile_count, 4, 2, 4, 16, width)]
         + kept(length)
         + [full(segments, width)]
         + kept(segments)
         + [
-            half(width, length), half(length, 4 * width), half(length, width), half(width, length),
+            half(width, length), half(length, 4 * width), half(length // 16, 16, width), half(width, length),
             full(length, 128), full(length, 128), full(width // 2, width), full(8, width),
+            half(seq_count * held, 16, width),
             pltpu.VMEM((3, 4, 1, length // 4), jnp.int32), pltpu.VMEM((8, length), jnp.int32), full(length, 8),
             pltpu.SMEM((held,), jnp.int32), pltpu.SMEM((held,), jnp.int32), pltpu.SMEM((held,), jnp.int32), pltpu.SMEM((held,), jnp.int32), full(4, 4, 2, 2, 2, 16, width), dma((2,)),
             full(dp_count, 8, 128), dma((7,)), dma((7,)), dma((3, 3)), dma((3, 3)),
-            dma((4,)), dma((tile_count,)), dma((4, held)), dma((2,)),
-            dma((3, groups)), dma((3, groups)), dma((3, groups)), dma((3, groups)),
+            dma((4,)), dma((tile_count,)), dma((held,)),
+            dma((3,)), dma((3,)), dma((3, groups)), dma((3, groups)),
             dma((2, groups)), dma((2, groups)), dma((2, groups)), dma((2, groups)),
             dma((groups,)), dma((groups,)), reduce_refs,
         ],
@@ -1469,12 +1411,87 @@
         compiler_params=pltpu.CompilerParams(
             collective_id=2, has_side_effects=True, vmem_limit_bytes=STEP_VMEM
         ),
-    )(
-        lengths, owner_slot, step_count, master, char_ids, targets, seg_ids, *gains,
-        first.reshape(flat.shape), second.reshape(flat.shape),
-    )
-    master_new, first_new, second_new, low_new = (value.reshape(master.shape) for value in results[2:6])
-    return (results[9], results[10], master_new, first_new, second_new, low_new) + tuple(results[6:9])
+    )(lengths, owner_slot, master, char_ids, targets, seg_ids, gains)[2:]
+
+
+def finish_kernel(
+    micro_count, step_ref, owned_ref, master_ref, first_ref, second_ref, reduced_ref, small_ref, square_ref,
+    gains_ref, gain_first_ref, gain_second_ref,
+    loss_out, norm_out, master_out, first_out, second_out, low_out, gains_out, gain_first_out, gain_second_out,
+):
+    small_sum = small_ref[...]
+    gain_sum = small_sum[0:6, :]
+    grad_norm = jnp.sqrt(total_of(square_ref[...]) + total_of(gain_sum * gain_sum))
+    clip = jnp.minimum(1.0, CLIP_NORM / (grad_norm + 1e-06))
+    steps = jnp.full((1, 1), step_ref[0], jnp.int32).astype(jnp.float32)
+    corrections = [1.0 / (1.0 - jnp.exp(steps * math.log(beta))) for beta in (BETA_ONE, BETA_TWO)]
+
+    def renew(param, moment_a, moment_b, grad_in, rate, decay):
+        new_first = BETA_ONE * moment_a + (1.0 - BETA_ONE) * grad_in
+        new_second = BETA_TWO * moment_b + (1.0 - BETA_TWO) * grad_in * grad_in
+        move = (new_first * corrections[0]) / (jnp.sqrt(new_second * corrections[1]) + ADAM_EPS)
+        return param - rate * (move + decay * param), new_first, new_second
+
+    for number in range(master_ref.shape[0]):
+        param, moment_a, moment_b = master_ref[number], first_ref[number], second_ref[number]
+        new_param, new_first, new_second = renew(
+            param, moment_a, moment_b, reduced_ref[number] * clip, RATE_TILES, WEIGHT_DECAY
+        )
+        keep = owned_ref[pl.program_id(0) * master_ref.shape[0] + number] > 0
+        new_param = jnp.where(keep, new_param, param)
+        master_out[number] = new_param
+        first_out[number] = jnp.where(keep, new_first, moment_a)
+        second_out[number] = jnp.where(keep, new_second, moment_b)
+        low_out[number] = new_param.astype(jnp.bfloat16)
+
+    @pl.when(pl.program_id(0) == 0)
+    def _():
+        gains_out[...], gain_first_out[...], gain_second_out[...] = renew(
+            gains_ref[...], gain_first_ref[...], gain_second_ref[...], gain_sum * clip, RATE_GAINS, 0.0
+        )
+        loss = jnp.zeros((1, 1), jnp.float32)
+        row = small_sum[6:7, :]
+        lane = lax.broadcasted_iota(jnp.int32, row.shape, 1)
+        for micro in range(micro_count):
+            entropy, soft, count = (
+                total_of(jnp.where(lane == micro + 8 * part, row, 0.0)) for part in range(3)
+            )
+            prior = -(
+                log_gamma(count + 1.0)
+                - log_gamma(soft + 1.0)
+                - log_gamma(count - soft + 1.0)
+                + soft * math.log(PRIOR_RATE)
+                + (count - soft) * math.log(1.0 - PRIOR_RATE)
+            )
+            loss = loss + (entropy + prior) / count
+        loss_out[0] = jnp.sum(loss) / micro_count
+        norm_out[0] = jnp.sum(grad_norm)
+
+
+def finish_call(micro_count, step_count, owned, master, first, second, reduced, small, squares, gains):
+    held, rows, width = master.shape
+    count = 5
+    smem = pl.BlockSpec(memory_space=pltpu.SMEM)
+    slots = pl.BlockSpec((held // count, rows, width), lambda i: (i, 0, 0))
+
+    def whole(value):
+        return pl.BlockSpec(value.shape, lambda i: (0,) * value.ndim)
+
+    gain_spec = whole(gains[0])
+    full = jax.ShapeDtypeStruct(master.shape, jnp.float32)
+    gain_shape = jax.ShapeDtypeStruct(gains[0].shape, jnp.float32)
+    one = jax.ShapeDtypeStruct((1,), jnp.float32)
+    return pl.pallas_call(
+        functools.partial(finish_kernel, micro_count),
+        grid=(count,),
+        out_shape=(
+            one, one, full, full, full, jax.ShapeDtypeStruct(master.shape, jnp.bfloat16),
+            gain_shape, gain_shape, gain_shape,
+        ),
+        in_specs=[smem] * 2 + [slots] * 4 + [whole(small), whole(squares)] + [gain_spec] * 3,
+        out_specs=(smem, smem, slots, slots, slots, slots, gain_spec, gain_spec, gain_spec),
+        name="finish",
+    )(step_count, owned, master, first, second, reduced.reshape(master.shape), small, squares, *gains)
 
 
 def body(
@@ -1495,9 +1512,12 @@
     model_width = master.shape[2]
     slot_count = master.shape[0] * lax.axis_size("seq")
     if (micro_count, lax.axis_size("seq"), lax.axis_size("dp")) == (4, 4, 8):
-        return step_call(
-            char_ids, targets, seg_ids, lengths, owner_slot, step_count, master, tile_first, tile_second,
-            gain_rows, gain_first, gain_second,
+        reduced, small, squares, owned = step_call(
+            char_ids, targets, seg_ids, lengths, owner_slot, master, gain_rows
+        )
+        return finish_call(
+            micro_count, step_count, owned, master, tile_first, tile_second, reduced, small, squares,
+            (gain_rows, gain_first, gain_second),
         )
     tile_total = jnp.zeros((owner_slot.shape[0], model_width, model_width), jnp.float32)
     gain_total = jnp.zeros_like(gain_rows)

time: 262 us -> 245 us (0.935)
  local copies, waits for them, and re-layouts: 9.87 us -> 1.31 us
  Pallas kernels: 247 us -> 242 us
  between operations: 4.77 us -> 1.48 us
    pallas_call x1, Pallas kernels: 247 us -> 234 us  [step_call(): pl.pallas_call(functools.partial(step_kernel, micro_count), out_shape=(fa...]
    unnamed x20 -> x1, local copies, waits for them, and re-layouts: 9.87 us -> 1.31 us
    pallas_call x0 -> x1, Pallas kernels: none -> 7.41 us  [finish_call(): pl.pallas_call(functools.partial(finish_kernel, micro_count), grid=(count...]
where the time goes in v7:
time: 245 us; the launch traced here: 244 us
  Pallas kernels  242 us (99%)
    pallas_call x1, Pallas kernels, step_call(): pl.pallas_call(functools.partial(step_kernel, micro_count), out_shape=(fa...  234 us
    pallas_call x1, Pallas kernels, finish_call(): pl.pallas_call(functools.partial(finish_kernel, micro_count), grid=(count...  7.41 us

profile of v7, /device:TPU:0, one launch (start us, length us, event | category | flops | bytes accessed | tf_op | source)
XLA Modules:
  0.0 244.3 jit_solution(4871111657814809249)
XLA Ops:
  0.6 1.3 copy.21.lengths_ref
  2.0 234.1 %step.1 = (f32[26,4,2,2,16,512]{5,4,3,2,1,0:T(8,128)}, f32[26,4,2,2,16,512]{5,4,3,2,1,0:T(8,128)}, f32[10,2,2,16,512]{4,3,2,1,0:T(8,128)}, f32[8,512]{1,0:T(8,128)}, f32[8,128]{1,0:T(8,128)}, /*index=5*/s32[10]{0:T(128)}) custom-call(s32[4,1]{1,0:T(4,128)} %copy.21.lengths_ref, s32[26]{0:T(128)} %owner_ref.1, f32[10,64,512]{2,1,0:T(8,128)} %master_ref.3, ...), custom_call_target="tpu_custom_call" | custom-call | tf_op jit(solution)/shard_map/step/pallas_call | solution.py:1385
  236.7 7.4 %finish.1 = (f32[1]{0:T(128)}, f32[1]{0:T(128)}, f32[10,64,512]{2,1,0:T(8,128)}, f32[10,64,512]{2,1,0:T(8,128)}, f32[10,64,512]{2,1,0:T(8,128)}, /*index=5*/bf16...) custom-call(s32[1]{0:T(128)S(6)} %copy.22.step_ref, s32[10]{0:T(128)} %get-tuple-element.13.owned_ref, ...), custom_call_target="tpu_custom_call" | custom-call | tf_op jit(solution)/shard_map/finish/pallas_call | solution.py:1484
